TPU v7x, 32 devices: a whole 2x2x4 slice. The times are simulated.
32 devices in a mesh: ctx: 8 (over z, core), tp: 4 (over y, x).
Axes of the slice: x: 2, y: 2, z: 4, core: 2. Of those that a mesh axis runs over, the one named last changes fastest.
Arguments:
- tokens: bfloat16 [2048, 4096], P('ctx', 'tp'), may hold values from -6 to 6
- w_z: bfloat16 [4096, 2048], P(None, 'tp'), may hold values from -0.09375 to 0.09375
- w_x: bfloat16 [4096, 2048], P(None, 'tp'), may hold values from -0.09375 to 0.09375
- w_bc: bfloat16 [4096, 512], P(None, 'tp'), may hold values from -0.09375 to 0.09375
- conv_x: float32 [4, 2048], P(None, 'tp'), may hold values from -3 to 3
- conv_bc: float32 [4, 512], P(None, 'tp'), may hold values from -3 to 3
- bias_x: float32 [2048], P('tp'), may hold values from -0.5 to 0.5
- bias_bc: float32 [512], P('tp'), may hold values from -0.5 to 0.5
- decay_logarithm: float32 [2048, 32], P('ctx', 'tp'), may hold values from -1.3 to 0, as said below
- head_step: float32 [32], P('tp'), may hold values from 0 to 0.3, as said below
- skip: float32 [32], P('tp'), may hold values from 0.5 to 1.5
- gain: float32 [2048], P('tp'), may hold values from 0.5 to 1.5
Outputs:
- normed: bfloat16 [2048, 2048], P('ctx', 'tp')
Inputs may be any that keep to these rules, and one draw needn't show every extreme that they name: decay_logarithm is negative. head_step is positive.
All inputs are finite; a program needn't handle non-finite values.
Results may differ from a plain program's by a relative error of at most 0.0095.
Values may be sent and summed in bfloat16 or wider, within the bound.
No kernel may reach another device: no remote copies, remote signals or barrier semaphores. Data moves between devices by JAX's collectives and lax.ppermute only.
A program may use at most 64 MiB of HBM per device.

v0:
```python
import jax
import jax.numpy as jnp
from jax import lax
from jax.sharding import PartitionSpec as P

KERNEL = 4
STRETCH = 256


def shifted(block, axis, distance):
    devices = range(lax.axis_size(axis))
    route = [(i - distance, i) for i in devices if i - distance in devices]
    return lax.ppermute(block, axis, route)


def partner(value, axis, distance):
    mask = 2**distance
    pairs = [(source, source ^ mask) for source in range(lax.axis_size(axis))]
    return lax.ppermute(value, axis, pairs)


def carried_in(shard, axis, combine, identity):
    size, place = (lax.axis_size(axis), lax.axis_index(axis))
    everything = jax.tree.map(lambda part: lax.all_gather(part, axis), shard)
    start = jax.tree.map(
        lambda part, zero: jnp.broadcast_to(jnp.asarray(zero, part.dtype), part.shape),
        shard,
        identity,
    )

    def lap(k, before):
        reached = k < place
        new = combine(before, jax.tree.map(lambda part: part[k], everything))
        return jax.tree.map(lambda a, b: jnp.where(reached, a, b), new, before)

    return lax.fori_loop(0, size, lap, start)


def state_combine(earlier, later):
    return (earlier[0] + later[0], jnp.exp(later[0])[:, None, None] * earlier[1] + later[1])


def local(
    tokens, w_z, w_x, w_bc, conv_x, conv_bc, bias_x, bias_bc, decay_logarithm, head_step, skip, gain
):
    tok_rows = tokens.shape[0]
    x_width = w_x.shape[1]
    bc_width = w_bc.shape[1]
    heads_local = head_step.shape[0]
    head_dim = x_width // heads_local
    gathered = lax.all_gather(tokens, "tp", axis=1, tiled=True)
    gate_sum = jnp.dot(gathered, w_z, preferred_element_type=jnp.float32)
    x_sum = jnp.dot(gathered, w_x, preferred_element_type=jnp.float32)
    bc_sum = jnp.dot(gathered, w_bc, preferred_element_type=jnp.float32)
    gate_in = gate_sum.astype(jnp.bfloat16)
    x_pre = x_sum.astype(jnp.bfloat16)
    bc_pre = bc_sum.astype(jnp.bfloat16)
    pre_conv = jnp.concatenate([x_pre, bc_pre], axis=1)
    rim_rows = shifted(pre_conv[tok_rows - (KERNEL - 1) :], "ctx", 1)
    extended = jnp.concatenate([rim_rows, pre_conv], axis=0).astype(jnp.float32)
    conv_taps = jnp.concatenate([conv_x, conv_bc], axis=1)
    conv_bias = jnp.concatenate([bias_x, bias_bc], axis=0)
    conv_total = conv_bias[None, :] + jnp.zeros((tok_rows, x_width + bc_width), jnp.float32)
    for offset in range(KERNEL):
        conv_total = conv_total + conv_taps[offset][None, :] * extended[offset : offset + tok_rows]
    conv_out = jax.nn.silu(conv_total).astype(jnp.bfloat16)
    x_conv = conv_out[:, :x_width]
    own_bc = conv_out[:, x_width:]
    other_bc = partner(own_bc, "tp", 0)
    holds_b = lax.axis_index("tp") % 2 == 0
    b_proj = jnp.where(holds_b, own_bc, other_bc)
    c_proj = jnp.where(holds_b, other_bc, own_bc)
    stretch_len = STRETCH
    stretch_count = tok_rows // stretch_len
    x_float = x_conv.astype(jnp.float32).reshape(stretch_count, stretch_len, heads_local, head_dim)
    cum_decay = jnp.cumsum(decay_logarithm.reshape(stretch_count, stretch_len, heads_local), axis=1)
    b_stretches = b_proj.reshape(stretch_count, stretch_len, bc_width)
    c_stretches = c_proj.reshape(stretch_count, stretch_len, bc_width)
    scores = jnp.einsum(
        "cin,cjn->cij", c_stretches, b_stretches, preferred_element_type=jnp.float32
    )
    causal = jnp.tril(jnp.ones((stretch_len, stretch_len), dtype=bool))[None, :, :, None]
    pair_diff = cum_decay[:, :, None, :] - cum_decay[:, None, :, :]
    segment = jnp.where(causal, jnp.exp(jnp.where(causal, pair_diff, 0.0)), 0.0)
    mixing = segment * scores[:, :, :, None] * head_step
    intra_out = jnp.einsum("cijh,cjhp->cihp", mixing, x_float, precision=lax.Precision.HIGHEST)
    b_float = b_stretches.astype(jnp.float32)
    c_float = c_stretches.astype(jnp.float32)
    end_weight = jnp.exp(cum_decay[:, -1:, :] - cum_decay) * head_step
    stretch_states = jnp.einsum(
        "cjh,cjhp,cjn->chpn", end_weight, x_float, b_float, precision=lax.Precision.HIGHEST
    )
    stretch_decay = cum_decay[:, -1, :]

    def advance(state, item):
        added, decay_sum = item
        return (jnp.exp(decay_sum)[:, None, None] * state + added, state)

    zero_state = jnp.zeros((heads_local, head_dim, bc_width), jnp.float32)
    section_final_state, prior_section_state = lax.scan(
        advance, zero_state, (stretch_states, stretch_decay)
    )
    total_decay = jnp.sum(stretch_decay, axis=0)
    _, incoming = carried_in(
        (total_decay, section_final_state),
        "ctx",
        state_combine,
        (jnp.zeros_like(total_decay), zero_state),
    )
    prefix_decay = jnp.cumsum(stretch_decay, axis=0) - stretch_decay
    entering = prior_section_state + jnp.exp(prefix_decay)[:, :, None, None] * incoming[None]
    inter_out = (
        jnp.einsum("cin,chpn->cihp", c_float, entering, precision=lax.Precision.HIGHEST)
        * jnp.exp(cum_decay)[:, :, :, None]
    )
    head_out = (intra_out + inter_out).reshape(tok_rows, heads_local, head_dim)
    head_out = head_out + skip[None, :, None] * x_conv.astype(jnp.float32).reshape(
        tok_rows, heads_local, head_dim
    )
    gated = head_out.reshape(tok_rows, x_width) * jax.nn.silu(gate_in.astype(jnp.float32))
    local_square = jnp.sum(gated * gated, axis=1)
    other_square = partner(local_square, "tp", 0)
    mean_square = (local_square + other_square) / (2 * x_width)
    scaled = gated * lax.rsqrt(mean_square + 1e-05)[:, None]
    return (scaled * gain[None, :]).astype(jnp.bfloat16)


def solution(mesh):
    in_specs = (
        P("ctx", "tp"),
        P(None, "tp"),
        P(None, "tp"),
        P(None, "tp"),
        P(None, "tp"),
        P(None, "tp"),
        P("tp"),
        P("tp"),
        P("ctx", "tp"),
        P("tp"),
        P("tp"),
        P("tp"),
    )
    out_specs = P("ctx", "tp")
    return jax.shard_map(local, mesh=mesh, in_specs=in_specs, out_specs=out_specs, check_vma=False)
```

profile of v0, /device:TPU:0, one launch (start us, length us, event | category | flops | bytes accessed | tf_op | source)
XLA Modules:
  0.0 117.3 jit_solution(2576824456044173264)
XLA Ops:
  6.5 0.0 copy-start
  6.5 0.0 all-gather.5.cloned.1.call-start
  6.5 0.7 all-gather.5.cloned.1.call-update
  7.3 0.0 all-gather.7.cloned.1.call-start
  7.3 1.3 %reduce-window.6 = f32[1,8,2,128]{3,1,2,0:T(8,128)S(1)} reduce-window(f32[1,8,2,128]{3,1,2,0:T(8,128)} %bitcast.71, f32[]{:T(128)} %constant.69.clone.1), window={size=1x1x1x128 pad=0_0x0_0x0_0x127_0}, to_apply=%region_0.1 | reduce-window | flops 260096 | bytes 16388 | tf_op jit(solution)/shard_map/reduce-window
  8.6 0.2 slice_reduce_fusion
  8.8 0.7 constant_dynamic-update-slice_fusion.1
  9.5 0.7 constant_dynamic-update-slice_fusion
  10.2 0.1 exponential_bitcast_fusion.1
  10.3 0.2 slice_reduce_fusion.5
  10.4 0.7 multiply_bitcast_fusion
  11.2 35.9 %all-gather.5.cloned.1.call-done = bf16[256,4096]{1,0:T(8,128)(2,1)} async-done(((bf16[256,1024]{1,0:T(8,128)(2,1)}), bf16[256,4096]{1,0:T(8,128)(2,1)}) %all-gather.5.cloned.1.call-update) | async-done | bytes 2097168 | tf_op jit(solution)/shard_map/all_gather | solution.py:51
  47.1 0.0 copy-start.1
  47.1 4.2 %convolution_convert_fusion.1 = bf16[256,512]{1,0:T(8,128)(2,1)S(1)} fusion(bf16[256,4096]{1,0:T(8,128)(2,1)} %all-gather.5.cloned.1.call-done, bf16[4096,512]{1,0:T(8,128)(2,1)} %param.16), kind=kOutput, calls=%fused_computation.16 | convolution fusion | flops 1073872896 | bytes 6553600 | tf_op jit(solution)/shard_map/dot_general | solution.py:53
  51.3 0.0 copy-done
  51.3 0.0 copy-done.1
  51.4 0.0 copy-start.3
  51.4 0.0 copy-start.6
  51.4 0.7 convolution_convert_fusion.2
  52.1 1.6 %collective-permute-start = (bf16[3,640]{1,0:T(4,128)(2,1)S(1)}, bf16[3,640]{1,0:T(4,128)(2,1)S(1)}, u32[]{:S(2)}, u32[]{:S(2)}) collective-permute-start(bf16[3,640]{1,0:T(4,128)(2,1)S(1)} %pad_maximum_fusion), channel_id=1, source_target_pairs={{0,4},{4,8},{8,12},{12,16},{16,20},{20,24},{24,28},{1,5},{5,9},{9,... | collective-permute-start | bytes 11528 | tf_op jit(solution)/shard_map/ppermute | solution.py:13
  53.7 0.0 copy-done.3
  53.7 0.0 copy-done.6
  53.7 0.8 collective-permute-done
  54.5 0.1 maximum_convert_fusion
  54.6 0.0 copy-start.4
  54.6 0.4 multiply_convert_fusion
  55.0 0.0 copy-start.5
  55.1 1.5 %collective-permute-start.1 = (bf16[256,128]{1,0:T(8,128)(2,1)S(1)}, bf16[256,128]{1,0:T(8,128)(2,1)S(1)}, u32[]{:S(2)}, u32[]{:S(2)}) collective-permute-start(bf16[256,128]{1,0:T(8,128)(2,1)S(1)} %slice.67), channel_id=1, source_target_pairs={{0,1},{1,0},{2,3},{3,2},{4,5},{5,4},{6,7},{7,6},{8,9},{9,8},{10,11... | collective-permute-start | bytes 196616 | tf_op jit(solution)/shard_map/ppermute | solution.py:19
  56.6 0.1 copy.28
  56.8 2.6 %collective-permute-done.1 = bf16[256,128]{1,0:T(8,128)(2,1)S(1)} collective-permute-done((bf16[256,128]{1,0:T(8,128)(2,1)S(1)}, bf16[256,128]{1,0:T(8,128)(2,1)S(1)}, u32[]{:S(2)}, u32[]{:S(2)}) %collective-permute-start.1) | collective-permute-done | bytes 65568 | tf_op jit(solution)/shard_map/ppermute | solution.py:19
  59.4 1.1 convolution_add_fusion
  60.5 0.0 all-gather.7.cloned.1.call-update
  60.5 0.1 copy.29
  60.6 0.0 copy-done.4
  60.6 0.1 mul.197
  60.7 0.1 mul.198
  60.8 14.2 %all-gather = f32[8,1,8]{2,1,0:T(1,128)S(1)} all-gather(f32[1,1,8]{2,1,0:T(1,128)S(1)} %copy.29), channel_id=2, replica_groups=mesh['ctx'=8,'tp'=4] {'ctx'}, dimensions={0}, use_global_device_ids=true | all-gather | bytes 288 | tf_op jit(solution)/shard_map/all_gather | solution.py:24
  75.0 0.1 fusion.32
  75.1 0.2 fusion.31
  75.3 0.0 copy-done.5
  75.3 1.8 %fusion.8 = f32[1,256,8,64]{1,3,2,0:T(8,128)S(1)} fusion(bf16[256,8,64]{0,2,1:T(8,128)(2,1)S(1)} %bitcast.69, f32[8]{0:T(128)S(1)} %copy-done.5, f32[256,256]{1,0:T(8,128)S(1)} %fusion.31, f32[256,8]{0,1:T(8,128)S(1)} %fusion.32, pred[256,256]{1,0:T(8,128)(4,1)S(1)} %iota_compare_fusion), kind=kOutput, calls=%fused_computation.10 | convolution fusion | flops 405274624 | bytes 1122336 | tf_op jit(solution)/shard_map/cijh,cjhp->cihp/dot_general | solution.py:86
  77.1 15.3 %all-gather.7.cloned.1.call-done = f32[64,64,128]{2,1,0:T(8,128)} async-done(((f32[8,64,128]{2,1,0:T(8,128)}), f32[64,64,128]{2,1,0:T(8,128)}) %all-gather.7.cloned.1.call-update) | async-done | bytes 2097168 | tf_op jit(solution)/shard_map/all_gather | solution.py:24
  92.4 8.7 %while.9 = (s32[]{:T(128)}, f32[8,64,128]{2,1,0:T(8,128)S(1)}, s32[]{:T(128)}, f32[8,8]{1,0:T(8,128)S(1)}, f32[8,8,64,128]{3,2,1,0:T(8,128)}, /*index=5*/s32[]{:T(128)}, s32[]{:T(128)}) while((s32[]{:T(128)}, f32[8,64,128]{2,1,0:T(8,128)S(1)}, s32[]{:T(128)}, f32[8,8]{1,0:T(8,128)S(1)}, f32[8,8,64,128]{3,2,1,0:T(8,128)}, ...), condition=%wide.region_3.4_spmd.clone, body=%wide.region_2.3_spmd.clone.sunk | while | flops 262148 | bytes 786633 | solution.py:36
  92.4 1.1 fusion.47
  93.5 1.1 fusion.47
  94.6 1.1 fusion.47
  95.7 1.1 fusion.47
  96.8 1.1 fusion.47
  97.8 1.1 fusion.47
  98.9 1.1 fusion.47
  100.0 1.1 fusion.47
  101.1 0.4 fusion.12
  101.5 0.2 copy.30
  101.7 0.0 copy-start.2
  101.7 4.3 %multiply_reduce_fusion = (f32[256]{0:T(256)S(1)}, f32[256,512]{1,0:T(8,128)S(1)}) fusion(bf16[256,4096]{1,0:T(8,128)(2,1)} %all-gather.5.cloned.1.call-done, bf16[4096,512]{1,0:T(8,128)(2,1)} %param.15, f32[256,512]{1,0:T(8,128)S(1)} %copy.30, bf16[256,640]{1,0:T(8,128)(2,1)S(1)} %multiply_convert_fusion, f32[512]{0:T(512)S(1)} %mul.198), kind=kOutput, calls=%fused_computation.35 | convolution fusion | flops 1075314432 | bytes 7605248 | tf_op jit(solution)/shard_map/dot_general | solution.py:52
  106.0 1.5 %collective-permute-start.2 = (f32[256]{0:T(256)S(1)}, f32[256]{0:T(256)S(1)}, u32[]{:S(2)}, u32[]{:S(2)}) collective-permute-start(f32[256]{0:T(256)S(1)} %get-tuple-element.153), channel_id=1, source_target_pairs={{0,1},{1,0},{2,3},{3,2},{4,5},{5,4},{6,7},{7,6},{8,9},{9,8},{10,11... | collective-permute-start | bytes 3080 | tf_op jit(solution)/shard_map/ppermute | solution.py:19
  107.6 2.1 %collective-permute-done.2 = f32[256]{0:T(256)S(1)} collective-permute-done((f32[256]{0:T(256)S(1)}, f32[256]{0:T(256)S(1)}, u32[]{:S(2)}, u32[]{:S(2)}) %collective-permute-start.2) | collective-permute-done | bytes 1056 | tf_op jit(solution)/shard_map/ppermute | solution.py:19
  109.7 0.0 copy-done.2
  109.7 0.8 multiply_convert_fusion.1
  (19 shorter events, 0.2 us)
Async XLA Ops:
  6.5 44.8 %copy-start = (bf16[4096,128]{1,0:T(8,128)(2,1)S(1)}, bf16[4096,128]{1,0:T(8,128)(2,1)}, u32[]{:S(2)}) copy-start(bf16[4096,128]{1,0:T(8,128)(2,1)} %param.17) | copy-start | bytes 3145732
  6.5 40.6 %all-gather.5.cloned.1.call-start = ((), (), s32[]{:S(2)}) async-start(), calls=%async_computation | async-start | bytes 2621440 | tf_op jit(solution)/shard_map/all_gather | solution.py:51
  7.3 85.1 %all-gather.7.cloned.1.call-start = ((), (), s32[]{:S(2)}) async-start(), calls=%async_computation.1 | async-start | bytes 2359296 | tf_op jit(solution)/shard_map/all_gather | solution.py:24
  47.1 4.2 %copy-start.1 = (bf16[256,4096]{1,0:T(8,128)(2,1)S(1)}, bf16[256,4096]{1,0:T(8,128)(2,1)}, u32[]{:S(2)}) copy-start(bf16[256,4096]{1,0:T(8,128)(2,1)} %all-gather.5.cloned.1.call-done) | copy-start | bytes 6291460
  51.4 2.3 %copy-start.3 = (f32[512]{0:T(512)S(1)}, f32[512]{0:T(512)}, u32[]{:S(2)}) copy-start(f32[512]{0:T(512)} %param.20) | copy-start | bytes 6148
  51.4 2.3 %copy-start.6 = (f32[128]{0:T(128)S(1)}, f32[128]{0:T(128)}, u32[]{:S(2)}) copy-start(f32[128]{0:T(128)} %param.21) | copy-start | bytes 1540
  52.1 2.4 %collective-permute-start = (bf16[3,640]{1,0:T(4,128)(2,1)S(1)}, bf16[3,640]{1,0:T(4,128)(2,1)S(1)}, u32[]{:S(2)}, u32[]{:S(2)}) collective-permute-start(bf16[3,640]{1,0:T(4,128)(2,1)S(1)} %pad_maximum_fusion), channel_id=1, source_target_pairs={{0,4},{4,8},{8,12},{12,16},{16,20},{20,24},{24,28},{1,5},{5,9},{9,... | collective-permute-start | bytes 11528 | tf_op jit(solution)/shard_map/ppermute | solution.py:13
  54.6 6.0 %copy-start.4 = (f32[8]{0:T(128)S(1)}, f32[8]{0:T(128)}, u32[]{:S(2)}) copy-start(f32[8]{0:T(128)} %param.24) | copy-start | bytes 100
  55.0 20.3 %copy-start.5 = (f32[8]{0:T(128)S(1)}, f32[8]{0:T(128)}, u32[]{:S(2)}) copy-start(f32[8]{0:T(128)} %param.23) | copy-start | bytes 100
  55.1 4.3 %collective-permute-start.1 = (bf16[256,128]{1,0:T(8,128)(2,1)S(1)}, bf16[256,128]{1,0:T(8,128)(2,1)S(1)}, u32[]{:S(2)}, u32[]{:S(2)}) collective-permute-start(bf16[256,128]{1,0:T(8,128)(2,1)S(1)} %slice.67), channel_id=1, source_target_pairs={{0,1},{1,0},{2,3},{3,2},{4,5},{5,4},{6,7},{7,6},{8,9},{9,8},{10,11... | collective-permute-start | bytes 196616 | tf_op jit(solution)/shard_map/ppermute | solution.py:19
  101.7 7.9 %copy-start.2 = (f32[512]{0:T(512)S(1)}, f32[512]{0:T(512)}, u32[]{:S(2)}) copy-start(f32[512]{0:T(512)} %param.25) | copy-start | bytes 6148
  106.0 3.6 %collective-permute-start.2 = (f32[256]{0:T(256)S(1)}, f32[256]{0:T(256)S(1)}, u32[]{:S(2)}, u32[]{:S(2)}) collective-permute-start(f32[256]{0:T(256)S(1)} %get-tuple-element.153), channel_id=1, source_target_pairs={{0,1},{1,0},{2,3},{3,2},{4,5},{5,4},{6,7},{7,6},{8,9},{9,8},{10,11... | collective-permute-start | bytes 3080 | tf_op jit(solution)/shard_map/ppermute | solution.py:19
Sparse Core Ops, SparseCore 0:
  9.2 37.8 all-gather.4
  60.6 31.6 all-gather.6
where the time goes:
time: 118 us; the launch traced here: 117 us
  waiting for transfers between devices  57.4 us (49%)
  blocking collectives  14.2 us (12%)
  between operations  13.6 us (12%)
  matrix products  12.7 us (11%)
  other arithmetic  12 us (10%)
  starting transfers between devices  4.68 us (4%)
  local copies, waits for them, and re-layouts  2.46 us (2%)
    all_gather x1, waiting for transfers between devices, local(): gathered = lax.all_gather(tokens, 'tp', axis=1, tiled=True)  35.9 us
    all_gather x1, waiting for transfers between devices, carried_in(): everything = jax.tree.map(lambda part: lax.all_gather(part, axis), shard)  15.3 us
    all_gather x1, blocking collectives, carried_in(): everything = jax.tree.map(lambda part: lax.all_gather(part, axis), shard)  14.2 us
    select_n x8, other arithmetic, lap(): return jax.tree.map(lambda a, b: jnp.where(reached, a, b), new, before)  8.42 us
    ppermute x2, waiting for transfers between devices, partner(): return lax.ppermute(value, axis, pairs)  4.73 us
    dot_general x1, matrix products, local(): gate_sum = jnp.dot(gathered, w_z, preferred_element_type=jnp.float32)  4.28 us
    dot_general x1, matrix products, local(): x_sum = jnp.dot(gathered, w_x, preferred_element_type=jnp.float32)  4.21 us
    ppermute x2, starting transfers between devices, partner(): return lax.ppermute(value, axis, pairs)  3.07 us
  transfers between devices with their start and end apart: 5, of which 5 were waited for; matrix products, arithmetic and copies ran while one was open for 5% of the time, Pallas kernels for 0%

commit v1 on v0

v1 whole, which is shorter than its diff:
```python
import jax
import jax.numpy as jnp
from jax import lax
from jax.sharding import PartitionSpec as P

KERNEL = 4
STRETCH = 256
RIM = 8


def hop(value, axis, distance):
    size = lax.axis_size(axis)
    return lax.ppermute(value, axis, [(i, (i + distance) % size) for i in range(size)])


def onward(value, axis, distance):
    size = lax.axis_size(axis)
    route = [(i, i + distance) for i in range(size) if i + distance < size]
    return lax.ppermute(value, axis, route)


def partner(value, axis, mask):
    pairs = [(i, i ^ mask) for i in range(lax.axis_size(axis))]
    return lax.ppermute(value, axis, pairs)


def gathered_blocks(tokens, axis):
    size = lax.axis_size(axis)
    half = tokens.shape[0] // 2
    first, second = tokens[:half], tokens[half:]
    blocks = [(0, tokens)]
    if size == 1:
        return blocks
    near_1 = partner(first, axis, 1)
    if size == 2:
        near_2 = partner(second, axis, 1)
        return blocks + [(1, jnp.concatenate([near_1, near_2], 0))]
    far_2 = partner(second, axis, 2)
    near_2 = partner(second, axis, 1)
    far_1 = partner(first, axis, 2)
    across_1 = partner(near_1, axis, 2)
    across_2 = partner(far_2, axis, 1)
    blocks.append((1, jnp.concatenate([near_1, near_2], 0)))
    blocks.append((2, jnp.concatenate([far_1, far_2], 0)))
    blocks.append((3, jnp.concatenate([across_1, across_2], 0)))
    mask = 4
    while mask < size:
        blocks += [(m | mask, partner(b, axis, mask)) for m, b in blocks]
        mask *= 2
    return blocks


def gathered_rim(rows, axis):
    size, place = lax.axis_size(axis), lax.axis_index(axis)
    rows = rows[None]
    mask = 1
    while mask < size:
        other = partner(rows, axis, mask)
        high = (place // mask) % 2 == 1
        rows = jnp.concatenate(
            [jnp.where(high, other, rows), jnp.where(high, rows, other)], axis=0
        )
        mask *= 2
    return rows.transpose(1, 0, 2).reshape(rows.shape[1], -1)


def causal_conv(rim, body, taps, bias):
    rows = body.shape[0]
    extended = jnp.concatenate([rim[RIM - KERNEL + 1 :], body], axis=0).astype(jnp.float32)
    total = bias[None, :]
    for offset in range(KERNEL):
        total = total + taps[offset][None, :] * extended[offset : offset + rows]
    return jax.nn.silu(total).astype(jnp.bfloat16)


def local(
    tokens, w_z, w_x, w_bc, conv_x, conv_bc, bias_x, bias_bc, decay_logarithm, head_step, skip, gain
):
    f32, bf16 = jnp.float32, jnp.bfloat16
    rows, depth = tokens.shape
    width = w_x.shape[1]
    heads = head_step.shape[0]
    dim = width // heads
    n = w_bc.shape[1]
    tp_place = lax.axis_index("tp")
    ctx_size, ctx_place = lax.axis_size("ctx"), lax.axis_index("ctx")
    chips, chip, core = ctx_size // 2, ctx_place // 2, ctx_place % 2

    rim_tokens = gathered_rim(onward(tokens[rows - RIM :], "ctx", 1), "tp")

    cum = jnp.cumsum(decay_logarithm, axis=0)
    total = cum[-1]
    total_sibling = partner(total, "ctx", 1)
    total_chip = total + total_sibling
    chip_before = [hop(total_chip, "ctx", 2 * k) for k in range(1, chips - 1)]

    def product(block, weights):
        return jnp.dot(block, weights, preferred_element_type=f32)

    def projected(blocks, weights):
        acc = None
        for mask, block in blocks:
            part = lax.dynamic_slice_in_dim(weights, (tp_place ^ mask) * depth, depth, 0)
            term = product(block, part)
            acc = term if acc is None else acc + term
        return acc.astype(bf16)

    blocks = gathered_blocks(tokens, "tp")
    bc_rim = product(rim_tokens, w_bc).astype(bf16)
    x_rim = product(rim_tokens, w_x).astype(bf16)
    bc_pre = projected(blocks, w_bc)
    own_bc = causal_conv(bc_rim, bc_pre, conv_bc, bias_bc)
    other_bc = partner(own_bc, "tp", 1)
    x_pre = projected(blocks, w_x)
    x_conv = causal_conv(x_rim, x_pre, conv_x, bias_x)
    holds_b = tp_place % 2 == 0
    b_proj = jnp.where(holds_b, own_bc, other_bc)
    c_proj = jnp.where(holds_b, other_bc, own_bc)

    x_heads = x_conv.reshape(rows, heads, dim)
    end_weight = jnp.exp(total[None, :] - cum) * head_step
    weighted = (x_heads.astype(f32) * end_weight[:, :, None]).astype(bf16)
    state = lax.dot_general(
        weighted.reshape(rows, width), b_proj, (((0,), (0,)), ((), ())), preferred_element_type=f32
    )
    state = state.reshape(2, width // 2, n)

    def rows_of(per_head):
        return jnp.repeat(per_head.reshape(2, heads // 2), dim, axis=1)

    def mine(halves):
        return jnp.where(core == 0, halves[0], halves[1])

    def others(halves):
        return jnp.where(core == 0, halves[1], halves[0])

    kept = mine(state)
    sibling = partner(others(state).astype(bf16), "ctx", 1).astype(f32)
    first_state = jnp.where(core == 0, kept, sibling)
    second_state = jnp.where(core == 0, sibling, kept)
    first_decay = jnp.where(core == 0, total, total_sibling)
    second_decay = jnp.where(core == 0, total_sibling, total)
    chip_state = second_state + jnp.exp(mine(rows_of(second_decay)))[:, None] * first_state
    send = chip_state.astype(bf16)
    before = jnp.zeros_like(chip_state)
    between = jnp.zeros_like(total)
    for k in range(1, chips):
        got = hop(send, "ctx", 2 * k).astype(f32)
        weight = jnp.where(chip >= k, jnp.exp(mine(rows_of(between))), 0.0)
        before = before + weight[:, None] * got
        if k < chips - 1:
            between = between + jnp.where(chip >= k, chip_before[k - 1], 0.0)
    after_first = first_state + jnp.exp(mine(rows_of(first_decay)))[:, None] * before
    keep = jnp.where(core == 0, before, after_first).astype(bf16)
    give = jnp.where(core == 0, after_first, before).astype(bf16)
    take = partner(give, "ctx", 1)
    low = jnp.where(core == 0, keep, take)
    high = jnp.where(core == 0, take, keep)
    entering = jnp.concatenate([low, high], axis=0)

    scores = lax.dot_general(
        c_proj, b_proj, (((1,), (1,)), ((), ())), preferred_element_type=f32
    )
    causal = jnp.tril(jnp.ones((rows, rows), dtype=bool))[None]
    cum_heads = cum.T
    pair_diff = cum_heads[:, :, None] - cum_heads[:, None, :]
    segment = jnp.where(causal, jnp.exp(jnp.where(causal, pair_diff, 0.0)), 0.0)
    mixing = (segment * scores[None] * head_step[:, None, None]).astype(bf16)
    intra = jnp.einsum("hij,jhp->ihp", mixing, x_heads, preferred_element_type=f32)
    intra = intra + skip[None, :, None] * x_heads.astype(f32)
    gate = jax.nn.silu(projected(blocks, w_z).astype(f32))

    inter = lax.dot_general(
        c_proj, entering, (((1,), (1,)), ((), ())), preferred_element_type=f32
    ).reshape(rows, heads, dim)
    out = intra + inter * jnp.exp(cum)[:, :, None]
    gated = out.reshape(rows, width) * gate
    local_square = jnp.sum(gated * gated, axis=1)
    other_square = partner(local_square, "tp", 1)
    mean_square = (local_square + other_square) / (2 * width)
    scaled = gated * lax.rsqrt(mean_square + 1e-05)[:, None]
    return (scaled * gain[None, :]).astype(bf16)


def solution(mesh):
    in_specs = (
        P("ctx", "tp"),
        P(None, "tp"),
        P(None, "tp"),
        P(None, "tp"),
        P(None, "tp"),
        P(None, "tp"),
        P("tp"),
        P("tp"),
        P("ctx", "tp"),
        P("tp"),
        P("tp"),
        P("tp"),
    )
    out_specs = P("ctx", "tp")
    return jax.shard_map(local, mesh=mesh, in_specs=in_specs, out_specs=out_specs, check_vma=False)
```

time: 118 us -> 88.7 us (0.75)
  waiting for transfers between devices: 57.4 us -> 23.4 us
  starting transfers between devices: 4.68 us -> 26.9 us
  blocking collectives: 14.2 us -> 0 us
  between operations: 13.6 us -> 0.7 us
  local copies, waits for them, and re-layouts: 2.46 us -> 12 us
  matrix products: 12.7 us -> 19.9 us
  other arithmetic: 12 us -> 5.24 us
    all_gather x2 -> x0, waiting for transfers between devices: 51.2 us -> none  [the longest x1 35.9 us: local(): gathered = lax.all_gather(tokens, 'tp', axis=1, tiled=True)]
    all_gather x1 -> x0, blocking collectives: 14.2 us -> none  [carried_in(): everything = jax.tree.map(lambda part: lax.all_gather(part, axis), shard)]
    ppermute x2 -> x13, starting transfers between devices: 3.07 us -> 15.2 us  [partner(): return lax.ppermute(value, axis, pairs)]
    ppermute x1 -> x6, waiting for transfers between devices: 0.77 us -> 11.8 us  [the longest x5 10.7 us: hop(): lax.ppermute(value, axis, [(i, (i + distance) % size) for i in range(size)])]
    ppermute x1 -> x6, starting transfers between devices: 1.57 us -> 11.7 us  [the longest x5 10.4 us: hop(): lax.ppermute(value, axis, [(i, (i + distance) % size) for i in range(size)])]
    select_n x8 -> x6, other arithmetic: 8.42 us -> 0.35 us  [the longest x1 0.17 us: local(): low = jnp.where(core == 0, keep, take)]
    dot_general x7 -> x18, matrix products: 12.7 us -> 19.9 us  [the longest x14 17.5 us: product(): return jnp.dot(block, weights, preferred_element_type=f32)]
    ppermute x2 -> x13, waiting for transfers between devices: 4.73 us -> 11.6 us  [partner(): return lax.ppermute(value, axis, pairs)]
  transfers between devices with their start and end apart: 5 -> 19, of which waited for: 5 -> 12; matrix products, arithmetic and copies ran while one was open for 5% -> 33% of each run, Pallas kernels for 0% -> 0%
where the time goes in v1:
time: 88.7 us; the launch traced here: 88.1 us
  starting transfers between devices  26.9 us (30%)
  waiting for transfers between devices  23.4 us (26%)
  matrix products  19.9 us (22%)
  local copies, waits for them, and re-layouts  12 us (14%)
  other arithmetic  5.24 us (6%)
    dot_general x14, matrix products, product(): return jnp.dot(block, weights, preferred_element_type=f32)  17.5 us
    ppermute x13, starting transfers between devices, partner(): return lax.ppermute(value, axis, pairs)  15.2 us
    ppermute x13, waiting for transfers between devices, partner(): return lax.ppermute(value, axis, pairs)  11.6 us
    ppermute x5, waiting for transfers between devices, hop(): lax.ppermute(value, axis, [(i, (i + distance) % size) for i in range(size)])  10.7 us
    ppermute x5, starting transfers between devices, hop(): lax.ppermute(value, axis, [(i, (i + distance) % size) for i in range(size)])  10.4 us
    unnamed x45, local copies, waits for them, and re-layouts  2.2 us
    slice x1, local copies, waits for them, and re-layouts, gathered_blocks(): first, second = (tokens[:half], tokens[half:])  1.96 us
    another operation x3, other arithmetic  1.95 us
  transfers between devices with their start and end apart: 19, of which 12 were waited for; matrix products, arithmetic and copies ran while one was open for 33% of the time, Pallas kernels for 0%

profile of v1, /device:TPU:0, one launch (start us, length us, event | category | flops | bytes accessed | tf_op | source)
XLA Modules:
  0.0 88.1 jit_solution(14789631349112998243)
XLA Ops:
  0.0 2.0 %fusion.67 = (bf16[128,1024]{1,0:T(8,128)(2,1)}, bf16[128,1024]{1,0:T(8,128)(2,1)}) fusion(bf16[256,1024]{1,0:T(8,128)(2,1)} %param.12), kind=kLoop, calls=%fused_computation.140 | loop fusion | bytes 1048576 | tf_op jit(solution)/shard_map/slice | solution.py:30
  2.0 3.0 %collective-permute-start.5 = (bf16[128,1024]{1,0:T(8,128)(2,1)}, bf16[128,1024]{1,0:T(8,128)(2,1)}, u32[]{:S(2)}, u32[]{:S(2)}) collective-permute-start(bf16[128,1024]{1,0:T(8,128)(2,1)} %get-tuple-element.12), channel_id=1, source_target_pairs={{0,2},{1,3},{2,0},{3,1},{4,6},{5,7},{6,4},{7,5},{8,10},{9,11},{10,... | collective-permute-start | bytes 786440 | tf_op jit(solution)/shard_map/ppermute | solution.py:24
  5.0 1.5 %collective-permute-start.3 = (bf16[128,1024]{1,0:T(8,128)(2,1)}, bf16[128,1024]{1,0:T(8,128)(2,1)}, u32[]{:S(2)}, u32[]{:S(2)}) collective-permute-start(bf16[128,1024]{1,0:T(8,128)(2,1)} %get-tuple-element.12), channel_id=1, source_target_pairs={{0,1},{1,0},{2,3},{3,2},{4,5},{5,4},{6,7},{7,6},{8,9},{9,8},{10,11... | collective-permute-start | bytes 786440 | tf_op jit(solution)/shard_map/ppermute | solution.py:24
  6.5 0.5 collective-permute-start.6
  7.0 1.2 %reduce-window.6 = f32[8,2,128]{2,0,1:T(8,128)S(1)} reduce-window(f32[8,2,128]{2,0,1:T(8,128)} %bitcast.65, f32[]{:T(128)} %constant.85.clone.1), window={size=1x1x128 pad=0_0x0_0x127_0}, to_apply=%region_0.1 | reduce-window | flops 260096 | bytes 16388 | tf_op jit(solution)/shard_map/reduce-window
  8.5 0.2 slice_reduce_fusion.1
  8.8 1.3 %slice.131 = bf16[8,1024]{1,0:T(8,128)(2,1)} slice(bf16[256,1024]{1,0:T(8,128)(2,1)} %param.12), slice={[248:256], [0:1024]} | slice | bytes 32768 | tf_op jit(solution)/shard_map/slice | solution.py:89
  10.1 0.7 add_bitcast_fusion.1
  10.8 0.6 iota_compare_fusion
  11.4 1.4 %slice_bitcast_fusion.3 = (f32[128]{0:T(128)}, f32[128]{0:T(128)}, f32[128]{0:T(128)}, f32[128]{0:T(128)}) fusion(f32[4,128]{1,0:T(4,128)} %param.17), kind=kLoop, calls=%fused_computation.136 | loop fusion | bytes 4096 | tf_op jit(solution)/shard_map/mul | solution.py:72
  12.9 1.3 %convolution_bitcast_fusion.3 = f32[256,128]{0,1:T(8,128)S(1)} fusion(bf16[256,1024]{1,0:T(8,128)(2,1)} %param.12, bf16[4096,128]{1,0:T(8,128)(2,1)S(1)} %copy-done, s32[]{:T(128)S(6)} %select_n.246), kind=kOutput, calls=%fused_computation.17 | convolution fusion | flops 67108864 | bytes 917508 | tf_op jit(solution)/shard_map/dot_general | solution.py:98
  14.2 1.8 %convolution_bitcast_fusion.1 = f32[256,512]{1,0:T(8,128)S(1)} fusion(bf16[256,1024]{1,0:T(8,128)(2,1)} %param.12, bf16[4096,512]{1,0:T(8,128)(2,1)} %param.14, s32[]{:T(128)S(6)} %select_n.246), kind=kOutput, calls=%fused_computation.8 | convolution fusion | flops 268435456 | bytes 2097156 | tf_op jit(solution)/shard_map/dot_general | solution.py:98
  16.1 0.6 fusion.68
  16.8 0.2 copy.39
  17.0 1.7 %convolution_bitcast_fusion = f32[256,512]{1,0:T(8,128)S(1)} fusion(bf16[256,1024]{1,0:T(8,128)(2,1)S(1)} %copy-done.2, bf16[4096,512]{1,0:T(8,128)(2,1)} %param.13, s32[]{:T(128)S(6)} %select_n.246), kind=kOutput, calls=%fused_computation.7 | convolution fusion | flops 268435456 | bytes 2097156 | tf_op jit(solution)/shard_map/dot_general | solution.py:98
  18.9 0.7 exp.68
  19.6 2.1 %collective-permute-start.13 = (f32[8]{0:T(128)S(1)}, f32[8]{0:T(128)S(1)}, u32[]{:S(2)}, u32[]{:S(2)}) collective-permute-start(f32[8]{0:T(128)S(1)} %get-tuple-element.25), channel_id=1, source_target_pairs={{0,8},{4,12},{8,16},{12,20},{16,24},{20,28},{24,0},{28,4},{1,9},{5... | collective-permute-start | bytes 104 | tf_op jit(solution)/shard_map/ppermute | solution.py:13
  21.9 3.3 %collective-permute-done.13 = f32[8]{0:T(128)S(1)} collective-permute-done((f32[8]{0:T(128)S(1)}, f32[8]{0:T(128)S(1)}, u32[]{:S(2)}, u32[]{:S(2)}) %collective-permute-start.13) | collective-permute-done | bytes 64 | tf_op jit(solution)/shard_map/ppermute | solution.py:13
  25.2 1.0 %collective-permute-start.15 = (f32[8]{0:T(128)S(1)}, f32[8]{0:T(128)S(1)}, u32[]{:S(2)}, u32[]{:S(2)}) collective-permute-start(f32[8]{0:T(128)S(1)} %get-tuple-element.25), channel_id=1, source_target_pairs={{0,16},{4,20},{8,24},{12,28},{16,0},{20,4},{24,8},{28,12},{1,17},{... | collective-permute-start | bytes 104 | tf_op jit(solution)/shard_map/ppermute | solution.py:13
  26.2 3.5 %collective-permute-done.15 = f32[8]{0:T(128)S(1)} collective-permute-done((f32[8]{0:T(128)S(1)}, f32[8]{0:T(128)S(1)}, u32[]{:S(2)}, u32[]{:S(2)}) %collective-permute-start.15) | collective-permute-done | bytes 64 | tf_op jit(solution)/shard_map/ppermute | solution.py:13
  29.7 1.3 %collective-permute-start = (bf16[8,1024]{1,0:T(8,128)(2,1)}, bf16[8,1024]{1,0:T(8,128)(2,1)S(1)}, u32[]{:S(2)}, u32[]{:S(2)}) collective-permute-start(bf16[8,1024]{1,0:T(8,128)(2,1)} %slice.131), channel_id=1, source_target_pairs={{0,4},{4,8},{8,12},{12,16},{16,20},{20,24},{24,28},{1,5},{5,9},{9,... | collective-permute-start | bytes 49160 | tf_op jit(solution)/shard_map/ppermute | solution.py:19
  31.0 1.0 %collective-permute-done = bf16[8,1024]{1,0:T(8,128)(2,1)S(1)} collective-permute-done((bf16[8,1024]{1,0:T(8,128)(2,1)}, bf16[8,1024]{1,0:T(8,128)(2,1)S(1)}, u32[]{:S(2)}, u32[]{:S(2)}) %collective-permute-start) | collective-permute-done | bytes 16416 | tf_op jit(solution)/shard_map/ppermute | solution.py:19
  32.0 1.7 %collective-permute-start.1 = (bf16[1,8,1024]{2,1,0:T(8,128)(2,1)S(1)}, bf16[1,8,1024]{2,1,0:T(8,128)(2,1)S(1)}, u32[]{:S(2)}, u32[]{:S(2)}) collective-permute-start(bf16[1,8,1024]{2,1,0:T(8,128)(2,1)S(1)} %bitcast.64), channel_id=1, source_target_pairs={{0,1},{1,0},{2,3},{3,2},{4,5},{5,4},{6,7},{7,6},{8,9},{9,8},{10,11... | collective-permute-start | bytes 49160 | tf_op jit(solution)/shard_map/ppermute | solution.py:24
  33.8 2.0 %collective-permute-done.1 = bf16[1,8,1024]{2,1,0:T(8,128)(2,1)S(1)} collective-permute-done((bf16[1,8,1024]{2,1,0:T(8,128)(2,1)S(1)}, bf16[1,8,1024]{2,1,0:T(8,128)(2,1)S(1)}, u32[]{:S(2)}, u32[]{:S(2)}) %collective-permute-start.1) | collective-permute-done | bytes 16416 | tf_op jit(solution)/shard_map/ppermute | solution.py:24
  35.8 1.8 %collective-permute-start.2 = (bf16[2,8,1024]{2,1,0:T(8,128)(2,1)S(1)}, bf16[2,8,1024]{2,1,0:T(8,128)(2,1)S(1)}, u32[]{:S(2)}, u32[]{:S(2)}) collective-permute-start(bf16[2,8,1024]{2,1,0:T(8,128)(2,1)S(1)} %pad_maximum_fusion.1), channel_id=1, source_target_pairs={{0,2},{1,3},{2,0},{3,1},{4,6},{5,7},{6,4},{7,5},{8,10},{9,11},{10,... | collective-permute-start | bytes 98312 | tf_op jit(solution)/shard_map/ppermute | solution.py:24
  37.9 0.7 select_n.279
  38.6 1.2 %collective-permute-done.2 = bf16[2,8,1024]{2,1,0:T(8,128)(2,1)S(1)} collective-permute-done((bf16[2,8,1024]{2,1,0:T(8,128)(2,1)S(1)}, bf16[2,8,1024]{2,1,0:T(8,128)(2,1)S(1)}, u32[]{:S(2)}, u32[]{:S(2)}) %collective-permute-start.2) | collective-permute-done | bytes 32800 | tf_op jit(solution)/shard_map/ppermute | solution.py:24
  39.8 2.8 %fusion.70 = bf16[8,512]{1,0:T(8,128)(2,1)S(1)} fusion(bf16[8,4096]{1,0:T(8,128)(2,1)S(1)} %bitcast.61, bf16[4096,512]{1,0:T(8,128)(2,1)} %param.14), kind=kOutput, calls=%fused_computation.143 | convolution fusion | flops 33554432 | bytes 4268032 | tf_op jit(solution)/shard_map/dot_general | solution.py:98
  42.6 0.3 convolution_convert_fusion
  42.9 0.7 copy.38
  43.6 1.1 %constant_dynamic-update-slice_fusion.3 = bf16[256,1024]{1,0:T(8,128)(2,1)S(1)} fusion(bf16[128,1024]{1,0:T(8,128)(2,1)} %collective-permute-done.5), kind=kLoop, calls=%fused_computation.96 | loop fusion | bytes 524288
  44.8 1.8 %fusion.19 = f32[256,512]{1,0:T(8,128)S(1)} fusion(bf16[256,1024]{1,0:T(8,128)(2,1)S(1)} %constant_dynamic-update-slice_fusion.2, bf16[4096,512]{1,0:T(8,128)(2,1)} %param.14, s32[]{:T(128)S(6)} %select_n.248), kind=kOutput, calls=%fused_computation.31 | convolution fusion | flops 268435456 | bytes 2097156 | tf_op jit(solution)/shard_map/dot_general | solution.py:98
  46.6 1.0 %constant_dynamic-update-slice_fusion.1 = bf16[256,1024]{1,0:T(8,128)(2,1)S(1)} fusion(bf16[128,1024]{1,0:T(8,128)(2,1)} %collective-permute-done.3), kind=kLoop, calls=%fused_computation.94 | loop fusion | bytes 524288
  47.6 1.7 %fusion.9 = f32[256,512]{1,0:T(8,128)S(1)} fusion(bf16[256,1024]{1,0:T(8,128)(2,1)S(1)} %constant_dynamic-update-slice_fusion.2, bf16[4096,512]{1,0:T(8,128)(2,1)} %param.13, s32[]{:T(128)S(6)} %select_n.248), kind=kOutput, calls=%fused_computation.21 | convolution fusion | flops 268435456 | bytes 2097156 | tf_op jit(solution)/shard_map/dot_general | solution.py:98
  49.3 1.0 %constant_dynamic-update-slice_fusion = bf16[256,1024]{1,0:T(8,128)(2,1)S(1)} fusion(bf16[256,1024]{1,0:T(8,128)(2,1)S(1)} %constant_dynamic-update-slice_fusion.1, bf16[128,1024]{1,0:T(8,128)(2,1)} %collective-permute-done.4), kind=kLoop, calls=%fused_computation.93 | loop fusion | bytes 524288 | tf_op jit(solution)/shard_map/concatenate | solution.py:43
  50.3 0.4 fusion
  50.8 1.8 %collective-permute-start.7 = (bf16[128,1024]{1,0:T(8,128)(2,1)}, bf16[128,1024]{1,0:T(8,128)(2,1)S(1)}, u32[]{:S(2)}, u32[]{:S(2)}) collective-permute-start(bf16[128,1024]{1,0:T(8,128)(2,1)} %collective-permute-done.3), channel_id=1, source_target_pairs={{0,2},{1,3},{2,0},{3,1},{4,6},{5,7},{6,4},{7,5},{8,10},{9,11},{10,... | collective-permute-start | bytes 786440 | tf_op jit(solution)/shard_map/ppermute | solution.py:24
  52.6 0.3 fusion.32
  53.0 1.6 %collective-permute-start.8 = (bf16[128,1024]{1,0:T(8,128)(2,1)S(1)}, bf16[128,1024]{1,0:T(8,128)(2,1)S(1)}, u32[]{:S(2)}, u32[]{:S(2)}) collective-permute-start(bf16[128,1024]{1,0:T(8,128)(2,1)S(1)} %collective-permute-done.6), channel_id=1, source_target_pairs={{0,1},{1,0},{2,3},{3,2},{4,5},{5,4},{6,7},{7,6},{8,9},{9,8},{10,11... | collective-permute-start | bytes 786440 | tf_op jit(solution)/shard_map/ppermute | solution.py:24
  54.5 0.3 fusion.6
  54.8 2.9 %collective-permute-done.7 = bf16[128,1024]{1,0:T(8,128)(2,1)S(1)} collective-permute-done((bf16[128,1024]{1,0:T(8,128)(2,1)}, bf16[128,1024]{1,0:T(8,128)(2,1)S(1)}, u32[]{:S(2)}, u32[]{:S(2)}) %collective-permute-start.7) | collective-permute-done | bytes 262176 | tf_op jit(solution)/shard_map/ppermute | solution.py:24
  57.8 1.6 %collective-permute-done.8 = bf16[128,1024]{1,0:T(8,128)(2,1)S(1)} collective-permute-done((bf16[128,1024]{1,0:T(8,128)(2,1)S(1)}, bf16[128,1024]{1,0:T(8,128)(2,1)S(1)}, u32[]{:S(2)}, u32[]{:S(2)}) %collective-permute-start.8) | collective-permute-done | bytes 262176 | tf_op jit(solution)/shard_map/ppermute | solution.py:24
  59.4 0.3 fusion.7
  59.9 0.3 multiply_convert_fusion.6
  60.2 1.6 %collective-permute-start.9 = (bf16[256,128]{0,1:T(8,128)(2,1)S(1)}, bf16[256,128]{0,1:T(8,128)(2,1)S(1)}, u32[]{:S(2)}, u32[]{:S(2)}) collective-permute-start(bf16[256,128]{0,1:T(8,128)(2,1)S(1)} %multiply_convert_fusion.6), channel_id=1, source_target_pairs={{0,1},{1,0},{2,3},{3,2},{4,5},{5,4},{6,7},{7,6},{8,9},{9,8},{10,11... | collective-permute-start | bytes 196616 | tf_op jit(solution)/shard_map/ppermute | solution.py:24
  61.7 0.4 fusion.3
  62.3 0.3 multiply_convert_fusion.4
  62.7 1.8 %collective-permute-done.9 = bf16[256,128]{0,1:T(8,128)(2,1)S(1)} collective-permute-done((bf16[256,128]{0,1:T(8,128)(2,1)S(1)}, bf16[256,128]{0,1:T(8,128)(2,1)S(1)}, u32[]{:S(2)}, u32[]{:S(2)}) %collective-permute-start.9) | collective-permute-done | bytes 65568 | tf_op jit(solution)/shard_map/ppermute | solution.py:24
  64.5 0.3 fusion.30
  64.9 2.5 %fusion.1 = f32[256,512]{1,0:T(8,128)} fusion(f32[256,512]{1,0:T(8,128)S(1)} %fusion.9, f32[256,512]{1,0:T(8,128)S(1)} %convolution_bitcast_fusion, bf16[256,1024]{1,0:T(8,128)(2,1)S(1)} %constant_dynamic-update-slice_fusion, bf16[4096,512]{1,0:T(8,128)(2,1)} %param.13, s32[]{:T(128)S(6)} %select_n.247), kind=kOutput, calls=%fused_computation.6 | convolution fusion | flops 268697600 | bytes 3145732 | tf_op jit(solution)/shard_map/dot_general | solution.py:98
  67.6 3.4 %collective-permute-start.12 = (bf16[256,128]{1,0:T(8,128)(2,1)S(1)}, bf16[256,128]{1,0:T(8,128)(2,1)S(1)}, u32[]{:S(2)}, u32[]{:S(2)}) collective-permute-start(bf16[256,128]{1,0:T(8,128)(2,1)S(1)} %fusion.37), channel_id=1, source_target_pairs={{0,8},{4,12},{8,16},{12,20},{16,24},{20,28},{24,0},{28,4},{1,9},{5... | collective-permute-start | bytes 196616 | tf_op jit(solution)/shard_map/ppermute | solution.py:13
  71.0 2.7 %collective-permute-start.14 = (bf16[256,128]{1,0:T(8,128)(2,1)S(1)}, bf16[256,128]{1,0:T(8,128)(2,1)S(1)}, u32[]{:S(2)}, u32[]{:S(2)}) collective-permute-start(bf16[256,128]{1,0:T(8,128)(2,1)S(1)} %fusion.37), channel_id=1, source_target_pairs={{0,16},{4,20},{8,24},{12,28},{16,0},{20,4},{24,8},{28,12},{1,17},{... | collective-permute-start | bytes 196616 | tf_op jit(solution)/shard_map/ppermute | solution.py:13
  73.7 1.2 %collective-permute-start.16 = (bf16[256,128]{1,0:T(8,128)(2,1)S(1)}, bf16[256,128]{1,0:T(8,128)(2,1)S(1)}, u32[]{:S(2)}, u32[]{:S(2)}) collective-permute-start(bf16[256,128]{1,0:T(8,128)(2,1)S(1)} %fusion.37), channel_id=1, source_target_pairs={{0,24},{4,28},{8,0},{12,4},{16,8},{20,12},{24,16},{28,20},{1,25},{... | collective-permute-start | bytes 196616 | tf_op jit(solution)/shard_map/ppermute | solution.py:13
  74.9 0.2 fusion.46
  75.1 1.0 %collective-permute-done.12 = bf16[256,128]{1,0:T(8,128)(2,1)S(1)} collective-permute-done((bf16[256,128]{1,0:T(8,128)(2,1)S(1)}, bf16[256,128]{1,0:T(8,128)(2,1)S(1)}, u32[]{:S(2)}, u32[]{:S(2)}) %collective-permute-start.12) | collective-permute-done | bytes 65568 | tf_op jit(solution)/shard_map/ppermute | solution.py:13
  76.2 2.6 %collective-permute-done.14 = bf16[256,128]{1,0:T(8,128)(2,1)S(1)} collective-permute-done((bf16[256,128]{1,0:T(8,128)(2,1)S(1)}, bf16[256,128]{1,0:T(8,128)(2,1)S(1)}, u32[]{:S(2)}, u32[]{:S(2)}) %collective-permute-start.14) | collective-permute-done | bytes 65568 | tf_op jit(solution)/shard_map/ppermute | solution.py:13
  78.8 0.3 collective-permute-done.16
  79.3 1.7 %fusion.2 = f32[256,8,64]{0,2,1:T(8,128)S(1)} fusion(bf16[256,8,64]{0,2,1:T(8,128)(2,1)S(1)} %bitcast.63, f32[8]{0:T(128)} %param.21, f32[256,256]{1,0:T(8,128)S(1)} %fusion.46, f32[8,256]{1,0:T(8,128)} %add_bitcast_fusion.1, pred[256,256]{1,0:T(8,128)(4,1)} %iota_compare_fusion, f32[8]{0:T(128)} %param.22), kind=kOutput, calls=%fused_computation.10 | convolution fusion | flops 70647808 | bytes 1122368 | tf_op jit(solution)/shard_map/hij,jhp->ihp/dot_general | solution.py:169
  81.3 0.2 fusion.42
  81.6 0.2 copy.42
  81.8 1.8 %multiply_reduce_fusion = (f32[256]{0:T(256)S(1)}, f32[256,512]{1,0:T(8,128)S(1)}) fusion(f32[256,512]{1,0:T(8,128)S(1)} %copy.42, f32[256,512]{1,0:T(8,128)S(1)} %copy-done.3, bf16[256,1024]{1,0:T(8,128)(2,1)S(1)} %constant_dynamic-update-slice_fusion.4, bf16[4096,512]{1,0:T(8,128)(2,1)} %param.13, s32[]{:T(128)S(6)} %select_n.249), kind=kOutput, calls=%fused_computation.45 | convolution fusion | flops 269745920 | bytes 3146756 | tf_op jit(solution)/shard_map/dot_general | solution.py:98
  83.7 1.6 %collective-permute-start.18 = (f32[256]{0:T(256)S(1)}, f32[256]{0:T(256)S(1)}, u32[]{:S(2)}, u32[]{:S(2)}) collective-permute-start(f32[256]{0:T(256)S(1)} %get-tuple-element.28), channel_id=1, source_target_pairs={{0,1},{1,0},{2,3},{3,2},{4,5},{5,4},{6,7},{7,6},{8,9},{9,8},{10,11... | collective-permute-start | bytes 3080 | tf_op jit(solution)/shard_map/ppermute | solution.py:24
  85.2 2.1 %collective-permute-done.18 = f32[256]{0:T(256)S(1)} collective-permute-done((f32[256]{0:T(256)S(1)}, f32[256]{0:T(256)S(1)}, u32[]{:S(2)}, u32[]{:S(2)}) %collective-permute-start.18) | collective-permute-done | bytes 1056 | tf_op jit(solution)/shard_map/ppermute | solution.py:24
  87.3 0.8 multiply_convert_fusion.2
  (90 shorter events, 2.5 us)
Async XLA Ops:
  0.0 12.9 %copy-start = (bf16[4096,128]{1,0:T(8,128)(2,1)S(1)}, bf16[4096,128]{1,0:T(8,128)(2,1)}, u32[]{:S(2)}) copy-start(bf16[4096,128]{1,0:T(8,128)(2,1)} %param.15) | copy-start | bytes 3145732
  0.0 17.0 %copy-start.2 = (bf16[256,1024]{1,0:T(8,128)(2,1)S(1)}, bf16[256,1024]{1,0:T(8,128)(2,1)}, u32[]{:S(2)}) copy-start(bf16[256,1024]{1,0:T(8,128)(2,1)} %param.12) | copy-start | bytes 1572868
  0.0 16.1 %copy-start.7 = (f32[4,512]{1,0:T(4,128)S(1)}, f32[4,512]{1,0:T(4,128)}, u32[]{:S(2)}) copy-start(f32[4,512]{1,0:T(4,128)} %param.16) | copy-start | bytes 24580
  0.0 16.7 %copy-start.19 = (f32[8]{0:T(128)S(1)}, f32[8]{0:T(128)}, u32[]{:S(2)}) copy-start(f32[8]{0:T(128)} %param.21) | copy-start | bytes 100
  2.0 41.7 %collective-permute-start.5 = (bf16[128,1024]{1,0:T(8,128)(2,1)}, bf16[128,1024]{1,0:T(8,128)(2,1)}, u32[]{:S(2)}, u32[]{:S(2)}) collective-permute-start(bf16[128,1024]{1,0:T(8,128)(2,1)} %get-tuple-element.12), channel_id=1, source_target_pairs={{0,2},{1,3},{2,0},{3,1},{4,6},{5,7},{6,4},{7,5},{8,10},{9,11},{10,... | collective-permute-start | bytes 786440 | tf_op jit(solution)/shard_map/ppermute | solution.py:24
  5.0 41.6 %collective-permute-start.3 = (bf16[128,1024]{1,0:T(8,128)(2,1)}, bf16[128,1024]{1,0:T(8,128)(2,1)}, u32[]{:S(2)}, u32[]{:S(2)}) collective-permute-start(bf16[128,1024]{1,0:T(8,128)(2,1)} %get-tuple-element.12), channel_id=1, source_target_pairs={{0,1},{1,0},{2,3},{3,2},{4,5},{5,4},{6,7},{7,6},{8,9},{9,8},{10,11... | collective-permute-start | bytes 786440 | tf_op jit(solution)/shard_map/ppermute | solution.py:24
  6.5 38.3 %collective-permute-start.6 = (bf16[128,1024]{1,0:T(8,128)(2,1)}, bf16[128,1024]{1,0:T(8,128)(2,1)S(1)}, u32[]{:S(2)}, u32[]{:S(2)}) collective-permute-start(bf16[128,1024]{1,0:T(8,128)(2,1)} %get-tuple-element.11), channel_id=1, source_target_pairs={{0,2},{1,3},{2,0},{3,1},{4,6},{5,7},{6,4},{7,5},{8,10},{9,11},{10,... | collective-permute-start | bytes 786440 | tf_op jit(solution)/shard_map/ppermute | solution.py:24
  7.0 42.4 %collective-permute-start.4 = (bf16[128,1024]{1,0:T(8,128)(2,1)}, bf16[128,1024]{1,0:T(8,128)(2,1)}, u32[]{:S(2)}, u32[]{:S(2)}) collective-permute-start(bf16[128,1024]{1,0:T(8,128)(2,1)} %get-tuple-element.11), channel_id=1, source_target_pairs={{0,1},{1,0},{2,3},{3,2},{4,5},{5,4},{6,7},{7,6},{8,9},{9,8},{10,11... | collective-permute-start | bytes 786440 | tf_op jit(solution)/shard_map/ppermute | solution.py:24
  8.7 10.0 %collective-permute-start.11 = (f32[8]{0:T(128)S(1)}, f32[8]{0:T(128)S(1)}, u32[]{:S(2)}, u32[]{:S(2)}) collective-permute-start(f32[8]{0:T(128)S(1)} %slice_reduce_fusion.1), channel_id=1, source_target_pairs={{0,4},{4,0},{8,12},{12,8},{16,20},{20,16},{24,28},{28,24},{1,5},{5... | collective-permute-start | bytes 104 | tf_op jit(solution)/shard_map/ppermute | solution.py:24
  19.6 5.7 %collective-permute-start.13 = (f32[8]{0:T(128)S(1)}, f32[8]{0:T(128)S(1)}, u32[]{:S(2)}, u32[]{:S(2)}) collective-permute-start(f32[8]{0:T(128)S(1)} %get-tuple-element.25), channel_id=1, source_target_pairs={{0,8},{4,12},{8,16},{12,20},{16,24},{20,28},{24,0},{28,4},{1,9},{5... | collective-permute-start | bytes 104 | tf_op jit(solution)/shard_map/ppermute | solution.py:13
  25.2 4.5 %collective-permute-start.15 = (f32[8]{0:T(128)S(1)}, f32[8]{0:T(128)S(1)}, u32[]{:S(2)}, u32[]{:S(2)}) collective-permute-start(f32[8]{0:T(128)S(1)} %get-tuple-element.25), channel_id=1, source_target_pairs={{0,16},{4,20},{8,24},{12,28},{16,0},{20,4},{24,8},{28,12},{1,17},{... | collective-permute-start | bytes 104 | tf_op jit(solution)/shard_map/ppermute | solution.py:13
  29.7 2.3 %collective-permute-start = (bf16[8,1024]{1,0:T(8,128)(2,1)}, bf16[8,1024]{1,0:T(8,128)(2,1)S(1)}, u32[]{:S(2)}, u32[]{:S(2)}) collective-permute-start(bf16[8,1024]{1,0:T(8,128)(2,1)} %slice.131), channel_id=1, source_target_pairs={{0,4},{4,8},{8,12},{12,16},{16,20},{20,24},{24,28},{1,5},{5,9},{9,... | collective-permute-start | bytes 49160 | tf_op jit(solution)/shard_map/ppermute | solution.py:19
  32.0 3.7 %collective-permute-start.1 = (bf16[1,8,1024]{2,1,0:T(8,128)(2,1)S(1)}, bf16[1,8,1024]{2,1,0:T(8,128)(2,1)S(1)}, u32[]{:S(2)}, u32[]{:S(2)}) collective-permute-start(bf16[1,8,1024]{2,1,0:T(8,128)(2,1)S(1)} %bitcast.64), channel_id=1, source_target_pairs={{0,1},{1,0},{2,3},{3,2},{4,5},{5,4},{6,7},{7,6},{8,9},{9,8},{10,11... | collective-permute-start | bytes 49160 | tf_op jit(solution)/shard_map/ppermute | solution.py:24
  35.8 4.0 %collective-permute-start.2 = (bf16[2,8,1024]{2,1,0:T(8,128)(2,1)S(1)}, bf16[2,8,1024]{2,1,0:T(8,128)(2,1)S(1)}, u32[]{:S(2)}, u32[]{:S(2)}) collective-permute-start(bf16[2,8,1024]{2,1,0:T(8,128)(2,1)S(1)} %pad_maximum_fusion.1), channel_id=1, source_target_pairs={{0,2},{1,3},{2,0},{3,1},{4,6},{5,7},{6,4},{7,5},{8,10},{9,11},{10,... | collective-permute-start | bytes 98312 | tf_op jit(solution)/shard_map/ppermute | solution.py:24
  43.6 6.7 %copy-start.1 = (bf16[4096,512]{1,0:T(8,128)(2,1)S(1)}, bf16[4096,512]{1,0:T(8,128)(2,1)}, u32[]{:S(2)}) copy-start(bf16[4096,512]{1,0:T(8,128)(2,1)} %param.14) | copy-start | bytes 12582916
  49.3 10.5 %copy-start.4 = (bf16[3,128]{0,1:T(8,128)(2,1)S(1)}, bf16[3,128]{0,1:T(8,128)(2,1)}, u32[]{:S(2)}) copy-start(bf16[3,128]{0,1:T(8,128)(2,1)} %copy.38) | copy-start | bytes 2308
  49.3 10.6 %copy-start.14 = (f32[128]{0:T(128)S(1)}, f32[128]{0:T(128)}, u32[]{:S(2)}) copy-start(f32[128]{0:T(128)} %get-tuple-element.21) | copy-start | bytes 1540
  49.3 10.6 %copy-start.15 = (f32[128]{0:T(128)S(1)}, f32[128]{0:T(128)}, u32[]{:S(2)}) copy-start(f32[128]{0:T(128)} %get-tuple-element.22) | copy-start | bytes 1540
  49.3 10.6 %copy-start.16 = (f32[128]{0:T(128)S(1)}, f32[128]{0:T(128)}, u32[]{:S(2)}) copy-start(f32[128]{0:T(128)} %get-tuple-element.23) | copy-start | bytes 1540
  49.3 10.6 %copy-start.17 = (f32[128]{0:T(128)S(1)}, f32[128]{0:T(128)}, u32[]{:S(2)}) copy-start(f32[128]{0:T(128)} %get-tuple-element.24) | copy-start | bytes 1540
  49.3 10.6 %copy-start.20 = (f32[128]{0:T(128)S(1)}, f32[128]{0:T(128)}, u32[]{:S(2)}) copy-start(f32[128]{0:T(128)} %param.19) | copy-start | bytes 1540
  50.8 11.5 %copy-start.8 = (f32[1,512]{1,0:T(1,128)S(1)}, f32[1,512]{1,0:T(1,128)}, u32[]{:S(2)}) copy-start(f32[1,512]{1,0:T(1,128)} %get-tuple-element.17) | copy-start | bytes 6148
  50.8 11.5 %copy-start.9 = (f32[1,512]{1,0:T(1,128)S(1)}, f32[1,512]{1,0:T(1,128)}, u32[]{:S(2)}) copy-start(f32[1,512]{1,0:T(1,128)} %get-tuple-element.18) | copy-start | bytes 6148
  50.8 11.5 %copy-start.10 = (f32[1,512]{1,0:T(1,128)S(1)}, f32[1,512]{1,0:T(1,128)}, u32[]{:S(2)}) copy-start(f32[1,512]{1,0:T(1,128)} %get-tuple-element.19) | copy-start | bytes 6148
  50.8 11.5 %copy-start.11 = (f32[1,512]{1,0:T(1,128)S(1)}, f32[1,512]{1,0:T(1,128)}, u32[]{:S(2)}) copy-start(f32[1,512]{1,0:T(1,128)} %get-tuple-element.20) | copy-start | bytes 6148
  50.8 11.5 %copy-start.18 = (f32[512]{0:T(512)S(1)}, f32[512]{0:T(512)}, u32[]{:S(2)}) copy-start(f32[512]{0:T(512)} %param.18) | copy-start | bytes 6148
  50.8 6.9 %collective-permute-start.7 = (bf16[128,1024]{1,0:T(8,128)(2,1)}, bf16[128,1024]{1,0:T(8,128)(2,1)S(1)}, u32[]{:S(2)}, u32[]{:S(2)}) collective-permute-start(bf16[128,1024]{1,0:T(8,128)(2,1)} %collective-permute-done.3), channel_id=1, source_target_pairs={{0,2},{1,3},{2,0},{3,1},{4,6},{5,7},{6,4},{7,5},{8,10},{9,11},{10,... | collective-permute-start | bytes 786440 | tf_op jit(solution)/shard_map/ppermute | solution.py:24
  53.0 6.4 %collective-permute-start.8 = (bf16[128,1024]{1,0:T(8,128)(2,1)S(1)}, bf16[128,1024]{1,0:T(8,128)(2,1)S(1)}, u32[]{:S(2)}, u32[]{:S(2)}) collective-permute-start(bf16[128,1024]{1,0:T(8,128)(2,1)S(1)} %collective-permute-done.6), channel_id=1, source_target_pairs={{0,1},{1,0},{2,3},{3,2},{4,5},{5,4},{6,7},{7,6},{8,9},{9,8},{10,11... | collective-permute-start | bytes 786440 | tf_op jit(solution)/shard_map/ppermute | solution.py:24
  60.2 4.3 %collective-permute-start.9 = (bf16[256,128]{0,1:T(8,128)(2,1)S(1)}, bf16[256,128]{0,1:T(8,128)(2,1)S(1)}, u32[]{:S(2)}, u32[]{:S(2)}) collective-permute-start(bf16[256,128]{0,1:T(8,128)(2,1)S(1)} %multiply_convert_fusion.6), channel_id=1, source_target_pairs={{0,1},{1,0},{2,3},{3,2},{4,5},{5,4},{6,7},{7,6},{8,9},{9,8},{10,11... | collective-permute-start | bytes 196616 | tf_op jit(solution)/shard_map/ppermute | solution.py:24
  62.2 5.3 %copy-start.12 = (f32[256]{0:T(256)S(1)}, f32[256]{0:T(256)}, u32[]{:S(2)}) copy-start(f32[256]{0:T(256)} %exp.68) | copy-start | bytes 3076
  62.3 16.8 %copy-start.5 = (f32[256]{0:T(256)S(1)}, f32[256]{0:T(256)}, u32[]{:S(2)}) copy-start(f32[256]{0:T(256)} %select_n.279) | copy-start | bytes 3076
  64.8 2.7 %collective-permute-start.10 = (bf16[256,128]{1,0:T(8,128)(2,1)S(1)}, bf16[256,128]{1,0:T(8,128)(2,1)S(1)}, u32[]{:S(2)}, u32[]{:S(2)}) collective-permute-start(bf16[256,128]{1,0:T(8,128)(2,1)S(1)} %select_convert_fusion.2), channel_id=1, source_target_pairs={{0,4},{4,0},{8,12},{12,8},{16,20},{20,16},{24,28},{28,24},{1,5},{5... | collective-permute-start | bytes 196616 | tf_op jit(solution)/shard_map/ppermute | solution.py:24
  67.5 13.6 %copy-start.6 = (f32[256]{0:T(256)S(1)}, f32[256]{0:T(256)}, u32[]{:S(2)}) copy-start(f32[256]{0:T(256)} %select_n.279) | copy-start | bytes 3076
  67.6 8.5 %collective-permute-start.12 = (bf16[256,128]{1,0:T(8,128)(2,1)S(1)}, bf16[256,128]{1,0:T(8,128)(2,1)S(1)}, u32[]{:S(2)}, u32[]{:S(2)}) collective-permute-start(bf16[256,128]{1,0:T(8,128)(2,1)S(1)} %fusion.37), channel_id=1, source_target_pairs={{0,8},{4,12},{8,16},{12,20},{16,24},{20,28},{24,0},{28,4},{1,9},{5... | collective-permute-start | bytes 196616 | tf_op jit(solution)/shard_map/ppermute | solution.py:13
  71.0 7.8 %collective-permute-start.14 = (bf16[256,128]{1,0:T(8,128)(2,1)S(1)}, bf16[256,128]{1,0:T(8,128)(2,1)S(1)}, u32[]{:S(2)}, u32[]{:S(2)}) collective-permute-start(bf16[256,128]{1,0:T(8,128)(2,1)S(1)} %fusion.37), channel_id=1, source_target_pairs={{0,16},{4,20},{8,24},{12,28},{16,0},{20,4},{24,8},{28,12},{1,17},{... | collective-permute-start | bytes 196616 | tf_op jit(solution)/shard_map/ppermute | solution.py:13
  73.7 5.4 %collective-permute-start.16 = (bf16[256,128]{1,0:T(8,128)(2,1)S(1)}, bf16[256,128]{1,0:T(8,128)(2,1)S(1)}, u32[]{:S(2)}, u32[]{:S(2)}) collective-permute-start(bf16[256,128]{1,0:T(8,128)(2,1)S(1)} %fusion.37), channel_id=1, source_target_pairs={{0,24},{4,28},{8,0},{12,4},{16,8},{20,12},{24,16},{28,20},{1,25},{... | collective-permute-start | bytes 196616 | tf_op jit(solution)/shard_map/ppermute | solution.py:13
  79.3 1.8 %collective-permute-start.17 = (bf16[256,128]{1,0:T(8,128)(2,1)S(1)}, bf16[256,128]{1,0:T(8,128)(2,1)S(1)}, u32[]{:S(2)}, u32[]{:S(2)}) collective-permute-start(bf16[256,128]{1,0:T(8,128)(2,1)S(1)} %select_convert_fusion), channel_id=1, source_target_pairs={{0,4},{4,0},{8,12},{12,8},{16,20},{20,16},{24,28},{28,24},{1,5},{5... | collective-permute-start | bytes 196616 | tf_op jit(solution)/shard_map/ppermute | solution.py:24
  79.3 2.5 %copy-start.3 = (f32[256,512]{1,0:T(8,128)S(1)}, f32[256,512]{1,0:T(8,128)}, u32[]{:S(2)}) copy-start(f32[256,512]{1,0:T(8,128)} %fusion.1) | copy-start | bytes 1572868
  81.3 6.0 %copy-start.13 = (f32[512]{0:T(512)S(1)}, f32[512]{0:T(512)}, u32[]{:S(2)}) copy-start(f32[512]{0:T(512)} %param.23) | copy-start | bytes 6148
  83.7 3.6 %collective-permute-start.18 = (f32[256]{0:T(256)S(1)}, f32[256]{0:T(256)S(1)}, u32[]{:S(2)}, u32[]{:S(2)}) collective-permute-start(f32[256]{0:T(256)S(1)} %get-tuple-element.28), channel_id=1, source_target_pairs={{0,1},{1,0},{2,3},{3,2},{4,5},{5,4},{6,7},{7,6},{8,9},{9,8},{10,11... | collective-permute-start | bytes 3080 | tf_op jit(solution)/shard_map/ppermute | solution.py:24

commit v2 on v0

v2 whole, which is shorter than its diff:
```python
import functools

import jax
import jax.numpy as jnp
from jax import lax
from jax.experimental import pallas as pl
from jax.experimental.pallas import tpu as pltpu
from jax.sharding import PartitionSpec as P

KERNEL = 4
RIM = 8
PAD = 8
F32, BF16 = jnp.float32, jnp.bfloat16
EXACT = lax.Precision.HIGHEST
VMEM = pl.BlockSpec(memory_space=pltpu.VMEM)
HBM = pl.BlockSpec(memory_space=pltpu.HBM)


def run(body, outs, *operands, scratch=(), flops=1000000, hbm=0, limit=4 << 20):
    single = not isinstance(outs, list)
    shapes = [jax.ShapeDtypeStruct(*o) for o in ([outs] if single else outs)]
    results = pl.pallas_call(
        body,
        out_shape=shapes,
        in_specs=[HBM] * hbm + [VMEM] * (len(operands) - hbm),
        out_specs=[VMEM] * len(shapes),
        scratch_shapes=list(scratch),
        compiler_params=pltpu.CompilerParams(vmem_limit_bytes=limit),
        cost_estimate=pl.CostEstimate(flops=flops, bytes_accessed=flops // 400, transcendentals=0),
        name=body.func.__name__ if isinstance(body, functools.partial) else body.__name__,
    )(*operands)
    return results[0] if single else results


def hop(value, axis, distance):
    size = lax.axis_size(axis)
    return lax.ppermute(value, axis, [(i, (i + distance) % size) for i in range(size)])


def partner(value, axis, mask):
    return lax.ppermute(value, axis, [(i, i ^ mask) for i in range(lax.axis_size(axis))])


def dot(a, b, **kwargs):
    return jnp.dot(a, b, preferred_element_type=F32, **kwargs)


def silu(v):
    return v / (1.0 + jnp.exp(-v))


def holds_b():
    return lax.axis_index("tp") % 2 == 0


def first_core():
    return lax.axis_index("ctx") % 2 == 0


def fetched_rows(start, source, out, arrival):
    copy = pltpu.make_async_copy(source.at[pl.ds(start, out.shape[0])], out, arrival)
    copy.start()
    copy.wait()


def own_product(w_bc, w_x, w_z, top, bottom, sums, weights, arrivals):
    size, depth, _ = weights.shape
    place = lax.axis_index("tp")
    copies = []
    for mask in range(size):
        source_rows = pl.ds(pl.multiple_of(jnp.bitwise_xor(place, mask) * depth, depth), depth)
        column = 0
        for i, w in enumerate((w_bc, w_x, w_z)):
            columns = pl.ds(column, w.shape[1])
            copies.append(
                pltpu.make_async_copy(
                    w.at[source_rows], weights.at[mask, :, columns], arrivals.at[mask, i]
                )
            )
            column += w.shape[1]
    for copy in copies:
        copy.start()
    for copy in copies[:3]:
        copy.wait()
    sums[...] = dot(jnp.concatenate([top[...], bottom[...]], axis=0), weights[0])
    for copy in copies[3:]:
        copy.wait()


def block_of(pieces, i):
    return jnp.concatenate([pieces[2 * i][...], pieces[2 * i + 1][...]], axis=0)


def middle_product(masks, *refs):
    pieces, (weights, before, _, out) = refs[: 2 * len(masks)], refs[2 * len(masks) :]
    total = before[...]
    for i, mask in enumerate(masks):
        total += dot(block_of(pieces, i), weights[mask])
    out[...] = total


def rim_product(rim, weights, out):
    total = None
    for mask in range(weights.shape[0]):
        columns = pl.ds(0, out.shape[1])
        term = dot(rim[pl.ds(mask * RIM, RIM), :], weights[mask, :, columns])
        total = term if total is None else total + term
    inside = lax.axis_index("ctx") > 0
    out[...] = jnp.where(inside, total, 0.0).astype(BF16).astype(F32)


def finished(masks, pieces, weights, before, start, width):
    columns = pl.ds(start, width)
    total = before[:, columns]
    for i, mask in enumerate(masks):
        total += dot(block_of(pieces, i), weights[mask, :, columns])
    return total.astype(BF16).astype(F32)


def convolved(pre, rim, taps, bias, extended):
    rows = pre.shape[0]
    extended[pl.ds(0, RIM), :] = rim
    extended[pl.ds(RIM, rows), :] = pre
    total = bias[...]
    for k in range(KERNEL):
        total = total + taps[pl.ds(k, 1), :] * extended[pl.ds(RIM - KERNEL + 1 + k, rows), :]
    return silu(total).astype(BF16)


def last_bc(masks, *refs):
    pieces, refs = refs[: 2 * len(masks)], refs[2 * len(masks) :]
    weights, before, rim, taps, bias, out, extended = refs
    width = out.shape[1]
    pre = finished(masks, pieces, weights, before, 0, width)
    out[...] = convolved(pre, rim[:, pl.ds(0, width)], taps, bias, extended)


def last_x(masks, *refs):
    pieces, refs = refs[: 2 * len(masks)], refs[2 * len(masks) :]
    weights, before, rim, taps, bias, end_weight, x_out, weighted_out, extended = refs
    width = x_out.shape[1]
    start = rim.shape[1] - width
    pre = finished(masks, pieces, weights, before, start, width)
    x = convolved(pre, rim[:, pl.ds(start, width)], taps, bias, extended)
    x_out[...] = x
    weighted_out[...] = (x.astype(F32) * end_weight[...]).astype(BF16)


def last_z(masks, *refs):
    pieces, (weights, before, _, out) = refs[: 2 * len(masks)], refs[2 * len(masks) :]
    width = out.shape[1]
    out[...] = silu(finished(masks, pieces, weights, before, before.shape[1] - width, width))


def decays(decay_t, step, skip, segment, grown, end_weight, whole, skip_wide):
    heads, rows = decay_t.shape
    width = grown.shape[1]
    dim = width // heads
    spread = (
        lax.broadcasted_iota(jnp.int32, (heads, width), 1) // dim
        == lax.broadcasted_iota(jnp.int32, (heads, width), 0)
    ).astype(F32)
    i = lax.broadcasted_iota(jnp.int32, (rows, rows), 0)
    j = lax.broadcasted_iota(jnp.int32, (rows, rows), 1)
    causal = i >= j
    cum = lax.dot_general(
        causal.astype(F32),
        decay_t[...],
        (((1,), (1,)), ((), ())),
        precision=EXACT,
        preferred_element_type=F32,
    )
    cum_t = dot(decay_t[...], (i <= j).astype(F32), precision=EXACT)
    cum_wide = dot(cum, spread, precision=EXACT)
    total = cum_wide[rows - 1 :]
    grown[...] = jnp.exp(cum_wide)
    end_weight[...] = jnp.exp(total - cum_wide) * dot(step[...], spread, precision=EXACT)
    whole[...] = jnp.broadcast_to(jnp.exp(total), whole.shape)
    skip_wide[...] = dot(skip[...], spread, precision=EXACT)
    for h in range(heads):
        difference = cum[:, h : h + 1] - cum_t[h : h + 1, :]
        factor = jnp.where(causal, jnp.exp(jnp.where(causal, difference, 0.0)), 0.0)
        segment[h] = (factor * step[:, h : h + 1]).astype(BF16)


def halves(wide):
    half = wide.shape[1] // 2
    return wide[:, :half], wide[:, half:]


def mine_other(wide):
    low, high = halves(wide)
    first = first_core()
    return jnp.where(first, low, high), jnp.where(first, high, low)


def write_message(out, state, decay):
    n = state.shape[0]
    out[pl.ds(0, n), :] = state.astype(BF16)
    decay = jnp.broadcast_to(decay, (PAD, decay.shape[1]))
    high = decay.astype(BF16).astype(F32)
    out[pl.ds(n, 2 * PAD), :] = jnp.concatenate([high, decay - high], axis=0).astype(BF16)


def read_message(ref):
    n = ref.shape[0] - 2 * PAD
    tail = ref[pl.ds(n, 2 * PAD), :].astype(F32)
    return ref[pl.ds(0, n), :].astype(F32), tail[:1] + tail[PAD : PAD + 1]


def section_state(own_bc, other_bc, weighted, whole, message, kept):
    b = jnp.where(holds_b(), own_bc[...], other_bc[...])
    state = lax.dot_general(
        b, weighted[...], (((0,), (0,)), ((), ())), preferred_element_type=F32
    )
    mine, other = mine_other(state)
    _, other_decay = mine_other(whole[...])
    kept[...] = mine
    write_message(message, other, other_decay[:1])


def pair_states(kept, whole, received):
    sibling, sibling_decay = read_message(received)
    mine_decay, _ = mine_other(whole[...])
    mine_decay = mine_decay[:1]
    first = first_core()
    mine = kept[...]
    return (
        (jnp.where(first, mine, sibling), jnp.where(first, mine_decay, sibling_decay)),
        (jnp.where(first, sibling, mine), jnp.where(first, sibling_decay, mine_decay)),
    )


def chip_state(kept, whole, received, message):
    (first, first_decay), (second, second_decay) = pair_states(kept, whole, received)
    write_message(message, second + second_decay * first, first_decay * second_decay)


def entering_state(kept, whole, received, *refs):
    got, (_, _, keep, give) = refs[:-4], refs[-4:]
    (first, first_decay), _ = pair_states(kept, whole, received)
    chip = lax.axis_index("ctx") // 2
    before = jnp.zeros_like(first)
    between = jnp.ones_like(first_decay)
    for k, ref in enumerate(got):
        state, decay = read_message(ref)
        before += jnp.where(chip > k, between, 0.0) * state
        between = between * decay
    after = first + first_decay * before
    lead = first_core()
    keep[...] = jnp.where(lead, before, after).astype(BF16)
    give[...] = jnp.where(lead, after, before).astype(BF16)


def within_section(own_bc, other_bc, x, segment, skip_wide, _, out):
    own, other = own_bc[...], other_bc[...]
    b = jnp.where(holds_b(), own, other)
    c = jnp.where(holds_b(), other, own)
    scores = lax.dot_general(c, b, (((1,), (1,)), ((), ())), preferred_element_type=F32)
    heads = segment.shape[0]
    dim = x.shape[1] // heads
    low = lax.broadcasted_iota(jnp.int32, (1, 2 * dim), 1) < dim
    for pair in range(heads // 2):
        columns = pl.ds(pair * 2 * dim, 2 * dim)
        mixing = jnp.concatenate(
            [(segment[2 * pair + s].astype(F32) * scores).astype(BF16) for s in range(2)], axis=1
        )
        both = x[:, columns]
        wide = both.astype(F32)
        stacked = jnp.concatenate(
            [jnp.where(low, wide, 0.0).astype(BF16), jnp.where(low, 0.0, wide).astype(BF16)], axis=0
        )
        out[:, columns] = dot(mixing, stacked) + skip_wide[:, columns] * wide


def gated_output(own_bc, other_bc, keep, take, within, grown, gate, gated_out, square_out):
    lead = first_core()
    low = jnp.where(lead, keep[...], take[...])
    high = jnp.where(lead, take[...], keep[...])
    c = jnp.where(holds_b(), other_bc[...], own_bc[...])
    half = low.shape[1]
    squares = None
    for s, entering in enumerate((low, high)):
        columns = pl.ds(s * half, half)
        inter = dot(c, entering) * grown[:, columns]
        gated = (within[:, columns] + inter) * gate[:, columns]
        gated_out[:, columns] = gated
        for start in range(0, half, 128):
            part = gated[:, start : start + 128]
            squares = part * part if squares is None else squares + part * part
    ones = jnp.ones((PAD, squares.shape[1]), F32)
    square_out[...] = lax.dot_general(
        ones, squares, (((1,), (1,)), ((), ())), precision=EXACT, preferred_element_type=F32
    )


def normed_output(gated, square, other_square, gain, out):
    width = gated.shape[1]
    mean = (square[...] + other_square[...]) / (2 * width)
    factor = lax.rsqrt(mean + 1e-05)
    share = jnp.full((PAD, 128), 1.0 / PAD, F32)
    column = lax.dot_general(
        factor, share, (((0,), (0,)), ((), ())), precision=EXACT, preferred_element_type=F32
    )
    for start in range(0, width, 128):
        columns = pl.ds(start, 128)
        out[:, columns] = (gated[:, columns] * column * gain[:, columns]).astype(BF16)


def gather_pieces(top, bottom, axis):
    size = lax.axis_size(axis)
    end = bottom.shape[0] - RIM
    near_bottom = partner(bottom, axis, 1)
    rim = jnp.concatenate([bottom[end:], near_bottom[end:]], axis=0)
    if size == 2:
        return {}, {1: [partner(top, axis, 1), near_bottom]}, rim
    far_top = partner(top, axis, 2)
    near_top = partner(top, axis, 1)
    far_bottom = partner(bottom, axis, 2)
    rim = jnp.concatenate([rim, partner(rim, axis, 2)], axis=0)
    across_bottom = partner(near_bottom, axis, 2)
    across_top = partner(far_top, axis, 1)
    early = {1: [near_top, near_bottom], 2: [far_top, far_bottom]}
    last = {3: [across_top, across_bottom]}
    mask = 4
    while mask < size:
        early = {**early, **last}
        last = {m | mask: [partner(h, axis, mask) for h in p] for m, p in early.items()}
        last[mask] = [partner(h, axis, mask) for h in (top, bottom)]
        rim = jnp.concatenate([rim, partner(rim, axis, mask)], axis=0)
        mask *= 2
    return early, last, rim


def local(
    tokens, w_z, w_x, w_bc, conv_x, conv_bc, bias_x, bias_bc, decay_logarithm, head_step, skip, gain
):
    rows, depth = tokens.shape
    width, bc_width = w_x.shape[1], w_bc.shape[1]
    heads = head_step.shape[0]
    n = bc_width
    chips = lax.axis_size("ctx") // 2

    half = rows // 2
    arrival = [pltpu.SemaphoreType.DMA]
    bottom, top = [
        run(functools.partial(fetched_rows, start), ((half, depth), BF16), tokens, scratch=arrival, hbm=1)
        for start in (half, 0)
    ]
    early, last, rim = gather_pieces(top, bottom, "tp")
    rim = hop(rim, "ctx", 1)

    def flops(*sizes):
        total = 2
        for s in sizes:
            total *= s
        return total

    size = lax.axis_size("tp")
    everything = bc_width + 2 * width
    sums, weights = run(
        own_product,
        [((rows, everything), F32), ((size, depth, everything), BF16)],
        w_bc, w_x, w_z, top, bottom,
        scratch=[pltpu.SemaphoreType.DMA((size, 3))],
        flops=flops(rows, depth, everything),
        hbm=3,
    )
    segment, grown, end_weight, whole, skip_wide = run(
        decays,
        [
            ((heads, rows, rows), BF16),
            ((rows, width), F32),
            ((rows, width), F32),
            ((PAD, width), F32),
            ((1, width), F32),
        ],
        decay_logarithm.T, head_step.reshape(1, -1), skip.reshape(1, -1),
        flops=flops(rows, rows, width),
    )
    if early:
        masks = tuple(sorted(early))
        sums = run(
            functools.partial(middle_product, masks),
            ((rows, everything), F32),
            *[h for m in masks for h in early[m]], weights, sums, skip_wide,
            flops=len(masks) * flops(rows, depth, everything),
        )
    rim_sums = run(
        rim_product,
        ((RIM, bc_width + width), F32),
        rim, weights,
        flops=flops(rows, depth, width),
    )

    masks = tuple(sorted(last))
    ends = [h for m in masks for h in last[m]]
    own_bc = run(
        functools.partial(last_bc, masks),
        ((rows, bc_width), BF16),
        *ends, weights, sums, rim_sums, conv_bc, bias_bc.reshape(1, -1),
        scratch=[pltpu.VMEM((rows + RIM, bc_width), F32)],
        flops=flops(rows, depth, bc_width),
    )
    other_bc = partner(own_bc, "tp", 1)
    x, weighted = run(
        functools.partial(last_x, masks),
        [((rows, width), BF16), ((rows, width), BF16)],
        *ends, weights, sums, rim_sums, conv_x, bias_x.reshape(1, -1), end_weight,
        scratch=[pltpu.VMEM((rows + RIM, width), F32)],
        flops=flops(rows, depth, width),
    )
    message_shape = ((n + 2 * PAD, width // 2), BF16)
    state_shape = (n, width // 2)
    message, kept = run(
        section_state,
        [message_shape, (state_shape, F32)],
        own_bc, other_bc, weighted, whole,
        flops=flops(rows, n, width),
    )
    received = partner(message, "ctx", 1)
    message = run(chip_state, message_shape, kept, whole, received)
    got = [hop(message, "ctx", 2 * k) for k in range(1, chips)]
    within = run(
        within_section,
        ((rows, width), F32),
        own_bc, other_bc, x, segment, skip_wide, message,
        flops=3 * flops(rows, rows, width),
    )
    gate = run(
        functools.partial(last_z, masks),
        ((rows, width), F32),
        *ends, weights, sums, message,
        flops=flops(rows, depth, width),
    )
    keep, give = run(
        entering_state, [(state_shape, BF16), (state_shape, BF16)], kept, whole, received, *got, within, gate
    )
    take = partner(give, "ctx", 1)
    gated, square = run(
        gated_output,
        [((rows, width), F32), ((PAD, rows), F32)],
        own_bc, other_bc, keep, take, within, grown, gate,
        flops=flops(rows, n, width),
    )
    other_square = partner(square, "tp", 1)
    return run(
        normed_output, ((rows, width), BF16), gated, square, other_square, gain.reshape(1, -1)
    )


def solution(mesh):
    in_specs = (
        P("ctx", "tp"),
        P(None, "tp"),
        P(None, "tp"),
        P(None, "tp"),
        P(None, "tp"),
        P(None, "tp"),
        P("tp"),
        P("tp"),
        P("ctx", "tp"),
        P("tp"),
        P("tp"),
        P("tp"),
    )
    out_specs = P("ctx", "tp")
    return jax.shard_map(local, mesh=mesh, in_specs=in_specs, out_specs=out_specs, check_vma=False)
```

time: 118 us -> 52.9 us (0.45)
  waiting for transfers between devices: 57.4 us -> 21.9 us
  blocking collectives: 14.2 us -> 0 us
  between operations: 13.6 us -> 0.26 us
  matrix products: 12.7 us -> 0 us
  other arithmetic: 12 us -> 0.01 us
  Pallas kernels: 0 us -> 9.86 us
  starting transfers between devices: 4.68 us -> 13.7 us
  local copies, waits for them, and re-layouts: 2.46 us -> 6.82 us
    all_gather x2 -> x0, waiting for transfers between devices: 51.2 us -> none  [the longest x1 35.9 us: local(): gathered = lax.all_gather(tokens, 'tp', axis=1, tiled=True)]
    ppermute x3 -> x15, waiting for transfers between devices: 5.5 us -> 21.9 us  [the longest x11 13.9 us: partner(): lax.ppermute(value, axis, [(i, i ^ mask) for i in range(lax.axis_size(axi...]
    all_gather x1 -> x0, blocking collectives: 14.2 us -> none  [carried_in(): everything = jax.tree.map(lambda part: lax.all_gather(part, axis), shard)]
    dot_general x7 -> x0, matrix products: 12.7 us -> none  [the longest x1 4.28 us: local(): gate_sum = jnp.dot(gathered, w_z, preferred_element_type=jnp.float32)]
    pallas_call x0 -> x15, Pallas kernels: none -> 9.86 us  [run(): pl.pallas_call(body, out_shape=shapes, in_specs=[HBM] * hbm + [VMEM] * (l...]
    ppermute x3 -> x15, starting transfers between devices: 4.64 us -> 13.7 us  [the longest x11 9.81 us: partner(): lax.ppermute(value, axis, [(i, i ^ mask) for i in range(lax.axis_size(axi...]
    select_n x8 -> x0, other arithmetic: 8.42 us -> none  [lap(): return jax.tree.map(lambda a, b: jnp.where(reached, a, b), new, before)]
    unnamed x15 -> x24, local copies, waits for them, and re-layouts: 0.74 us -> 6.81 us
  transfers between devices with their start and end apart: 5 -> 15, of which waited for: 5 -> 8; matrix products, arithmetic and copies ran while one was open for 5% -> 0% of each run, Pallas kernels for 0% -> 14%
where the time goes in v2:
time: 52.9 us; the launch traced here: 52.6 us
  waiting for transfers between devices  21.9 us (41%)
  starting transfers between devices  13.7 us (26%)
  Pallas kernels  9.86 us (19%)
  local copies, waits for them, and re-layouts  6.82 us (13%)
    ppermute x11, waiting for transfers between devices, partner(): lax.ppermute(value, axis, [(i, i ^ mask) for i in range(lax.axis_size(axi...  13.9 us
    pallas_call x15, Pallas kernels, run(): pl.pallas_call(body, out_shape=shapes, in_specs=[HBM] * hbm + [VMEM] * (l...  9.86 us
    ppermute x11, starting transfers between devices, partner(): lax.ppermute(value, axis, [(i, i ^ mask) for i in range(lax.axis_size(axi...  9.81 us
    ppermute x4, waiting for transfers between devices, hop(): lax.ppermute(value, axis, [(i, (i + distance) % size) for i in range(size)])  7.99 us
    unnamed x24, local copies, waits for them, and re-layouts  6.81 us
    ppermute x4, starting transfers between devices, hop(): lax.ppermute(value, axis, [(i, (i + distance) % size) for i in range(size)])  3.93 us
  transfers between devices with their start and end apart: 15, of which 8 were waited for; matrix products, arithmetic and copies ran while one was open for 0% of the time, Pallas kernels for 14%

profile of v2, /device:TPU:0, one launch (start us, length us, event | category | flops | bytes accessed | tf_op | source)
XLA Modules:
  0.0 52.6 jit_solution(1195920059680182856)
XLA Ops:
  0.0 0.0 copy-start.2
  0.0 1.0 %copy-done.2 = bf16[256,1024]{1,0:T(8,128)(2,1)S(1)} copy-done((bf16[256,1024]{1,0:T(8,128)(2,1)S(1)}, bf16[256,1024]{1,0:T(8,128)(2,1)}, u32[]{:S(2)}) %copy-start.2) | copy-done | bytes 524312
  1.1 3.0 %collective-permute-start.2 = (bf16[128,1024]{1,0:T(8,128)(2,1)S(1)}, bf16[128,1024]{1,0:T(8,128)(2,1)S(1)}, u32[]{:S(2)}, u32[]{:S(2)}) collective-permute-start(bf16[128,1024]{1,0:T(8,128)(2,1)S(1)} %fetched_rows.3.bottom), channel_id=1, source_target_pairs={{0,1},{1,0},{2,3},{3,2},{4,5},{5,4},{6,7},{7,6},{8,9},{9,8},{10,11... | collective-permute-start | bytes 786440 | tf_op jit(solution)/shard_map/ppermute | solution.py:41
  4.1 1.6 %collective-permute-start = (bf16[128,1024]{1,0:T(8,128)(2,1)S(1)}, bf16[128,1024]{1,0:T(8,128)(2,1)S(1)}, u32[]{:S(2)}, u32[]{:S(2)}) collective-permute-start(bf16[128,1024]{1,0:T(8,128)(2,1)S(1)} %fetched_rows.2.top), channel_id=1, source_target_pairs={{0,2},{1,3},{2,0},{3,1},{4,6},{5,7},{6,4},{7,5},{8,10},{9,11},{10,... | collective-permute-start | bytes 786440 | tf_op jit(solution)/shard_map/ppermute | solution.py:41
  5.7 0.5 collective-permute-start.5
  6.2 0.1 collective-permute-start.4
  6.3 4.9 %collective-permute-done.2.refs_1_ = bf16[128,1024]{1,0:T(8,128)(2,1)S(1)} collective-permute-done((bf16[128,1024]{1,0:T(8,128)(2,1)S(1)}, bf16[128,1024]{1,0:T(8,128)(2,1)S(1)}, u32[]{:S(2)}, u32[]{:S(2)}) %collective-permute-start.2) | collective-permute-done | bytes 262176 | tf_op jit(solution)/shard_map/ppermute | solution.py:41
  11.3 0.0 copy-start.9
  11.3 0.0 copy-start.11
  11.3 2.1 %collective-permute-start.6 = (bf16[16,1024]{1,0:T(8,128)(2,1)S(1)}, bf16[16,1024]{1,0:T(8,128)(2,1)S(1)}, u32[]{:S(2)}, u32[]{:S(2)}) collective-permute-start(bf16[16,1024]{1,0:T(8,128)(2,1)S(1)} %pad_maximum_fusion.1), channel_id=1, source_target_pairs={{0,2},{1,3},{2,0},{3,1},{4,6},{5,7},{6,4},{7,5},{8,10},{9,11},{10,... | collective-permute-start | bytes 98312 | tf_op jit(solution)/shard_map/ppermute | solution.py:41
  13.4 0.1 collective-permute-start.3
  13.5 0.0 collective-permute-done.refs_2_
  13.5 1.9 %collective-permute-start.1 = (bf16[128,1024]{1,0:T(8,128)(2,1)S(1)}, bf16[128,1024]{1,0:T(8,128)(2,1)S(1)}, u32[]{:S(2)}, u32[]{:S(2)}) collective-permute-start(bf16[128,1024]{1,0:T(8,128)(2,1)S(1)} %collective-permute-done.refs_2_), channel_id=1, source_target_pairs={{0,1},{1,0},{2,3},{3,2},{4,5},{5,4},{6,7},{7,6},{8,9},{9,8},{10,11... | collective-permute-start | bytes 786440 | tf_op jit(solution)/shard_map/ppermute | solution.py:41
  15.4 0.0 copy-start
  15.4 2.2 %copy-done = bf16[4096,512]{1,0:T(8,128)(2,1)S(1)} copy-done((bf16[4096,512]{1,0:T(8,128)(2,1)S(1)}, bf16[4096,512]{1,0:T(8,128)(2,1)}, u32[]{:S(2)}) %copy-start) | copy-done | bytes 4194328
  17.6 0.0 copy-start.1
  17.6 2.2 %copy-done.1 = bf16[4096,512]{1,0:T(8,128)(2,1)S(1)} copy-done((bf16[4096,512]{1,0:T(8,128)(2,1)S(1)}, bf16[4096,512]{1,0:T(8,128)(2,1)}, u32[]{:S(2)}) %copy-start.1) | copy-done | bytes 4194328
  19.8 1.2 %copy-done.3 = bf16[4096,128]{1,0:T(8,128)(2,1)S(1)} copy-done((bf16[4096,128]{1,0:T(8,128)(2,1)S(1)}, bf16[4096,128]{1,0:T(8,128)(2,1)}, u32[]{:S(2)}) %copy-start.3) | copy-done | bytes 1048600
  21.0 1.7 %own_product.1 = (f32[256,1152]{1,0:T(8,128)S(1)}, bf16[4,1024,1152]{2,1,0:T(8,128)(2,1)S(1)}) custom-call(bf16[4096,128]{1,0:T(8,128)(2,1)S(1)} %copy-done.3, bf16[4096,512]{1,0:T(8,128)(2,1)S(1)} %copy-done, bf16[4096,512]{1,0:T(8,128)(2,1)S(1)} %copy-done.1, bf16[128,1024]{1,0:T(8,128)(2,1)S(1)} %fetched_rows.2.top, bf16[128,1024]{1,0:T(8,128)(2,1)S(1)} %fetched_rows.3.bottom), custom_call_target="tpu_custom_call" | custom-call | flops 603979776 | bytes 1509949 | tf_op jit(solution)/shard_map/own_product/pallas_call | solution.py:22
  22.7 0.0 copy-done.9
  22.8 0.0 copy-done.10
  22.8 0.0 copy-done.11
  22.8 1.2 %decays.1 = (bf16[8,256,256]{2,1,0:T(8,128)(2,1)S(1)}, f32[256,512]{1,0:T(8,128)S(1)}, f32[256,512]{1,0:T(8,128)S(1)}, f32[8,512]{1,0:T(8,128)S(1)}, f32[1,512]{1,0:T(1,128)S(1)}) custom-call(f32[8,256]{1,0:T(8,128)S(1)} %bitcast.9, f32[1,8]{1,0:T(1,128)S(1)} %bitcast.10, f32[1,8]{1,0:T(1,128)S(1)} %bitcast.11), custom_call_target="tpu_custom_call" | custom-call | flops 67108864 | bytes 167772 | tf_op jit(solution)/shard_map/decays/pallas_call | solution.py:22
  23.9 0.0 collective-permute-done.6
  24.0 0.1 collective-permute-start.7
  24.0 0.0 collective-permute-done.5.refs_3_
  24.0 0.0 collective-permute-done.4.refs_0_
  24.0 1.5 %middle_product.1.refs_3_ = f32[256,1152]{1,0:T(8,128)S(1)} custom-call(bf16[128,1024]{1,0:T(8,128)(2,1)S(1)} %collective-permute-done.4.refs_0_, bf16[128,1024]{1,0:T(8,128)(2,1)S(1)} %collective-permute-done.2.refs_1_, bf16[128,1024]{1,0:T(8,128)(2,1)S(1)} %collective-permute-done.refs_2_, bf16[128,1024]{1,0:T(8,128)(2,1)S(1)} %collective-permute-done.5.refs_3_, ...), custom_call_target="tpu_custom_call" | custom-call | flops 1207959552 | bytes 3019898 | tf_op jit(solution)/shard_map/middle_product/pallas_call | solution.py:22
  25.6 0.0 copy-start.5
  25.6 0.0 copy-start.8
  25.6 3.9 %collective-permute-done.7.rim = bf16[32,1024]{1,0:T(8,128)(2,1)S(1)} collective-permute-done((bf16[32,1024]{1,0:T(8,128)(2,1)S(1)}, bf16[32,1024]{1,0:T(8,128)(2,1)S(1)}, u32[]{:S(2)}, u32[]{:S(2)}) %collective-permute-start.7) | collective-permute-done | bytes 65568 | tf_op jit(solution)/shard_map/ppermute | solution.py:37
  29.5 0.8 %rim_product.1.refs_4_ = f32[8,640]{1,0:T(8,128)S(1)} custom-call(bf16[32,1024]{1,0:T(8,128)(2,1)S(1)} %collective-permute-done.7.rim, bf16[4,1024,1152]{2,1,0:T(8,128)(2,1)S(1)} %get-tuple-element.20.refs_4_.weights.refs_2_), custom_call_target="tpu_custom_call" | custom-call | flops 268435456 | bytes 671088 | tf_op jit(solution)/shard_map/rim_product/pallas_call | solution.py:22
  30.3 0.0 collective-permute-done.3.refs_1_
  30.3 0.0 collective-permute-done.1.refs_0_
  30.3 0.0 copy-done.5
  30.3 0.0 copy-done.8
  30.3 0.0 copy-start.4
  30.3 0.0 copy-start.6
  30.4 0.4 last_bc.1.own_bc
  30.7 0.2 collective-permute-start.8
  30.9 0.1 copy-done.4
  31.0 0.0 copy-done.6
  31.0 1.1 %last_x.1 = (bf16[256,512]{1,0:T(8,128)(2,1)S(1)}, bf16[256,512]{1,0:T(8,128)(2,1)S(1)}) custom-call(bf16[128,1024]{1,0:T(8,128)(2,1)S(1)} %collective-permute-done.1.refs_0_, bf16[128,1024]{1,0:T(8,128)(2,1)S(1)} %collective-permute-done.3.refs_1_, bf16[4,1024,1152]{2,1,0:T(8,128)(2,1)S(1)} %get-tuple-element.20.refs_4_.weights.refs_2_, ...), custom_call_target="tpu_custom_call" | custom-call | flops 268435456 | bytes 671088 | tf_op jit(solution)/shard_map/last_x/pallas_call | solution.py:22
  32.1 2.9 %collective-permute-done.8.other_bc = bf16[256,128]{1,0:T(8,128)(2,1)S(1)} collective-permute-done((bf16[256,128]{1,0:T(8,128)(2,1)S(1)}, bf16[256,128]{1,0:T(8,128)(2,1)S(1)}, u32[]{:S(2)}, u32[]{:S(2)}) %collective-permute-start.8) | collective-permute-done | bytes 65568 | tf_op jit(solution)/shard_map/ppermute | solution.py:41
  35.1 0.2 section_state.1
  35.3 0.1 collective-permute-start.9
  35.4 1.3 %collective-permute-done.9.received = bf16[144,256]{1,0:T(8,128)(2,1)S(1)} collective-permute-done((bf16[144,256]{1,0:T(8,128)(2,1)S(1)}, bf16[144,256]{1,0:T(8,128)(2,1)S(1)}, u32[]{:S(2)}, u32[]{:S(2)}) %collective-permute-start.9) | collective-permute-done | bytes 73760 | tf_op jit(solution)/shard_map/ppermute | solution.py:41
  36.7 0.1 collective-permute-start.10
  36.7 2.4 %collective-permute-start.11 = (bf16[144,256]{1,0:T(8,128)(2,1)S(1)}, bf16[144,256]{1,0:T(8,128)(2,1)S(1)}, u32[]{:S(2)}, u32[]{:S(2)}) collective-permute-start(bf16[144,256]{1,0:T(8,128)(2,1)S(1)} %chip_state.1._.refs_4_), channel_id=1, source_target_pairs={{0,16},{4,20},{8,24},{12,28},{16,0},{20,4},{24,8},{28,12},{1,17},{... | collective-permute-start | bytes 221192 | tf_op jit(solution)/shard_map/ppermute | solution.py:37
  39.1 1.5 %collective-permute-start.12 = (bf16[144,256]{1,0:T(8,128)(2,1)S(1)}, bf16[144,256]{1,0:T(8,128)(2,1)S(1)}, u32[]{:S(2)}, u32[]{:S(2)}) collective-permute-start(bf16[144,256]{1,0:T(8,128)(2,1)S(1)} %chip_state.1._.refs_4_), channel_id=1, source_target_pairs={{0,24},{4,28},{8,0},{12,4},{16,8},{20,12},{24,16},{28,20},{1,25},{... | collective-permute-start | bytes 221192 | tf_op jit(solution)/shard_map/ppermute | solution.py:37
  40.5 0.7 %within_section.1.refs_3_.within = f32[256,512]{1,0:T(8,128)S(1)} custom-call(bf16[256,128]{1,0:T(8,128)(2,1)S(1)} %last_bc.1.own_bc, bf16[256,128]{1,0:T(8,128)(2,1)S(1)} %collective-permute-done.8.other_bc, bf16[256,512]{1,0:T(8,128)(2,1)S(1)} %get-tuple-element.28.x, bf16[8,256,256]{2,1,0:T(8,128)(2,1)S(1)} %get-tuple-element.29.segment, ...), custom_call_target="tpu_custom_call" | custom-call | flops 201326592 | bytes 503316 | tf_op jit(solution)/shard_map/within_section/pallas_call | solution.py:22
  41.2 0.0 copy-start.7
  41.2 0.5 %last_z.1.refs_4_.gate = f32[256,512]{1,0:T(8,128)S(1)} custom-call(bf16[128,1024]{1,0:T(8,128)(2,1)S(1)} %collective-permute-done.1.refs_0_, bf16[128,1024]{1,0:T(8,128)(2,1)S(1)} %collective-permute-done.3.refs_1_, bf16[4,1024,1152]{2,1,0:T(8,128)(2,1)S(1)} %get-tuple-element.20.refs_4_.weights.refs_2_, f32[256,1152]{1,0:T(8,128)S(1)} %middle_product.1.refs_3_, ...), custom_call_target="tpu_custom_call" | custom-call | flops 268435456 | bytes 671088 | tf_op jit(solution)/shard_map/last_z/pallas_call | solution.py:22
  41.8 1.9 %collective-permute-done.10.refs_0_ = bf16[144,256]{1,0:T(8,128)(2,1)S(1)} collective-permute-done((bf16[144,256]{1,0:T(8,128)(2,1)S(1)}, bf16[144,256]{1,0:T(8,128)(2,1)S(1)}, u32[]{:S(2)}, u32[]{:S(2)}) %collective-permute-start.10) | collective-permute-done | bytes 73760 | tf_op jit(solution)/shard_map/ppermute | solution.py:37
  43.7 2.1 %collective-permute-done.11.refs_1_ = bf16[144,256]{1,0:T(8,128)(2,1)S(1)} collective-permute-done((bf16[144,256]{1,0:T(8,128)(2,1)S(1)}, bf16[144,256]{1,0:T(8,128)(2,1)S(1)}, u32[]{:S(2)}, u32[]{:S(2)}) %collective-permute-start.11) | collective-permute-done | bytes 73760 | tf_op jit(solution)/shard_map/ppermute | solution.py:37
  45.9 0.0 collective-permute-done.12.refs_2_
  45.9 0.1 entering_state.1
  46.0 0.1 collective-permute-start.13
  46.1 1.2 %collective-permute-done.13.take = bf16[128,256]{1,0:T(8,128)(2,1)S(1)} collective-permute-done((bf16[128,256]{1,0:T(8,128)(2,1)S(1)}, bf16[128,256]{1,0:T(8,128)(2,1)S(1)}, u32[]{:S(2)}, u32[]{:S(2)}) %collective-permute-start.13) | collective-permute-done | bytes 65568 | tf_op jit(solution)/shard_map/ppermute | solution.py:41
  47.3 0.5 %gated_output.1 = (f32[256,512]{1,0:T(8,128)S(1)}, f32[8,256]{1,0:T(8,128)S(1)}) custom-call(bf16[256,128]{1,0:T(8,128)(2,1)S(1)} %last_bc.1.own_bc, bf16[256,128]{1,0:T(8,128)(2,1)S(1)} %collective-permute-done.8.other_bc, bf16[128,256]{1,0:T(8,128)(2,1)S(1)} %get-tuple-element.30.keep, bf16[128,256]{1,0:T(8,128)(2,1)S(1)} %collective-permute-done.13.take, ...), custom_call_target="tpu_custom_call" | custom-call | flops 33554432 | bytes 83886 | tf_op jit(solution)/shard_map/gated_output/pallas_call | solution.py:22
  47.8 0.2 collective-permute-start.14
  48.0 3.5 %collective-permute-done.14.other_square = f32[8,256]{1,0:T(8,128)S(1)} collective-permute-done((f32[8,256]{1,0:T(8,128)S(1)}, f32[8,256]{1,0:T(8,128)S(1)}, u32[]{:S(2)}, u32[]{:S(2)}) %collective-permute-start.14) | collective-permute-done | bytes 8224 | tf_op jit(solution)/shard_map/ppermute | solution.py:41
  51.5 0.0 copy-done.7
  51.5 1.1 %normed_output.1 = bf16[256,512]{1,0:T(8,128)(2,1)} custom-call(f32[256,512]{1,0:T(8,128)S(1)} %get-tuple-element.33.gated, f32[8,256]{1,0:T(8,128)S(1)} %get-tuple-element.34.square, f32[8,256]{1,0:T(8,128)S(1)} %collective-permute-done.14.other_square, f32[1,512]{1,0:T(1,128)S(1)} %bitcast.7), custom_call_target="tpu_custom_call" | custom-call | flops 1000000 | bytes 2500 | tf_op jit(solution)/shard_map/normed_output/pallas_call | solution.py:22
  (9 shorter events, 0.1 us)
Async XLA Ops:
  0.0 1.0 %copy-start.2 = (bf16[256,1024]{1,0:T(8,128)(2,1)S(1)}, bf16[256,1024]{1,0:T(8,128)(2,1)}, u32[]{:S(2)}) copy-start(bf16[256,1024]{1,0:T(8,128)(2,1)} %source.3) | copy-start | bytes 1572868
  1.1 10.2 %collective-permute-start.2 = (bf16[128,1024]{1,0:T(8,128)(2,1)S(1)}, bf16[128,1024]{1,0:T(8,128)(2,1)S(1)}, u32[]{:S(2)}, u32[]{:S(2)}) collective-permute-start(bf16[128,1024]{1,0:T(8,128)(2,1)S(1)} %fetched_rows.3.bottom), channel_id=1, source_target_pairs={{0,1},{1,0},{2,3},{3,2},{4,5},{5,4},{6,7},{7,6},{8,9},{9,8},{10,11... | collective-permute-start | bytes 786440 | tf_op jit(solution)/shard_map/ppermute | solution.py:41
  4.1 9.3 %collective-permute-start = (bf16[128,1024]{1,0:T(8,128)(2,1)S(1)}, bf16[128,1024]{1,0:T(8,128)(2,1)S(1)}, u32[]{:S(2)}, u32[]{:S(2)}) collective-permute-start(bf16[128,1024]{1,0:T(8,128)(2,1)S(1)} %fetched_rows.2.top), channel_id=1, source_target_pairs={{0,2},{1,3},{2,0},{3,1},{4,6},{5,7},{6,4},{7,5},{8,10},{9,11},{10,... | collective-permute-start | bytes 786440 | tf_op jit(solution)/shard_map/ppermute | solution.py:41
  5.7 18.3 %collective-permute-start.5 = (bf16[128,1024]{1,0:T(8,128)(2,1)S(1)}, bf16[128,1024]{1,0:T(8,128)(2,1)S(1)}, u32[]{:S(2)}, u32[]{:S(2)}) collective-permute-start(bf16[128,1024]{1,0:T(8,128)(2,1)S(1)} %fetched_rows.3.bottom), channel_id=1, source_target_pairs={{0,2},{1,3},{2,0},{3,1},{4,6},{5,7},{6,4},{7,5},{8,10},{9,11},{10,... | collective-permute-start | bytes 786440 | tf_op jit(solution)/shard_map/ppermute | solution.py:41
  6.2 17.8 %collective-permute-start.4 = (bf16[128,1024]{1,0:T(8,128)(2,1)S(1)}, bf16[128,1024]{1,0:T(8,128)(2,1)S(1)}, u32[]{:S(2)}, u32[]{:S(2)}) collective-permute-start(bf16[128,1024]{1,0:T(8,128)(2,1)S(1)} %fetched_rows.2.top), channel_id=1, source_target_pairs={{0,1},{1,0},{2,3},{3,2},{4,5},{5,4},{6,7},{7,6},{8,9},{9,8},{10,11... | collective-permute-start | bytes 786440 | tf_op jit(solution)/shard_map/ppermute | solution.py:41
  11.3 11.5 %copy-start.9 = (f32[256,8]{0,1:T(8,128)S(1)}, f32[256,8]{0,1:T(8,128)}, u32[]{:S(2)}) copy-start(f32[256,8]{0,1:T(8,128)} %param.20) | copy-start | bytes 24580
  11.3 11.5 %copy-start.10 = (f32[8]{0:T(128)S(1)}, f32[8]{0:T(128)}, u32[]{:S(2)}) copy-start(f32[8]{0:T(128)} %param.21) | copy-start | bytes 100
  11.3 11.5 %copy-start.11 = (f32[8]{0:T(128)S(1)}, f32[8]{0:T(128)}, u32[]{:S(2)}) copy-start(f32[8]{0:T(128)} %param.22) | copy-start | bytes 100
  11.3 12.6 %collective-permute-start.6 = (bf16[16,1024]{1,0:T(8,128)(2,1)S(1)}, bf16[16,1024]{1,0:T(8,128)(2,1)S(1)}, u32[]{:S(2)}, u32[]{:S(2)}) collective-permute-start(bf16[16,1024]{1,0:T(8,128)(2,1)S(1)} %pad_maximum_fusion.1), channel_id=1, source_target_pairs={{0,2},{1,3},{2,0},{3,1},{4,6},{5,7},{6,4},{7,5},{8,10},{9,11},{10,... | collective-permute-start | bytes 98312 | tf_op jit(solution)/shard_map/ppermute | solution.py:41
  13.4 16.9 %collective-permute-start.3 = (bf16[128,1024]{1,0:T(8,128)(2,1)S(1)}, bf16[128,1024]{1,0:T(8,128)(2,1)S(1)}, u32[]{:S(2)}, u32[]{:S(2)}) collective-permute-start(bf16[128,1024]{1,0:T(8,128)(2,1)S(1)} %collective-permute-done.2.refs_1_), channel_id=1, source_target_pairs={{0,2},{1,3},{2,0},{3,1},{4,6},{5,7},{6,4},{7,5},{8,10},{9,11},{10,... | collective-permute-start | bytes 786440 | tf_op jit(solution)/shard_map/ppermute | solution.py:41
  13.5 16.8 %collective-permute-start.1 = (bf16[128,1024]{1,0:T(8,128)(2,1)S(1)}, bf16[128,1024]{1,0:T(8,128)(2,1)S(1)}, u32[]{:S(2)}, u32[]{:S(2)}) collective-permute-start(bf16[128,1024]{1,0:T(8,128)(2,1)S(1)} %collective-permute-done.refs_2_), channel_id=1, source_target_pairs={{0,1},{1,0},{2,3},{3,2},{4,5},{5,4},{6,7},{7,6},{8,9},{9,8},{10,11... | collective-permute-start | bytes 786440 | tf_op jit(solution)/shard_map/ppermute | solution.py:41
  15.4 2.2 %copy-start = (bf16[4096,512]{1,0:T(8,128)(2,1)S(1)}, bf16[4096,512]{1,0:T(8,128)(2,1)}, u32[]{:S(2)}) copy-start(bf16[4096,512]{1,0:T(8,128)(2,1)} %w_x.1) | copy-start | bytes 12582916
  17.6 2.2 %copy-start.1 = (bf16[4096,512]{1,0:T(8,128)(2,1)S(1)}, bf16[4096,512]{1,0:T(8,128)(2,1)}, u32[]{:S(2)}) copy-start(bf16[4096,512]{1,0:T(8,128)(2,1)} %w_z.1) | copy-start | bytes 12582916
  19.8 1.2 %copy-start.3 = (bf16[4096,128]{1,0:T(8,128)(2,1)S(1)}, bf16[4096,128]{1,0:T(8,128)(2,1)}, u32[]{:S(2)}) copy-start(bf16[4096,128]{1,0:T(8,128)(2,1)} %w_bc.1) | copy-start | bytes 3145732
  24.0 5.5 %collective-permute-start.7 = (bf16[32,1024]{1,0:T(8,128)(2,1)S(1)}, bf16[32,1024]{1,0:T(8,128)(2,1)S(1)}, u32[]{:S(2)}, u32[]{:S(2)}) collective-permute-start(bf16[32,1024]{1,0:T(8,128)(2,1)S(1)} %pad_maximum_fusion), channel_id=1, source_target_pairs={{0,4},{4,8},{8,12},{12,16},{16,20},{20,24},{24,28},{28,0},{1,5},{5... | collective-permute-start | bytes 196616 | tf_op jit(solution)/shard_map/ppermute | solution.py:37
  25.6 4.7 %copy-start.5 = (f32[4,128]{1,0:T(4,128)S(1)}, f32[4,128]{1,0:T(4,128)}, u32[]{:S(2)}) copy-start(f32[4,128]{1,0:T(4,128)} %refs_5_.2) | copy-start | bytes 6148
  25.6 4.7 %copy-start.8 = (f32[128]{0:T(128)S(1)}, f32[128]{0:T(128)}, u32[]{:S(2)}) copy-start(f32[128]{0:T(128)} %param.19) | copy-start | bytes 1540
  30.3 0.7 %copy-start.4 = (f32[4,512]{1,0:T(4,128)S(1)}, f32[4,512]{1,0:T(4,128)}, u32[]{:S(2)}) copy-start(f32[4,512]{1,0:T(4,128)} %refs_5_.3) | copy-start | bytes 24580
  30.3 0.7 %copy-start.6 = (f32[512]{0:T(512)S(1)}, f32[512]{0:T(512)}, u32[]{:S(2)}) copy-start(f32[512]{0:T(512)} %param.18) | copy-start | bytes 6148
  30.7 4.3 %collective-permute-start.8 = (bf16[256,128]{1,0:T(8,128)(2,1)S(1)}, bf16[256,128]{1,0:T(8,128)(2,1)S(1)}, u32[]{:S(2)}, u32[]{:S(2)}) collective-permute-start(bf16[256,128]{1,0:T(8,128)(2,1)S(1)} %last_bc.1.own_bc), channel_id=1, source_target_pairs={{0,1},{1,0},{2,3},{3,2},{4,5},{5,4},{6,7},{7,6},{8,9},{9,8},{10,11... | collective-permute-start | bytes 196616 | tf_op jit(solution)/shard_map/ppermute | solution.py:41
  35.3 1.3 %collective-permute-start.9 = (bf16[144,256]{1,0:T(8,128)(2,1)S(1)}, bf16[144,256]{1,0:T(8,128)(2,1)S(1)}, u32[]{:S(2)}, u32[]{:S(2)}) collective-permute-start(bf16[144,256]{1,0:T(8,128)(2,1)S(1)} %get-tuple-element.27), channel_id=1, source_target_pairs={{0,4},{4,0},{8,12},{12,8},{16,20},{20,16},{24,28},{28,24},{1,5},{5... | collective-permute-start | bytes 221192 | tf_op jit(solution)/shard_map/ppermute | solution.py:41
  36.7 7.1 %collective-permute-start.10 = (bf16[144,256]{1,0:T(8,128)(2,1)S(1)}, bf16[144,256]{1,0:T(8,128)(2,1)S(1)}, u32[]{:S(2)}, u32[]{:S(2)}) collective-permute-start(bf16[144,256]{1,0:T(8,128)(2,1)S(1)} %chip_state.1._.refs_4_), channel_id=1, source_target_pairs={{0,8},{4,12},{8,16},{12,20},{16,24},{20,28},{24,0},{28,4},{1,9},{5... | collective-permute-start | bytes 221192 | tf_op jit(solution)/shard_map/ppermute | solution.py:37
  36.7 9.2 %collective-permute-start.11 = (bf16[144,256]{1,0:T(8,128)(2,1)S(1)}, bf16[144,256]{1,0:T(8,128)(2,1)S(1)}, u32[]{:S(2)}, u32[]{:S(2)}) collective-permute-start(bf16[144,256]{1,0:T(8,128)(2,1)S(1)} %chip_state.1._.refs_4_), channel_id=1, source_target_pairs={{0,16},{4,20},{8,24},{12,28},{16,0},{20,4},{24,8},{28,12},{1,17},{... | collective-permute-start | bytes 221192 | tf_op jit(solution)/shard_map/ppermute | solution.py:37
  39.1 6.8 %collective-permute-start.12 = (bf16[144,256]{1,0:T(8,128)(2,1)S(1)}, bf16[144,256]{1,0:T(8,128)(2,1)S(1)}, u32[]{:S(2)}, u32[]{:S(2)}) collective-permute-start(bf16[144,256]{1,0:T(8,128)(2,1)S(1)} %chip_state.1._.refs_4_), channel_id=1, source_target_pairs={{0,24},{4,28},{8,0},{12,4},{16,8},{20,12},{24,16},{28,20},{1,25},{... | collective-permute-start | bytes 221192 | tf_op jit(solution)/shard_map/ppermute | solution.py:37
  41.2 10.3 %copy-start.7 = (f32[512]{0:T(512)S(1)}, f32[512]{0:T(512)}, u32[]{:S(2)}) copy-start(f32[512]{0:T(512)} %param.23) | copy-start | bytes 6148
  46.0 1.3 %collective-permute-start.13 = (bf16[128,256]{1,0:T(8,128)(2,1)S(1)}, bf16[128,256]{1,0:T(8,128)(2,1)S(1)}, u32[]{:S(2)}, u32[]{:S(2)}) collective-permute-start(bf16[128,256]{1,0:T(8,128)(2,1)S(1)} %get-tuple-element.31), channel_id=1, source_target_pairs={{0,4},{4,0},{8,12},{12,8},{16,20},{20,16},{24,28},{28,24},{1,5},{5... | collective-permute-start | bytes 196616 | tf_op jit(solution)/shard_map/ppermute | solution.py:41
  47.8 3.7 %collective-permute-start.14 = (f32[8,256]{1,0:T(8,128)S(1)}, f32[8,256]{1,0:T(8,128)S(1)}, u32[]{:S(2)}, u32[]{:S(2)}) collective-permute-start(f32[8,256]{1,0:T(8,128)S(1)} %get-tuple-element.34.square), channel_id=1, source_target_pairs={{0,1},{1,0},{2,3},{3,2},{4,5},{5,4},{6,7},{7,6},{8,9},{9,8},{10,11... | collective-permute-start | bytes 24584 | tf_op jit(solution)/shard_map/ppermute | solution.py:41

commit v3 on v2

--- a/solution.py
+++ b/solution.py
@@ -9,7 +9,8 @@
 
 KERNEL = 4
 RIM = 8
-PAD = 8
+ROWS = 8
+PAD = 4
 F32, BF16 = jnp.float32, jnp.bfloat16
 EXACT = lax.Precision.HIGHEST
 VMEM = pl.BlockSpec(memory_space=pltpu.VMEM)
@@ -19,6 +20,10 @@
 def run(body, outs, *operands, scratch=(), flops=1000000, hbm=0, limit=4 << 20):
     single = not isinstance(outs, list)
     shapes = [jax.ShapeDtypeStruct(*o) for o in ([outs] if single else outs)]
+    operands = [
+        pltpu.with_memory_space_constraint(o, pltpu.HBM) if i < hbm else o
+        for i, o in enumerate(operands)
+    ]
     results = pl.pallas_call(
         body,
         out_shape=shapes,
@@ -288,7 +293,7 @@
         for start in range(0, half, 128):
             part = gated[:, start : start + 128]
             squares = part * part if squares is None else squares + part * part
-    ones = jnp.ones((PAD, squares.shape[1]), F32)
+    ones = jnp.ones((ROWS, squares.shape[1]), F32)
     square_out[...] = lax.dot_general(
         ones, squares, (((1,), (1,)), ((), ())), precision=EXACT, preferred_element_type=F32
     )
@@ -298,7 +303,7 @@
     width = gated.shape[1]
     mean = (square[...] + other_square[...]) / (2 * width)
     factor = lax.rsqrt(mean + 1e-05)
-    share = jnp.full((PAD, 128), 1.0 / PAD, F32)
+    share = jnp.full((ROWS, 128), 1.0 / ROWS, F32)
     column = lax.dot_general(
         factor, share, (((0,), (0,)), ((), ())), precision=EXACT, preferred_element_type=F32
     )
@@ -307,11 +312,16 @@
         out[:, columns] = (gated[:, columns] * column * gain[:, columns]).astype(BF16)
 
 
-def gather_pieces(top, bottom, axis):
+def last_rows(bottom, near_bottom, _, out):
+    end = bottom.shape[0] - RIM
+    out[pl.ds(0, RIM), :] = bottom[pl.ds(end, RIM), :]
+    out[pl.ds(RIM, RIM), :] = near_bottom[pl.ds(end, RIM), :]
+
+
+def gather_pieces(top, bottom, sums, axis):
     size = lax.axis_size(axis)
-    end = bottom.shape[0] - RIM
     near_bottom = partner(bottom, axis, 1)
-    rim = jnp.concatenate([bottom[end:], near_bottom[end:]], axis=0)
+    rim = run(last_rows, ((2 * RIM, bottom.shape[1]), BF16), bottom, near_bottom, sums)
     if size == 2:
         return {}, {1: [partner(top, axis, 1), near_bottom]}, rim
     far_top = partner(top, axis, 2)
@@ -347,9 +357,6 @@
         run(functools.partial(fetched_rows, start), ((half, depth), BF16), tokens, scratch=arrival, hbm=1)
         for start in (half, 0)
     ]
-    early, last, rim = gather_pieces(top, bottom, "tp")
-    rim = hop(rim, "ctx", 1)
-
     def flops(*sizes):
         total = 2
         for s in sizes:
@@ -366,13 +373,15 @@
         flops=flops(rows, depth, everything),
         hbm=3,
     )
+    early, last, rim = gather_pieces(top, bottom, sums, "tp")
+    rim = hop(rim, "ctx", 1)
     segment, grown, end_weight, whole, skip_wide = run(
         decays,
         [
             ((heads, rows, rows), BF16),
             ((rows, width), F32),
             ((rows, width), F32),
-            ((PAD, width), F32),
+            ((ROWS, width), F32),
             ((1, width), F32),
         ],
         decay_logarithm.T, head_step.reshape(1, -1), skip.reshape(1, -1),
@@ -439,7 +448,7 @@
     take = partner(give, "ctx", 1)
     gated, square = run(
         gated_output,
-        [((rows, width), F32), ((PAD, rows), F32)],
+        [((rows, width), F32), ((ROWS, rows), F32)],
         own_bc, other_bc, keep, take, within, grown, gate,
         flops=flops(rows, n, width),
     )

time: 52.9 us -> 49.1 us (0.928)
  local copies, waits for them, and re-layouts: 6.82 us -> 0.26 us
  Pallas kernels: 9.86 us -> 13.8 us
  starting transfers between devices: 13.7 us -> 12.5 us
    unnamed x24 -> x16, local copies, waits for them, and re-layouts: 6.81 us -> 0.26 us
    pallas_call x15 -> x16, Pallas kernels: 9.86 us -> 13.8 us  [run(): pl.pallas_call(body, out_shape=shapes, in_specs=[HBM] * hbm + [VMEM] * (l...]
    ppermute x11, starting transfers between devices: 9.81 us -> 8.6 us  [partner(): lax.ppermute(value, axis, [(i, i ^ mask) for i in range(lax.axis_size(axi...]
  transfers between devices with their start and end apart: 15 -> 15, of which waited for: 8 -> 10; matrix products, arithmetic and copies ran while one was open for 0% -> 0% of each run, Pallas kernels for 14% -> 22%
where the time goes in v3:
time: 49.1 us; the launch traced here: 48.9 us
  waiting for transfers between devices  22.1 us (45%)
  Pallas kernels  13.8 us (28%)
  starting transfers between devices  12.5 us (25%)
    ppermute x11, waiting for transfers between devices, partner(): lax.ppermute(value, axis, [(i, i ^ mask) for i in range(lax.axis_size(axi...  14.4 us
    pallas_call x16, Pallas kernels, run(): pl.pallas_call(body, out_shape=shapes, in_specs=[HBM] * hbm + [VMEM] * (l...  13.8 us
    ppermute x11, starting transfers between devices, partner(): lax.ppermute(value, axis, [(i, i ^ mask) for i in range(lax.axis_size(axi...  8.6 us
    ppermute x4, waiting for transfers between devices, hop(): lax.ppermute(value, axis, [(i, (i + distance) % size) for i in range(size)])  7.72 us
    ppermute x4, starting transfers between devices, hop(): lax.ppermute(value, axis, [(i, (i + distance) % size) for i in range(size)])  3.87 us
  transfers between devices with their start and end apart: 15, of which 10 were waited for; matrix products, arithmetic and copies ran while one was open for 0% of the time, Pallas kernels for 22%

profile of v3, /device:TPU:0, one launch (start us, length us, event | category | flops | bytes accessed | tf_op | source)
XLA Modules:
  0.0 48.9 jit_solution(664980493086817258)
XLA Ops:
  0.0 1.0 %fetched_rows.3.bottom = bf16[128,1024]{1,0:T(8,128)(2,1)S(1)} custom-call(bf16[256,1024]{1,0:T(8,128)(2,1)} %source.3), custom_call_target="tpu_custom_call" | custom-call | flops 1000000 | bytes 2500 | tf_op jit(solution)/shard_map/fetched_rows/pallas_call | solution.py:27
  1.0 3.0 %collective-permute-start.2 = (bf16[128,1024]{1,0:T(8,128)(2,1)S(1)}, bf16[128,1024]{1,0:T(8,128)(2,1)S(1)}, u32[]{:S(2)}, u32[]{:S(2)}) collective-permute-start(bf16[128,1024]{1,0:T(8,128)(2,1)S(1)} %fetched_rows.3.bottom), channel_id=1, source_target_pairs={{0,1},{1,0},{2,3},{3,2},{4,5},{5,4},{6,7},{7,6},{8,9},{9,8},{10,11... | collective-permute-start | bytes 786440 | tf_op jit(solution)/shard_map/ppermute | solution.py:46
  4.0 1.0 %fetched_rows.2.top = bf16[128,1024]{1,0:T(8,128)(2,1)S(1)} custom-call(bf16[256,1024]{1,0:T(8,128)(2,1)} %source.3), custom_call_target="tpu_custom_call" | custom-call | flops 1000000 | bytes 2500 | tf_op jit(solution)/shard_map/fetched_rows/pallas_call | solution.py:27
  5.0 0.0 copy-start.5
  5.0 0.0 copy-start.6
  5.0 0.0 copy-start.7
  5.0 1.6 %collective-permute-start = (bf16[128,1024]{1,0:T(8,128)(2,1)S(1)}, bf16[128,1024]{1,0:T(8,128)(2,1)S(1)}, u32[]{:S(2)}, u32[]{:S(2)}) collective-permute-start(bf16[128,1024]{1,0:T(8,128)(2,1)S(1)} %fetched_rows.2.top), channel_id=1, source_target_pairs={{0,2},{1,3},{2,0},{3,1},{4,6},{5,7},{6,4},{7,5},{8,10},{9,11},{10,... | collective-permute-start | bytes 786440 | tf_op jit(solution)/shard_map/ppermute | solution.py:46
  6.6 0.5 %collective-permute-start.5 = (bf16[128,1024]{1,0:T(8,128)(2,1)S(1)}, bf16[128,1024]{1,0:T(8,128)(2,1)S(1)}, u32[]{:S(2)}, u32[]{:S(2)}) collective-permute-start(bf16[128,1024]{1,0:T(8,128)(2,1)S(1)} %fetched_rows.3.bottom), channel_id=1, source_target_pairs={{0,2},{1,3},{2,0},{3,1},{4,6},{5,7},{6,4},{7,5},{8,10},{9,11},{10,... | collective-permute-start | bytes 786440 | tf_op jit(solution)/shard_map/ppermute | solution.py:46
  7.1 0.1 collective-permute-start.4
  7.2 3.8 %own_product.1 = (f32[256,1152]{1,0:T(8,128)S(1)}, bf16[4,1024,1152]{2,1,0:T(8,128)(2,1)S(1)}) custom-call(bf16[4096,128]{1,0:T(8,128)(2,1)} %w_bc.1, bf16[4096,512]{1,0:T(8,128)(2,1)} %w_x.1, bf16[4096,512]{1,0:T(8,128)(2,1)} %w_z.1, bf16[128,1024]{1,0:T(8,128)(2,1)S(1)} %fetched_rows.2.top, bf16[128,1024]{1,0:T(8,128)(2,1)S(1)} %fetched_rows.3.bottom), custom_call_target="tpu_custom_call" | custom-call | flops 603979776 | bytes 1509949 | tf_op jit(solution)/shard_map/own_product/pallas_call | solution.py:27
  11.0 0.1 collective-permute-done.2.refs_1_.near_bottom
  11.2 2.0 %collective-permute-start.6 = (bf16[16,1024]{1,0:T(8,128)(2,1)S(1)}, bf16[16,1024]{1,0:T(8,128)(2,1)S(1)}, u32[]{:S(2)}, u32[]{:S(2)}) collective-permute-start(bf16[16,1024]{1,0:T(8,128)(2,1)S(1)} %last_rows.1), channel_id=1, source_target_pairs={{0,2},{1,3},{2,0},{3,1},{4,6},{5,7},{6,4},{7,5},{8,10},{9,11},{10,... | collective-permute-start | bytes 98312 | tf_op jit(solution)/shard_map/ppermute | solution.py:46
  13.2 0.0 collective-permute-start.3
  13.2 1.0 %collective-permute-done.refs_2_ = bf16[128,1024]{1,0:T(8,128)(2,1)S(1)} collective-permute-done((bf16[128,1024]{1,0:T(8,128)(2,1)S(1)}, bf16[128,1024]{1,0:T(8,128)(2,1)S(1)}, u32[]{:S(2)}, u32[]{:S(2)}) %collective-permute-start) | collective-permute-done | bytes 262176 | tf_op jit(solution)/shard_map/ppermute | solution.py:46
  14.2 1.0 %collective-permute-start.1 = (bf16[128,1024]{1,0:T(8,128)(2,1)S(1)}, bf16[128,1024]{1,0:T(8,128)(2,1)S(1)}, u32[]{:S(2)}, u32[]{:S(2)}) collective-permute-start(bf16[128,1024]{1,0:T(8,128)(2,1)S(1)} %collective-permute-done.refs_2_), channel_id=1, source_target_pairs={{0,1},{1,0},{2,3},{3,2},{4,5},{5,4},{6,7},{7,6},{8,9},{9,8},{10,11... | collective-permute-start | bytes 786440 | tf_op jit(solution)/shard_map/ppermute | solution.py:46
  15.2 0.0 copy-done.5
  15.2 0.0 copy-done.6
  15.2 0.0 copy-done.7
  15.2 1.1 %decays.1 = (bf16[8,256,256]{2,1,0:T(8,128)(2,1)S(1)}, f32[256,512]{1,0:T(8,128)S(1)}, f32[256,512]{1,0:T(8,128)S(1)}, f32[8,512]{1,0:T(8,128)S(1)}, f32[1,512]{1,0:T(1,128)S(1)}) custom-call(f32[8,256]{1,0:T(8,128)S(1)} %bitcast.9, f32[1,8]{1,0:T(1,128)S(1)} %bitcast.10, f32[1,8]{1,0:T(1,128)S(1)} %bitcast.11), custom_call_target="tpu_custom_call" | custom-call | flops 67108864 | bytes 167772 | tf_op jit(solution)/shard_map/decays/pallas_call | solution.py:27
  16.4 4.2 %collective-permute-done.6 = bf16[16,1024]{1,0:T(8,128)(2,1)S(1)} collective-permute-done((bf16[16,1024]{1,0:T(8,128)(2,1)S(1)}, bf16[16,1024]{1,0:T(8,128)(2,1)S(1)}, u32[]{:S(2)}, u32[]{:S(2)}) %collective-permute-start.6) | collective-permute-done | bytes 32800 | tf_op jit(solution)/shard_map/ppermute | solution.py:46
  20.6 0.0 collective-permute-start.7
  20.6 0.0 collective-permute-done.5.refs_3_
  20.6 0.0 collective-permute-done.4.refs_0_
  20.6 1.5 %middle_product.1.refs_3_ = f32[256,1152]{1,0:T(8,128)S(1)} custom-call(bf16[128,1024]{1,0:T(8,128)(2,1)S(1)} %collective-permute-done.4.refs_0_, bf16[128,1024]{1,0:T(8,128)(2,1)S(1)} %collective-permute-done.2.refs_1_.near_bottom, bf16[128,1024]{1,0:T(8,128)(2,1)S(1)} %collective-permute-done.refs_2_, ...), custom_call_target="tpu_custom_call" | custom-call | flops 1207959552 | bytes 3019898 | tf_op jit(solution)/shard_map/middle_product/pallas_call | solution.py:27
  22.1 0.0 copy-start.1
  22.2 0.0 copy-start.4
  22.2 3.9 %collective-permute-done.7.rim = bf16[32,1024]{1,0:T(8,128)(2,1)S(1)} collective-permute-done((bf16[32,1024]{1,0:T(8,128)(2,1)S(1)}, bf16[32,1024]{1,0:T(8,128)(2,1)S(1)}, u32[]{:S(2)}, u32[]{:S(2)}) %collective-permute-start.7) | collective-permute-done | bytes 65568 | tf_op jit(solution)/shard_map/ppermute | solution.py:42
  26.1 0.8 %rim_product.1.refs_4_ = f32[8,640]{1,0:T(8,128)S(1)} custom-call(bf16[32,1024]{1,0:T(8,128)(2,1)S(1)} %collective-permute-done.7.rim, bf16[4,1024,1152]{2,1,0:T(8,128)(2,1)S(1)} %get-tuple-element.20.refs_4_.weights.refs_2_), custom_call_target="tpu_custom_call" | custom-call | flops 268435456 | bytes 671088 | tf_op jit(solution)/shard_map/rim_product/pallas_call | solution.py:27
  26.8 0.0 collective-permute-done.3.refs_1_
  26.8 0.0 collective-permute-done.1.refs_0_
  26.9 0.0 copy-done.1
  26.9 0.0 copy-done.4
  26.9 0.0 copy-start
  26.9 0.0 copy-start.2
  26.9 0.4 last_bc.1.own_bc
  27.3 0.1 collective-permute-start.8
  27.4 0.2 copy-done
  27.6 0.0 copy-done.2
  27.6 1.1 %last_x.1 = (bf16[256,512]{1,0:T(8,128)(2,1)S(1)}, bf16[256,512]{1,0:T(8,128)(2,1)S(1)}) custom-call(bf16[128,1024]{1,0:T(8,128)(2,1)S(1)} %collective-permute-done.1.refs_0_, bf16[128,1024]{1,0:T(8,128)(2,1)S(1)} %collective-permute-done.3.refs_1_, bf16[4,1024,1152]{2,1,0:T(8,128)(2,1)S(1)} %get-tuple-element.20.refs_4_.weights.refs_2_, ...), custom_call_target="tpu_custom_call" | custom-call | flops 268435456 | bytes 671088 | tf_op jit(solution)/shard_map/last_x/pallas_call | solution.py:27
  28.7 2.9 %collective-permute-done.8.other_bc = bf16[256,128]{1,0:T(8,128)(2,1)S(1)} collective-permute-done((bf16[256,128]{1,0:T(8,128)(2,1)S(1)}, bf16[256,128]{1,0:T(8,128)(2,1)S(1)}, u32[]{:S(2)}, u32[]{:S(2)}) %collective-permute-start.8) | collective-permute-done | bytes 65568 | tf_op jit(solution)/shard_map/ppermute | solution.py:46
  31.6 0.2 section_state.1
  31.8 0.1 collective-permute-start.9
  31.9 1.2 %collective-permute-done.9.received = bf16[136,256]{1,0:T(8,128)(2,1)S(1)} collective-permute-done((bf16[136,256]{1,0:T(8,128)(2,1)S(1)}, bf16[136,256]{1,0:T(8,128)(2,1)S(1)}, u32[]{:S(2)}, u32[]{:S(2)}) %collective-permute-start.9) | collective-permute-done | bytes 69664 | tf_op jit(solution)/shard_map/ppermute | solution.py:46
  33.2 0.1 collective-permute-start.10
  33.3 2.4 %collective-permute-start.11 = (bf16[136,256]{1,0:T(8,128)(2,1)S(1)}, bf16[136,256]{1,0:T(8,128)(2,1)S(1)}, u32[]{:S(2)}, u32[]{:S(2)}) collective-permute-start(bf16[136,256]{1,0:T(8,128)(2,1)S(1)} %chip_state.1._.refs_4_), channel_id=1, source_target_pairs={{0,16},{4,20},{8,24},{12,28},{16,0},{20,4},{24,8},{28,12},{1,17},{... | collective-permute-start | bytes 208904 | tf_op jit(solution)/shard_map/ppermute | solution.py:42
  35.6 1.5 %collective-permute-start.12 = (bf16[136,256]{1,0:T(8,128)(2,1)S(1)}, bf16[136,256]{1,0:T(8,128)(2,1)S(1)}, u32[]{:S(2)}, u32[]{:S(2)}) collective-permute-start(bf16[136,256]{1,0:T(8,128)(2,1)S(1)} %chip_state.1._.refs_4_), channel_id=1, source_target_pairs={{0,24},{4,28},{8,0},{12,4},{16,8},{20,12},{24,16},{28,20},{1,25},{... | collective-permute-start | bytes 208904 | tf_op jit(solution)/shard_map/ppermute | solution.py:42
  37.1 0.7 %within_section.1.refs_3_.within = f32[256,512]{1,0:T(8,128)S(1)} custom-call(bf16[256,128]{1,0:T(8,128)(2,1)S(1)} %last_bc.1.own_bc, bf16[256,128]{1,0:T(8,128)(2,1)S(1)} %collective-permute-done.8.other_bc, bf16[256,512]{1,0:T(8,128)(2,1)S(1)} %get-tuple-element.28.x, bf16[8,256,256]{2,1,0:T(8,128)(2,1)S(1)} %get-tuple-element.29.segment, ...), custom_call_target="tpu_custom_call" | custom-call | flops 201326592 | bytes 503316 | tf_op jit(solution)/shard_map/within_section/pallas_call | solution.py:27
  37.8 0.0 copy-start.3
  37.8 0.5 %last_z.1.refs_4_.gate = f32[256,512]{1,0:T(8,128)S(1)} custom-call(bf16[128,1024]{1,0:T(8,128)(2,1)S(1)} %collective-permute-done.1.refs_0_, bf16[128,1024]{1,0:T(8,128)(2,1)S(1)} %collective-permute-done.3.refs_1_, bf16[4,1024,1152]{2,1,0:T(8,128)(2,1)S(1)} %get-tuple-element.20.refs_4_.weights.refs_2_, f32[256,1152]{1,0:T(8,128)S(1)} %middle_product.1.refs_3_, ...), custom_call_target="tpu_custom_call" | custom-call | flops 268435456 | bytes 671088 | tf_op jit(solution)/shard_map/last_z/pallas_call | solution.py:27
  38.3 1.8 %collective-permute-done.10.refs_0_ = bf16[136,256]{1,0:T(8,128)(2,1)S(1)} collective-permute-done((bf16[136,256]{1,0:T(8,128)(2,1)S(1)}, bf16[136,256]{1,0:T(8,128)(2,1)S(1)}, u32[]{:S(2)}, u32[]{:S(2)}) %collective-permute-start.10) | collective-permute-done | bytes 69664 | tf_op jit(solution)/shard_map/ppermute | solution.py:42
  40.2 2.0 %collective-permute-done.11.refs_1_ = bf16[136,256]{1,0:T(8,128)(2,1)S(1)} collective-permute-done((bf16[136,256]{1,0:T(8,128)(2,1)S(1)}, bf16[136,256]{1,0:T(8,128)(2,1)S(1)}, u32[]{:S(2)}, u32[]{:S(2)}) %collective-permute-start.11) | collective-permute-done | bytes 69664 | tf_op jit(solution)/shard_map/ppermute | solution.py:42
  42.2 0.0 collective-permute-done.12.refs_2_
  42.2 0.1 entering_state.1
  42.3 0.1 collective-permute-start.13
  42.4 1.2 %collective-permute-done.13.take = bf16[128,256]{1,0:T(8,128)(2,1)S(1)} collective-permute-done((bf16[128,256]{1,0:T(8,128)(2,1)S(1)}, bf16[128,256]{1,0:T(8,128)(2,1)S(1)}, u32[]{:S(2)}, u32[]{:S(2)}) %collective-permute-start.13) | collective-permute-done | bytes 65568 | tf_op jit(solution)/shard_map/ppermute | solution.py:46
  43.6 0.5 %gated_output.1 = (f32[256,512]{1,0:T(8,128)S(1)}, f32[8,256]{1,0:T(8,128)S(1)}) custom-call(bf16[256,128]{1,0:T(8,128)(2,1)S(1)} %last_bc.1.own_bc, bf16[256,128]{1,0:T(8,128)(2,1)S(1)} %collective-permute-done.8.other_bc, bf16[128,256]{1,0:T(8,128)(2,1)S(1)} %get-tuple-element.30.keep, bf16[128,256]{1,0:T(8,128)(2,1)S(1)} %collective-permute-done.13.take, ...), custom_call_target="tpu_custom_call" | custom-call | flops 33554432 | bytes 83886 | tf_op jit(solution)/shard_map/gated_output/pallas_call | solution.py:27
  44.1 0.1 collective-permute-start.14
  44.2 3.6 %collective-permute-done.14.other_square = f32[8,256]{1,0:T(8,128)S(1)} collective-permute-done((f32[8,256]{1,0:T(8,128)S(1)}, f32[8,256]{1,0:T(8,128)S(1)}, u32[]{:S(2)}, u32[]{:S(2)}) %collective-permute-start.14) | collective-permute-done | bytes 8224 | tf_op jit(solution)/shard_map/ppermute | solution.py:46
  47.8 0.0 copy-done.3
  47.8 1.1 %normed_output.1 = bf16[256,512]{1,0:T(8,128)(2,1)} custom-call(f32[256,512]{1,0:T(8,128)S(1)} %get-tuple-element.33.gated, f32[8,256]{1,0:T(8,128)S(1)} %get-tuple-element.34.square, f32[8,256]{1,0:T(8,128)S(1)} %collective-permute-done.14.other_square, f32[1,512]{1,0:T(1,128)S(1)} %bitcast.7), custom_call_target="tpu_custom_call" | custom-call | flops 1000000 | bytes 2500 | tf_op jit(solution)/shard_map/normed_output/pallas_call | solution.py:27
  (3 shorter events, 0.0 us)
Async XLA Ops:
  1.0 10.2 %collective-permute-start.2 = (bf16[128,1024]{1,0:T(8,128)(2,1)S(1)}, bf16[128,1024]{1,0:T(8,128)(2,1)S(1)}, u32[]{:S(2)}, u32[]{:S(2)}) collective-permute-start(bf16[128,1024]{1,0:T(8,128)(2,1)S(1)} %fetched_rows.3.bottom), channel_id=1, source_target_pairs={{0,1},{1,0},{2,3},{3,2},{4,5},{5,4},{6,7},{7,6},{8,9},{9,8},{10,11... | collective-permute-start | bytes 786440 | tf_op jit(solution)/shard_map/ppermute | solution.py:46
  5.0 10.2 %copy-start.5 = (f32[256,8]{0,1:T(8,128)S(1)}, f32[256,8]{0,1:T(8,128)}, u32[]{:S(2)}) copy-start(f32[256,8]{0,1:T(8,128)} %param.20) | copy-start | bytes 24580
  5.0 10.2 %copy-start.6 = (f32[8]{0:T(128)S(1)}, f32[8]{0:T(128)}, u32[]{:S(2)}) copy-start(f32[8]{0:T(128)} %param.21) | copy-start | bytes 100
  5.0 10.2 %copy-start.7 = (f32[8]{0:T(128)S(1)}, f32[8]{0:T(128)}, u32[]{:S(2)}) copy-start(f32[8]{0:T(128)} %param.22) | copy-start | bytes 100
  5.0 9.2 %collective-permute-start = (bf16[128,1024]{1,0:T(8,128)(2,1)S(1)}, bf16[128,1024]{1,0:T(8,128)(2,1)S(1)}, u32[]{:S(2)}, u32[]{:S(2)}) collective-permute-start(bf16[128,1024]{1,0:T(8,128)(2,1)S(1)} %fetched_rows.2.top), channel_id=1, source_target_pairs={{0,2},{1,3},{2,0},{3,1},{4,6},{5,7},{6,4},{7,5},{8,10},{9,11},{10,... | collective-permute-start | bytes 786440 | tf_op jit(solution)/shard_map/ppermute | solution.py:46
  6.6 14.0 %collective-permute-start.5 = (bf16[128,1024]{1,0:T(8,128)(2,1)S(1)}, bf16[128,1024]{1,0:T(8,128)(2,1)S(1)}, u32[]{:S(2)}, u32[]{:S(2)}) collective-permute-start(bf16[128,1024]{1,0:T(8,128)(2,1)S(1)} %fetched_rows.3.bottom), channel_id=1, source_target_pairs={{0,2},{1,3},{2,0},{3,1},{4,6},{5,7},{6,4},{7,5},{8,10},{9,11},{10,... | collective-permute-start | bytes 786440 | tf_op jit(solution)/shard_map/ppermute | solution.py:46
  7.1 13.5 %collective-permute-start.4 = (bf16[128,1024]{1,0:T(8,128)(2,1)S(1)}, bf16[128,1024]{1,0:T(8,128)(2,1)S(1)}, u32[]{:S(2)}, u32[]{:S(2)}) collective-permute-start(bf16[128,1024]{1,0:T(8,128)(2,1)S(1)} %fetched_rows.2.top), channel_id=1, source_target_pairs={{0,1},{1,0},{2,3},{3,2},{4,5},{5,4},{6,7},{7,6},{8,9},{9,8},{10,11... | collective-permute-start | bytes 786440 | tf_op jit(solution)/shard_map/ppermute | solution.py:46
  11.2 9.4 %collective-permute-start.6 = (bf16[16,1024]{1,0:T(8,128)(2,1)S(1)}, bf16[16,1024]{1,0:T(8,128)(2,1)S(1)}, u32[]{:S(2)}, u32[]{:S(2)}) collective-permute-start(bf16[16,1024]{1,0:T(8,128)(2,1)S(1)} %last_rows.1), channel_id=1, source_target_pairs={{0,2},{1,3},{2,0},{3,1},{4,6},{5,7},{6,4},{7,5},{8,10},{9,11},{10,... | collective-permute-start | bytes 98312 | tf_op jit(solution)/shard_map/ppermute | solution.py:46
  13.2 13.6 %collective-permute-start.3 = (bf16[128,1024]{1,0:T(8,128)(2,1)S(1)}, bf16[128,1024]{1,0:T(8,128)(2,1)S(1)}, u32[]{:S(2)}, u32[]{:S(2)}) collective-permute-start(bf16[128,1024]{1,0:T(8,128)(2,1)S(1)} %collective-permute-done.2.refs_1_.near_bottom), channel_id=1, source_target_pairs={{0,2},{1,3},{2,0},{3,1},{4,6},{5,7},{6,4},{7,5},{8,10},{9,11},{10,... | collective-permute-start | bytes 786440 | tf_op jit(solution)/shard_map/ppermute | solution.py:46
  14.2 12.6 %collective-permute-start.1 = (bf16[128,1024]{1,0:T(8,128)(2,1)S(1)}, bf16[128,1024]{1,0:T(8,128)(2,1)S(1)}, u32[]{:S(2)}, u32[]{:S(2)}) collective-permute-start(bf16[128,1024]{1,0:T(8,128)(2,1)S(1)} %collective-permute-done.refs_2_), channel_id=1, source_target_pairs={{0,1},{1,0},{2,3},{3,2},{4,5},{5,4},{6,7},{7,6},{8,9},{9,8},{10,11... | collective-permute-start | bytes 786440 | tf_op jit(solution)/shard_map/ppermute | solution.py:46
  20.6 5.5 %collective-permute-start.7 = (bf16[32,1024]{1,0:T(8,128)(2,1)S(1)}, bf16[32,1024]{1,0:T(8,128)(2,1)S(1)}, u32[]{:S(2)}, u32[]{:S(2)}) collective-permute-start(bf16[32,1024]{1,0:T(8,128)(2,1)S(1)} %pad_maximum_fusion), channel_id=1, source_target_pairs={{0,4},{4,8},{8,12},{12,16},{16,20},{20,24},{24,28},{28,0},{1,5},{5... | collective-permute-start | bytes 196616 | tf_op jit(solution)/shard_map/ppermute | solution.py:42
  22.1 4.7 %copy-start.1 = (f32[4,128]{1,0:T(4,128)S(1)}, f32[4,128]{1,0:T(4,128)}, u32[]{:S(2)}) copy-start(f32[4,128]{1,0:T(4,128)} %refs_5_.2) | copy-start | bytes 6148
  22.2 4.7 %copy-start.4 = (f32[128]{0:T(128)S(1)}, f32[128]{0:T(128)}, u32[]{:S(2)}) copy-start(f32[128]{0:T(128)} %param.19) | copy-start | bytes 1540
  26.9 0.7 %copy-start = (f32[4,512]{1,0:T(4,128)S(1)}, f32[4,512]{1,0:T(4,128)}, u32[]{:S(2)}) copy-start(f32[4,512]{1,0:T(4,128)} %refs_5_.3) | copy-start | bytes 24580
  26.9 0.7 %copy-start.2 = (f32[512]{0:T(512)S(1)}, f32[512]{0:T(512)}, u32[]{:S(2)}) copy-start(f32[512]{0:T(512)} %param.18) | copy-start | bytes 6148
  27.3 4.3 %collective-permute-start.8 = (bf16[256,128]{1,0:T(8,128)(2,1)S(1)}, bf16[256,128]{1,0:T(8,128)(2,1)S(1)}, u32[]{:S(2)}, u32[]{:S(2)}) collective-permute-start(bf16[256,128]{1,0:T(8,128)(2,1)S(1)} %last_bc.1.own_bc), channel_id=1, source_target_pairs={{0,1},{1,0},{2,3},{3,2},{4,5},{5,4},{6,7},{7,6},{8,9},{9,8},{10,11... | collective-permute-start | bytes 196616 | tf_op jit(solution)/shard_map/ppermute | solution.py:46
  31.8 1.3 %collective-permute-start.9 = (bf16[136,256]{1,0:T(8,128)(2,1)S(1)}, bf16[136,256]{1,0:T(8,128)(2,1)S(1)}, u32[]{:S(2)}, u32[]{:S(2)}) collective-permute-start(bf16[136,256]{1,0:T(8,128)(2,1)S(1)} %get-tuple-element.27), channel_id=1, source_target_pairs={{0,4},{4,0},{8,12},{12,8},{16,20},{20,16},{24,28},{28,24},{1,5},{5... | collective-permute-start | bytes 208904 | tf_op jit(solution)/shard_map/ppermute | solution.py:46
  33.2 7.0 %collective-permute-start.10 = (bf16[136,256]{1,0:T(8,128)(2,1)S(1)}, bf16[136,256]{1,0:T(8,128)(2,1)S(1)}, u32[]{:S(2)}, u32[]{:S(2)}) collective-permute-start(bf16[136,256]{1,0:T(8,128)(2,1)S(1)} %chip_state.1._.refs_4_), channel_id=1, source_target_pairs={{0,8},{4,12},{8,16},{12,20},{16,24},{20,28},{24,0},{28,4},{1,9},{5... | collective-permute-start | bytes 208904 | tf_op jit(solution)/shard_map/ppermute | solution.py:42
  33.3 8.9 %collective-permute-start.11 = (bf16[136,256]{1,0:T(8,128)(2,1)S(1)}, bf16[136,256]{1,0:T(8,128)(2,1)S(1)}, u32[]{:S(2)}, u32[]{:S(2)}) collective-permute-start(bf16[136,256]{1,0:T(8,128)(2,1)S(1)} %chip_state.1._.refs_4_), channel_id=1, source_target_pairs={{0,16},{4,20},{8,24},{12,28},{16,0},{20,4},{24,8},{28,12},{1,17},{... | collective-permute-start | bytes 208904 | tf_op jit(solution)/shard_map/ppermute | solution.py:42
  35.6 6.5 %collective-permute-start.12 = (bf16[136,256]{1,0:T(8,128)(2,1)S(1)}, bf16[136,256]{1,0:T(8,128)(2,1)S(1)}, u32[]{:S(2)}, u32[]{:S(2)}) collective-permute-start(bf16[136,256]{1,0:T(8,128)(2,1)S(1)} %chip_state.1._.refs_4_), channel_id=1, source_target_pairs={{0,24},{4,28},{8,0},{12,4},{16,8},{20,12},{24,16},{28,20},{1,25},{... | collective-permute-start | bytes 208904 | tf_op jit(solution)/shard_map/ppermute | solution.py:42
  37.8 10.0 %copy-start.3 = (f32[512]{0:T(512)S(1)}, f32[512]{0:T(512)}, u32[]{:S(2)}) copy-start(f32[512]{0:T(512)} %param.23) | copy-start | bytes 6148
  42.3 1.3 %collective-permute-start.13 = (bf16[128,256]{1,0:T(8,128)(2,1)S(1)}, bf16[128,256]{1,0:T(8,128)(2,1)S(1)}, u32[]{:S(2)}, u32[]{:S(2)}) collective-permute-start(bf16[128,256]{1,0:T(8,128)(2,1)S(1)} %get-tuple-element.31), channel_id=1, source_target_pairs={{0,4},{4,0},{8,12},{12,8},{16,20},{20,16},{24,28},{28,24},{1,5},{5... | collective-permute-start | bytes 196616 | tf_op jit(solution)/shard_map/ppermute | solution.py:46
  44.1 3.7 %collective-permute-start.14 = (f32[8,256]{1,0:T(8,128)S(1)}, f32[8,256]{1,0:T(8,128)S(1)}, u32[]{:S(2)}, u32[]{:S(2)}) collective-permute-start(f32[8,256]{1,0:T(8,128)S(1)} %get-tuple-element.34.square), channel_id=1, source_target_pairs={{0,1},{1,0},{2,3},{3,2},{4,5},{5,4},{6,7},{7,6},{8,9},{9,8},{10,11... | collective-permute-start | bytes 24584 | tf_op jit(solution)/shard_map/ppermute | solution.py:46

commit v4 on v3

--- a/solution.py
+++ b/solution.py
@@ -7,7 +7,9 @@
 from jax.experimental.pallas import tpu as pltpu
 from jax.sharding import PartitionSpec as P
 
+
 KERNEL = 4
+UPPER = 8
 RIM = 8
 ROWS = 8
 PAD = 4
@@ -24,7 +26,7 @@
         pltpu.with_memory_space_constraint(o, pltpu.HBM) if i < hbm else o
         for i, o in enumerate(operands)
     ]
-    results = pl.pallas_call(
+    call = pl.pallas_call(
         body,
         out_shape=shapes,
         in_specs=[HBM] * hbm + [VMEM] * (len(operands) - hbm),
@@ -32,20 +34,24 @@
         scratch_shapes=list(scratch),
         compiler_params=pltpu.CompilerParams(vmem_limit_bytes=limit),
         cost_estimate=pl.CostEstimate(flops=flops, bytes_accessed=flops // 400, transcendentals=0),
-        name=body.func.__name__ if isinstance(body, functools.partial) else body.__name__,
-    )(*operands)
+    )
+    results = call(*operands)
     return results[0] if single else results
-
-
-def hop(value, axis, distance):
-    size = lax.axis_size(axis)
-    return lax.ppermute(value, axis, [(i, (i + distance) % size) for i in range(size)])
 
 
 def partner(value, axis, mask):
     return lax.ppermute(value, axis, [(i, i ^ mask) for i in range(lax.axis_size(axis))])
 
 
+def across_chips(value, mask):
+    return partner(value, "ctx", 2 * mask)
+
+
+def onward(value, axis):
+    size = lax.axis_size(axis)
+    return lax.ppermute(value, axis, [(i, (i + 1) % size) for i in range(size)])
+
+
 def dot(a, b, **kwargs):
     return jnp.dot(a, b, preferred_element_type=F32, **kwargs)
 
@@ -62,29 +68,42 @@
     return lax.axis_index("ctx") % 2 == 0
 
 
-def fetched_rows(start, source, out, arrival):
-    copy = pltpu.make_async_copy(source.at[pl.ds(start, out.shape[0])], out, arrival)
-    copy.start()
-    copy.wait()
-
-
-def own_product(w_bc, w_x, w_z, top, bottom, sums, weights, arrivals):
-    size, depth, _ = weights.shape
-    place = lax.axis_index("tp")
+def fetched_halves(source, top, bottom, rim, arrivals):
+    rows = source.shape[0]
+    copies = [
+        pltpu.make_async_copy(source.at[pl.ds(start, out.shape[0])], out, arrivals.at[i])
+        for i, (start, out) in enumerate(((top.shape[0], bottom), (0, top), (rows - RIM, rim)))
+    ]
+    for copy in copies:
+        copy.start()
+    for copy in copies:
+        copy.wait()
+
+
+def weight_copies(sources, weights, arrivals, masks):
+    depth = weights.shape[1]
     copies = []
-    for mask in range(size):
-        source_rows = pl.ds(pl.multiple_of(jnp.bitwise_xor(place, mask) * depth, depth), depth)
+    for slot, mask in enumerate(masks):
+        start = pl.multiple_of(jnp.bitwise_xor(lax.axis_index("tp"), mask) * depth, depth)
         column = 0
-        for i, w in enumerate((w_bc, w_x, w_z)):
-            columns = pl.ds(column, w.shape[1])
+        for i, w in enumerate(sources):
+            there = weights.at[slot, :, pl.ds(column, w.shape[1])]
             copies.append(
-                pltpu.make_async_copy(
-                    w.at[source_rows], weights.at[mask, :, columns], arrivals.at[mask, i]
-                )
+                pltpu.make_async_copy(w.at[pl.ds(start, depth)], there, arrivals.at[slot, i])
             )
             column += w.shape[1]
     for copy in copies:
         copy.start()
+    return copies
+
+
+def last_weights(masks, w_bc, w_x, w_z, weights, arrivals):
+    for copy in weight_copies((w_bc, w_x, w_z), weights, arrivals, masks):
+        copy.wait()
+
+
+def own_product(masks, w_bc, w_x, w_z, top, bottom, sums, weights, arrivals):
+    copies = weight_copies((w_bc, w_x, w_z), weights, arrivals, masks)
     for copy in copies[:3]:
         copy.wait()
     sums[...] = dot(jnp.concatenate([top[...], bottom[...]], axis=0), weights[0])
@@ -97,18 +116,21 @@
 
 
 def middle_product(masks, *refs):
-    pieces, (weights, before, _, out) = refs[: 2 * len(masks)], refs[2 * len(masks) :]
+    pieces, (weights, before, out) = refs[: 2 * len(masks)], refs[2 * len(masks) :]
     total = before[...]
     for i, mask in enumerate(masks):
         total += dot(block_of(pieces, i), weights[mask])
     out[...] = total
 
 
-def rim_product(rim, weights, out):
+def rim_product(*refs):
+    pieces, (early, last, out) = refs[:-3], refs[-3:]
+    columns = pl.ds(0, out.shape[1])
     total = None
-    for mask in range(weights.shape[0]):
-        columns = pl.ds(0, out.shape[1])
-        term = dot(rim[pl.ds(mask * RIM, RIM), :], weights[mask, :, columns])
+    for mask, piece in enumerate(pieces):
+        count = early.shape[0]
+        part = early[mask, :, columns] if mask < count else last[mask - count, :, columns]
+        term = dot(piece[...], part)
         total = term if total is None else total + term
     inside = lax.axis_index("ctx") > 0
     out[...] = jnp.where(inside, total, 0.0).astype(BF16).astype(F32)
@@ -117,8 +139,8 @@
 def finished(masks, pieces, weights, before, start, width):
     columns = pl.ds(start, width)
     total = before[:, columns]
-    for i, mask in enumerate(masks):
-        total += dot(block_of(pieces, i), weights[mask, :, columns])
+    for i in range(len(masks)):
+        total += dot(block_of(pieces, i), weights[i, :, columns])
     return total.astype(BF16).astype(F32)
 
 
@@ -157,7 +179,18 @@
     out[...] = silu(finished(masks, pieces, weights, before, before.shape[1] - width, width))
 
 
-def decays(decay_t, step, skip, segment, grown, end_weight, whole, skip_wide):
+def decays(*refs):
+    sources, refs = refs[:3], refs[3:]
+    segment, grown, end_weight, whole, skip_wide, *held, arrivals = refs
+    copies = [
+        pltpu.make_async_copy(source, there, arrivals.at[i])
+        for i, (source, there) in enumerate(zip(sources, held))
+    ]
+    for copy in copies:
+        copy.start()
+    for copy in copies:
+        copy.wait()
+    decay_t, step, skip = held
     heads, rows = decay_t.shape
     width = grown.shape[1]
     dim = width // heads
@@ -245,12 +278,14 @@
     got, (_, _, keep, give) = refs[:-4], refs[-4:]
     (first, first_decay), _ = pair_states(kept, whole, received)
     chip = lax.axis_index("ctx") // 2
+    messages = [read_message(ref) for ref in got]
+    places = [jnp.bitwise_xor(chip, mask) for mask in range(1, len(got) + 1)]
     before = jnp.zeros_like(first)
-    between = jnp.ones_like(first_decay)
-    for k, ref in enumerate(got):
-        state, decay = read_message(ref)
-        before += jnp.where(chip > k, between, 0.0) * state
-        between = between * decay
+    for place, (state, _) in zip(places, messages):
+        weight = jnp.ones_like(first_decay)
+        for other, (_, decay) in zip(places, messages):
+            weight *= jnp.where((other > place) & (other < chip), decay, 1.0)
+        before += jnp.where(place < chip, weight, 0.0) * state
     after = first + first_decay * before
     lead = first_core()
     keep[...] = jnp.where(lead, before, after).astype(BF16)
@@ -312,22 +347,12 @@
         out[:, columns] = (gated[:, columns] * column * gain[:, columns]).astype(BF16)
 
 
-def last_rows(bottom, near_bottom, _, out):
-    end = bottom.shape[0] - RIM
-    out[pl.ds(0, RIM), :] = bottom[pl.ds(end, RIM), :]
-    out[pl.ds(RIM, RIM), :] = near_bottom[pl.ds(end, RIM), :]
-
-
-def gather_pieces(top, bottom, sums, axis):
+def gather_pieces(top, bottom, axis):
     size = lax.axis_size(axis)
     near_bottom = partner(bottom, axis, 1)
-    rim = run(last_rows, ((2 * RIM, bottom.shape[1]), BF16), bottom, near_bottom, sums)
-    if size == 2:
-        return {}, {1: [partner(top, axis, 1), near_bottom]}, rim
     far_top = partner(top, axis, 2)
     near_top = partner(top, axis, 1)
     far_bottom = partner(bottom, axis, 2)
-    rim = jnp.concatenate([rim, partner(rim, axis, 2)], axis=0)
     across_bottom = partner(near_bottom, axis, 2)
     across_top = partner(far_top, axis, 1)
     early = {1: [near_top, near_bottom], 2: [far_top, far_bottom]}
@@ -337,9 +362,15 @@
         early = {**early, **last}
         last = {m | mask: [partner(h, axis, mask) for h in p] for m, p in early.items()}
         last[mask] = [partner(h, axis, mask) for h in (top, bottom)]
-        rim = jnp.concatenate([rim, partner(rim, axis, mask)], axis=0)
         mask *= 2
-    return early, last, rim
+    return early, last
+
+
+def gather_rim(rim, axis):
+    pieces = [onward(rim, "ctx")]
+    for mask in range(1, lax.axis_size(axis)):
+        pieces.append(partner(pieces[0], axis, mask))
+    return pieces
 
 
 def local(
@@ -351,30 +382,41 @@
     n = bc_width
     chips = lax.axis_size("ctx") // 2
 
-    half = rows // 2
-    arrival = [pltpu.SemaphoreType.DMA]
-    bottom, top = [
-        run(functools.partial(fetched_rows, start), ((half, depth), BF16), tokens, scratch=arrival, hbm=1)
-        for start in (half, 0)
-    ]
+    upper = rows * UPPER // 16
+    top, bottom, rim = run(
+        fetched_halves,
+        [((upper, depth), BF16), ((rows - upper, depth), BF16), ((RIM, depth), BF16)],
+        tokens,
+        scratch=[pltpu.SemaphoreType.DMA((3,))],
+        hbm=1,
+    )
+
     def flops(*sizes):
         total = 2
         for s in sizes:
             total *= s
         return total
 
-    size = lax.axis_size("tp")
+    early, last = gather_pieces(top, bottom, "tp")
+    rims = gather_rim(rim, "tp")
     everything = bc_width + 2 * width
+    masks = (0, *sorted(early))
     sums, weights = run(
-        own_product,
-        [((rows, everything), F32), ((size, depth, everything), BF16)],
+        functools.partial(own_product, masks),
+        [((rows, everything), F32), ((len(masks), depth, everything), BF16)],
         w_bc, w_x, w_z, top, bottom,
-        scratch=[pltpu.SemaphoreType.DMA((size, 3))],
+        scratch=[pltpu.SemaphoreType.DMA((len(masks), 3))],
         flops=flops(rows, depth, everything),
         hbm=3,
     )
-    early, last, rim = gather_pieces(top, bottom, sums, "tp")
-    rim = hop(rim, "ctx", 1)
+    masks = tuple(sorted(last))
+    weights_end = run(
+        functools.partial(last_weights, masks),
+        ((len(masks), depth, everything), BF16),
+        w_bc, w_x, w_z,
+        scratch=[pltpu.SemaphoreType.DMA((len(masks), 3))],
+        hbm=3,
+    )
     segment, grown, end_weight, whole, skip_wide = run(
         decays,
         [
@@ -385,20 +427,26 @@
             ((1, width), F32),
         ],
         decay_logarithm.T, head_step.reshape(1, -1), skip.reshape(1, -1),
+        scratch=[
+            pltpu.VMEM((heads, rows), F32),
+            pltpu.VMEM((1, heads), F32),
+            pltpu.VMEM((1, heads), F32),
+            pltpu.SemaphoreType.DMA((3,)),
+        ],
+        hbm=3,
         flops=flops(rows, rows, width),
     )
-    if early:
-        masks = tuple(sorted(early))
-        sums = run(
-            functools.partial(middle_product, masks),
-            ((rows, everything), F32),
-            *[h for m in masks for h in early[m]], weights, sums, skip_wide,
-            flops=len(masks) * flops(rows, depth, everything),
-        )
+    masks = tuple(sorted(early))
+    sums = run(
+        functools.partial(middle_product, masks),
+        ((rows, everything), F32),
+        *[h for m in masks for h in early[m]], weights, sums,
+        flops=len(masks) * flops(rows, depth, everything),
+    )
     rim_sums = run(
         rim_product,
         ((RIM, bc_width + width), F32),
-        rim, weights,
+        *rims, weights, weights_end,
         flops=flops(rows, depth, width),
     )
 
@@ -407,7 +455,7 @@
     own_bc = run(
         functools.partial(last_bc, masks),
         ((rows, bc_width), BF16),
-        *ends, weights, sums, rim_sums, conv_bc, bias_bc.reshape(1, -1),
+        *ends, weights_end, sums, rim_sums, conv_bc, bias_bc.reshape(1, -1),
         scratch=[pltpu.VMEM((rows + RIM, bc_width), F32)],
         flops=flops(rows, depth, bc_width),
     )
@@ -415,7 +463,7 @@
     x, weighted = run(
         functools.partial(last_x, masks),
         [((rows, width), BF16), ((rows, width), BF16)],
-        *ends, weights, sums, rim_sums, conv_x, bias_x.reshape(1, -1), end_weight,
+        *ends, weights_end, sums, rim_sums, conv_x, bias_x.reshape(1, -1), end_weight,
         scratch=[pltpu.VMEM((rows + RIM, width), F32)],
         flops=flops(rows, depth, width),
     )
@@ -429,7 +477,9 @@
     )
     received = partner(message, "ctx", 1)
     message = run(chip_state, message_shape, kept, whole, received)
-    got = [hop(message, "ctx", 2 * k) for k in range(1, chips)]
+    got = []
+    for mask in range(1, chips):
+        got.append(across_chips(message, mask))
     within = run(
         within_section,
         ((rows, width), F32),
@@ -439,7 +489,7 @@
     gate = run(
         functools.partial(last_z, masks),
         ((rows, width), F32),
-        *ends, weights, sums, message,
+        *ends, weights_end, sums, message,
         flops=flops(rows, depth, width),
     )
     keep, give = run(

time: 49.1 us -> 59.5 us (1.21)
  waiting for transfers between devices: 22.1 us -> 27.3 us
  starting transfers between devices: 12.5 us -> 17.2 us
  Pallas kernels: 13.8 us -> 14.6 us
    ppermute x11 -> x16, starting transfers between devices: 8.6 us -> 17.2 us  [partner(): lax.ppermute(value, axis, [(i, i ^ mask) for i in range(lax.axis_size(axi...]
    ppermute x11 -> x16, waiting for transfers between devices: 14.4 us -> 22.3 us  [partner(): lax.ppermute(value, axis, [(i, i ^ mask) for i in range(lax.axis_size(axi...]
    ppermute x4 -> x1, starting transfers between devices: 3.87 us -> 0.01 us  [onward(): return lax.ppermute(value, axis, [(i, (i + 1) % size) for i in range(size)])]
    ppermute x4 -> x1, waiting for transfers between devices: 7.72 us -> 4.96 us  [onward(): return lax.ppermute(value, axis, [(i, (i + 1) % size) for i in range(size)])]
    pallas_call x16 -> x15, Pallas kernels: 13.8 us -> 14.6 us  [run(): results = call(*operands)]
  transfers between devices with their start and end apart: 15 -> 17, of which waited for: 10 -> 10; matrix products, arithmetic and copies ran while one was open for 0% -> 0% of each run, Pallas kernels for 22% -> 19%
where the time goes in v4:
time: 59.5 us; the launch traced here: 59.3 us
  waiting for transfers between devices  27.3 us (46%)
  starting transfers between devices  17.2 us (29%)
  Pallas kernels  14.6 us (25%)
    ppermute x16, waiting for transfers between devices, partner(): lax.ppermute(value, axis, [(i, i ^ mask) for i in range(lax.axis_size(axi...  22.3 us
    ppermute x16, starting transfers between devices, partner(): lax.ppermute(value, axis, [(i, i ^ mask) for i in range(lax.axis_size(axi...  17.2 us
    pallas_call x15, Pallas kernels, run(): results = call(*operands)  14.6 us
    ppermute x1, waiting for transfers between devices, onward(): return lax.ppermute(value, axis, [(i, (i + 1) % size) for i in range(size)])  4.96 us
  transfers between devices with their start and end apart: 17, of which 10 were waited for; matrix products, arithmetic and copies ran while one was open for 0% of the time, Pallas kernels for 19%

profile of v4, /device:TPU:0, one launch (start us, length us, event | category | flops | bytes accessed | tf_op | source)
XLA Modules:
  0.0 59.3 jit_solution(9259100601515131055)
XLA Ops:
  0.0 1.1 %shard_map.118 = (bf16[128,1024]{1,0:T(8,128)(2,1)S(1)}, bf16[128,1024]{1,0:T(8,128)(2,1)S(1)}, bf16[8,1024]{1,0:T(8,128)(2,1)S(1)}) custom-call(bf16[256,1024]{1,0:T(8,128)(2,1)} %source.1), custom_call_target="tpu_custom_call" | custom-call | flops 1000000 | bytes 2500 | tf_op jit(solution)/shard_map/pallas_call | solution.py:38
  1.1 3.1 %collective-permute-start = (bf16[128,1024]{1,0:T(8,128)(2,1)S(1)}, bf16[128,1024]{1,0:T(8,128)(2,1)S(1)}, u32[]{:S(2)}, u32[]{:S(2)}) collective-permute-start(bf16[128,1024]{1,0:T(8,128)(2,1)S(1)} %get-tuple-element.23.top), channel_id=1, source_target_pairs={{0,2},{1,3},{2,0},{3,1},{4,6},{5,7},{6,4},{7,5},{8,10},{9,11},{10,... | collective-permute-start | bytes 786440 | tf_op jit(solution)/shard_map/ppermute | solution.py:43
  4.1 1.5 %collective-permute-start.2 = (bf16[128,1024]{1,0:T(8,128)(2,1)S(1)}, bf16[128,1024]{1,0:T(8,128)(2,1)S(1)}, u32[]{:S(2)}, u32[]{:S(2)}) collective-permute-start(bf16[128,1024]{1,0:T(8,128)(2,1)S(1)} %get-tuple-element.24.bottom), channel_id=1, source_target_pairs={{0,1},{1,0},{2,3},{3,2},{4,5},{5,4},{6,7},{7,6},{8,9},{9,8},{10,11... | collective-permute-start | bytes 786440 | tf_op jit(solution)/shard_map/ppermute | solution.py:43
  5.6 0.5 collective-permute-start.4
  6.2 0.1 collective-permute-start.5
  6.2 5.0 %collective-permute-done.refs_2_ = bf16[128,1024]{1,0:T(8,128)(2,1)S(1)} collective-permute-done((bf16[128,1024]{1,0:T(8,128)(2,1)S(1)}, bf16[128,1024]{1,0:T(8,128)(2,1)S(1)}, u32[]{:S(2)}, u32[]{:S(2)}) %collective-permute-start) | collective-permute-done | bytes 262176 | tf_op jit(solution)/shard_map/ppermute | solution.py:43
  11.3 2.0 %collective-permute-start.1 = (bf16[128,1024]{1,0:T(8,128)(2,1)S(1)}, bf16[128,1024]{1,0:T(8,128)(2,1)S(1)}, u32[]{:S(2)}, u32[]{:S(2)}) collective-permute-start(bf16[128,1024]{1,0:T(8,128)(2,1)S(1)} %collective-permute-done.refs_2_), channel_id=1, source_target_pairs={{0,1},{1,0},{2,3},{3,2},{4,5},{5,4},{6,7},{7,6},{8,9},{9,8},{10,11... | collective-permute-start | bytes 786440 | tf_op jit(solution)/shard_map/ppermute | solution.py:43
  13.3 0.0 collective-permute-done.2.refs_1_
  13.3 1.5 %collective-permute-start.3 = (bf16[128,1024]{1,0:T(8,128)(2,1)S(1)}, bf16[128,1024]{1,0:T(8,128)(2,1)S(1)}, u32[]{:S(2)}, u32[]{:S(2)}) collective-permute-start(bf16[128,1024]{1,0:T(8,128)(2,1)S(1)} %collective-permute-done.2.refs_1_), channel_id=1, source_target_pairs={{0,2},{1,3},{2,0},{3,1},{4,6},{5,7},{6,4},{7,5},{8,10},{9,11},{10,... | collective-permute-start | bytes 786440 | tf_op jit(solution)/shard_map/ppermute | solution.py:43
  14.8 0.0 collective-permute-start.6
  14.8 5.0 %collective-permute-done.6.refs_0_ = bf16[8,1024]{1,0:T(8,128)(2,1)S(1)} collective-permute-done((bf16[8,1024]{1,0:T(8,128)(2,1)S(1)}, bf16[8,1024]{1,0:T(8,128)(2,1)S(1)}, u32[]{:S(2)}, u32[]{:S(2)}) %collective-permute-start.6) | collective-permute-done | bytes 16416 | tf_op jit(solution)/shard_map/ppermute | solution.py:52
  19.8 0.5 collective-permute-start.7
  20.3 3.2 %collective-permute-done.7.refs_1_ = bf16[8,1024]{1,0:T(8,128)(2,1)S(1)} collective-permute-done((bf16[8,1024]{1,0:T(8,128)(2,1)S(1)}, bf16[8,1024]{1,0:T(8,128)(2,1)S(1)}, u32[]{:S(2)}, u32[]{:S(2)}) %collective-permute-start.7) | collective-permute-done | bytes 16416 | tf_op jit(solution)/shard_map/ppermute | solution.py:43
  23.5 0.5 collective-permute-start.8
  24.0 3.2 %collective-permute-done.8.refs_2_ = bf16[8,1024]{1,0:T(8,128)(2,1)S(1)} collective-permute-done((bf16[8,1024]{1,0:T(8,128)(2,1)S(1)}, bf16[8,1024]{1,0:T(8,128)(2,1)S(1)}, u32[]{:S(2)}, u32[]{:S(2)}) %collective-permute-start.8) | collective-permute-done | bytes 16416 | tf_op jit(solution)/shard_map/ppermute | solution.py:43
  27.2 1.5 %collective-permute-start.9 = (bf16[8,1024]{1,0:T(8,128)(2,1)S(1)}, bf16[8,1024]{1,0:T(8,128)(2,1)S(1)}, u32[]{:S(2)}, u32[]{:S(2)}) collective-permute-start(bf16[8,1024]{1,0:T(8,128)(2,1)S(1)} %collective-permute-done.6.refs_0_), channel_id=1, source_target_pairs={{0,3},{1,2},{2,1},{3,0},{4,7},{5,6},{6,5},{7,4},{8,11},{9,10},{10,... | collective-permute-start | bytes 49160 | tf_op jit(solution)/shard_map/ppermute | solution.py:43
  28.7 3.1 %shard_map.120 = (f32[256,1152]{1,0:T(8,128)S(1)}, bf16[3,1024,1152]{2,1,0:T(8,128)(2,1)S(1)}) custom-call(bf16[4096,128]{1,0:T(8,128)(2,1)} %w_bc.3, bf16[4096,512]{1,0:T(8,128)(2,1)} %w_x.3, bf16[4096,512]{1,0:T(8,128)(2,1)} %w_z.3, bf16[128,1024]{1,0:T(8,128)(2,1)S(1)} %get-tuple-element.23.top, bf16[128,1024]{1,0:T(8,128)(2,1)S(1)} %get-tuple-element.24.bottom), custom_call_target="tpu_custom_call" | custom-call | flops 603979776 | bytes 1509949 | tf_op jit(solution)/shard_map/pallas_call | solution.py:38
  31.8 1.7 %shard_map.119.refs_5_.refs_2_ = bf16[1,1024,1152]{2,1,0:T(8,128)(2,1)S(1)} custom-call(bf16[4096,128]{1,0:T(8,128)(2,1)} %w_bc.3, bf16[4096,512]{1,0:T(8,128)(2,1)} %w_x.3, bf16[4096,512]{1,0:T(8,128)(2,1)} %w_z.3), custom_call_target="tpu_custom_call" | custom-call | flops 1000000 | bytes 2500 | tf_op jit(solution)/shard_map/pallas_call | solution.py:38
  33.5 0.0 collective-permute-done.9.refs_3_
  33.5 0.8 %shard_map.122.refs_4_ = f32[8,640]{1,0:T(8,128)S(1)} custom-call(bf16[8,1024]{1,0:T(8,128)(2,1)S(1)} %collective-permute-done.6.refs_0_, bf16[8,1024]{1,0:T(8,128)(2,1)S(1)} %collective-permute-done.7.refs_1_, bf16[8,1024]{1,0:T(8,128)(2,1)S(1)} %collective-permute-done.8.refs_2_, bf16[8,1024]{1,0:T(8,128)(2,1)S(1)} %collective-permute-done.9.refs_3_, ...), custom_call_target="tpu_custom_call" | custom-call | flops 268435456 | bytes 671088 | tf_op jit(solution)/shard_map/pallas_call | solution.py:38
  34.3 0.0 collective-permute-done.4.refs_0_
  34.3 0.0 collective-permute-done.5.refs_3_
  34.3 0.0 copy-start.2
  34.3 0.0 copy-start.4
  34.3 1.5 %shard_map.121.refs_3_ = f32[256,1152]{1,0:T(8,128)S(1)} custom-call(bf16[128,1024]{1,0:T(8,128)(2,1)S(1)} %collective-permute-done.4.refs_0_, bf16[128,1024]{1,0:T(8,128)(2,1)S(1)} %collective-permute-done.2.refs_1_, bf16[128,1024]{1,0:T(8,128)(2,1)S(1)} %collective-permute-done.refs_2_, bf16[128,1024]{1,0:T(8,128)(2,1)S(1)} %collective-permute-done.5.refs_3_, ...), custom_call_target="tpu_custom_call" | custom-call | flops 1207959552 | bytes 3019898 | tf_op jit(solution)/shard_map/pallas_call | solution.py:38
  35.9 0.0 copy-start
  35.9 0.0 copy-start.1
  35.9 0.0 collective-permute-done.1.refs_0_
  35.9 0.0 collective-permute-done.3.refs_1_
  35.9 0.0 copy-done.2
  35.9 0.0 copy-done.4
  35.9 0.4 shard_map.123.own_bc
  36.3 0.6 %collective-permute-start.10 = (bf16[256,128]{1,0:T(8,128)(2,1)S(1)}, bf16[256,128]{1,0:T(8,128)(2,1)S(1)}, u32[]{:S(2)}, u32[]{:S(2)}) collective-permute-start(bf16[256,128]{1,0:T(8,128)(2,1)S(1)} %shard_map.123.own_bc), channel_id=1, source_target_pairs={{0,1},{1,0},{2,3},{3,2},{4,5},{5,4},{6,7},{7,6},{8,9},{9,8},{10,11... | collective-permute-start | bytes 196616 | tf_op jit(solution)/shard_map/ppermute | solution.py:43
  36.9 1.9 %shard_map.124 = (bf16[8,256,256]{2,1,0:T(8,128)(2,1)S(1)}, f32[256,512]{1,0:T(8,128)S(1)}, f32[256,512]{1,0:T(8,128)S(1)}, f32[8,512]{1,0:T(8,128)S(1)}, f32[1,512]{1,0:T(1,128)S(1)}) custom-call(f32[8,256]{1,0:T(8,128)} %bitcast.9, f32[1,8]{1,0:T(1,128)} %bitcast.10, f32[1,8]{1,0:T(1,128)} %bitcast.11), custom_call_target="tpu_custom_call" | custom-call | flops 67108864 | bytes 167772 | tf_op jit(solution)/shard_map/pallas_call | solution.py:38
  38.8 0.0 copy-done
  38.8 0.0 copy-done.1
  38.8 1.1 %shard_map.125 = (bf16[256,512]{1,0:T(8,128)(2,1)S(1)}, bf16[256,512]{1,0:T(8,128)(2,1)S(1)}) custom-call(bf16[128,1024]{1,0:T(8,128)(2,1)S(1)} %collective-permute-done.1.refs_0_, bf16[128,1024]{1,0:T(8,128)(2,1)S(1)} %collective-permute-done.3.refs_1_, bf16[1,1024,1152]{2,1,0:T(8,128)(2,1)S(1)} %shard_map.119.refs_5_.refs_2_, ...), custom_call_target="tpu_custom_call" | custom-call | flops 268435456 | bytes 671088 | tf_op jit(solution)/shard_map/pallas_call | solution.py:38
  39.9 0.7 %collective-permute-done.10.other_bc = bf16[256,128]{1,0:T(8,128)(2,1)S(1)} collective-permute-done((bf16[256,128]{1,0:T(8,128)(2,1)S(1)}, bf16[256,128]{1,0:T(8,128)(2,1)S(1)}, u32[]{:S(2)}, u32[]{:S(2)}) %collective-permute-start.10) | collective-permute-done | bytes 65568 | tf_op jit(solution)/shard_map/ppermute | solution.py:43
  40.6 0.2 shard_map.126
  40.9 0.1 collective-permute-start.11
  40.9 1.2 %collective-permute-done.11.received = bf16[136,256]{1,0:T(8,128)(2,1)S(1)} collective-permute-done((bf16[136,256]{1,0:T(8,128)(2,1)S(1)}, bf16[136,256]{1,0:T(8,128)(2,1)S(1)}, u32[]{:S(2)}, u32[]{:S(2)}) %collective-permute-start.11) | collective-permute-done | bytes 69664 | tf_op jit(solution)/shard_map/ppermute | solution.py:43
  42.2 1.6 %collective-permute-start.12 = (bf16[136,256]{1,0:T(8,128)(2,1)S(1)}, bf16[136,256]{1,0:T(8,128)(2,1)S(1)}, u32[]{:S(2)}, u32[]{:S(2)}) collective-permute-start(bf16[136,256]{1,0:T(8,128)(2,1)S(1)} %shard_map.127._.refs_4_), channel_id=1, source_target_pairs={{0,8},{4,12},{8,0},{12,4},{16,24},{20,28},{24,16},{28,20},{1,9},{5... | collective-permute-start | bytes 208904 | tf_op jit(solution)/shard_map/ppermute | solution.py:43
  43.8 2.6 %collective-permute-start.13 = (bf16[136,256]{1,0:T(8,128)(2,1)S(1)}, bf16[136,256]{1,0:T(8,128)(2,1)S(1)}, u32[]{:S(2)}, u32[]{:S(2)}) collective-permute-start(bf16[136,256]{1,0:T(8,128)(2,1)S(1)} %shard_map.127._.refs_4_), channel_id=1, source_target_pairs={{0,16},{4,20},{8,24},{12,28},{16,0},{20,4},{24,8},{28,12},{1,17},{... | collective-permute-start | bytes 208904 | tf_op jit(solution)/shard_map/ppermute | solution.py:43
  46.4 0.3 collective-permute-start.14
  46.7 0.7 %shard_map.128.refs_3_.within = f32[256,512]{1,0:T(8,128)S(1)} custom-call(bf16[256,128]{1,0:T(8,128)(2,1)S(1)} %shard_map.123.own_bc, bf16[256,128]{1,0:T(8,128)(2,1)S(1)} %collective-permute-done.10.other_bc, bf16[256,512]{1,0:T(8,128)(2,1)S(1)} %get-tuple-element.33.x, bf16[8,256,256]{2,1,0:T(8,128)(2,1)S(1)} %get-tuple-element.34.segment, ...), custom_call_target="tpu_custom_call" | custom-call | flops 201326592 | bytes 503316 | tf_op jit(solution)/shard_map/pallas_call | solution.py:38
  47.4 0.0 copy-start.3
  47.4 0.5 shard_map.129.refs_4_.gate
  47.9 0.0 collective-permute-done.12.refs_0_
  47.9 3.7 %collective-permute-done.13.refs_1_ = bf16[136,256]{1,0:T(8,128)(2,1)S(1)} collective-permute-done((bf16[136,256]{1,0:T(8,128)(2,1)S(1)}, bf16[136,256]{1,0:T(8,128)(2,1)S(1)}, u32[]{:S(2)}, u32[]{:S(2)}) %collective-permute-start.13) | collective-permute-done | bytes 69664 | tf_op jit(solution)/shard_map/ppermute | solution.py:43
  51.6 1.0 %collective-permute-done.14.refs_2_ = bf16[136,256]{1,0:T(8,128)(2,1)S(1)} collective-permute-done((bf16[136,256]{1,0:T(8,128)(2,1)S(1)}, bf16[136,256]{1,0:T(8,128)(2,1)S(1)}, u32[]{:S(2)}, u32[]{:S(2)}) %collective-permute-start.14) | collective-permute-done | bytes 69664 | tf_op jit(solution)/shard_map/ppermute | solution.py:43
  52.6 0.1 shard_map.130
  52.7 0.1 collective-permute-start.15
  52.8 1.2 %collective-permute-done.15.take = bf16[128,256]{1,0:T(8,128)(2,1)S(1)} collective-permute-done((bf16[128,256]{1,0:T(8,128)(2,1)S(1)}, bf16[128,256]{1,0:T(8,128)(2,1)S(1)}, u32[]{:S(2)}, u32[]{:S(2)}) %collective-permute-start.15) | collective-permute-done | bytes 65568 | tf_op jit(solution)/shard_map/ppermute | solution.py:43
  54.1 0.5 shard_map.131
  54.6 0.8 %collective-permute-start.16 = (f32[8,256]{1,0:T(8,128)S(1)}, f32[8,256]{1,0:T(8,128)S(1)}, u32[]{:S(2)}, u32[]{:S(2)}) collective-permute-start(f32[8,256]{1,0:T(8,128)S(1)} %get-tuple-element.40.square), channel_id=1, source_target_pairs={{0,1},{1,0},{2,3},{3,2},{4,5},{5,4},{6,7},{7,6},{8,9},{9,8},{10,11... | collective-permute-start | bytes 24584 | tf_op jit(solution)/shard_map/ppermute | solution.py:43
  55.4 2.9 %collective-permute-done.16.other_square = f32[8,256]{1,0:T(8,128)S(1)} collective-permute-done((f32[8,256]{1,0:T(8,128)S(1)}, f32[8,256]{1,0:T(8,128)S(1)}, u32[]{:S(2)}, u32[]{:S(2)}) %collective-permute-start.16) | collective-permute-done | bytes 8224 | tf_op jit(solution)/shard_map/ppermute | solution.py:43
  58.3 0.0 copy-done.3
  58.3 1.1 %shard_map.132 = bf16[256,512]{1,0:T(8,128)(2,1)} custom-call(f32[256,512]{1,0:T(8,128)S(1)} %get-tuple-element.39.gated, f32[8,256]{1,0:T(8,128)S(1)} %get-tuple-element.40.square, f32[8,256]{1,0:T(8,128)S(1)} %collective-permute-done.16.other_square, f32[1,512]{1,0:T(1,128)S(1)} %bitcast.7), custom_call_target="tpu_custom_call" | custom-call | flops 1000000 | bytes 2500 | tf_op jit(solution)/shard_map/pallas_call | solution.py:38
  (1 shorter events, 0.0 us)
Async XLA Ops:
  1.1 10.2 %collective-permute-start = (bf16[128,1024]{1,0:T(8,128)(2,1)S(1)}, bf16[128,1024]{1,0:T(8,128)(2,1)S(1)}, u32[]{:S(2)}, u32[]{:S(2)}) collective-permute-start(bf16[128,1024]{1,0:T(8,128)(2,1)S(1)} %get-tuple-element.23.top), channel_id=1, source_target_pairs={{0,2},{1,3},{2,0},{3,1},{4,6},{5,7},{6,4},{7,5},{8,10},{9,11},{10,... | collective-permute-start | bytes 786440 | tf_op jit(solution)/shard_map/ppermute | solution.py:43
  4.1 9.2 %collective-permute-start.2 = (bf16[128,1024]{1,0:T(8,128)(2,1)S(1)}, bf16[128,1024]{1,0:T(8,128)(2,1)S(1)}, u32[]{:S(2)}, u32[]{:S(2)}) collective-permute-start(bf16[128,1024]{1,0:T(8,128)(2,1)S(1)} %get-tuple-element.24.bottom), channel_id=1, source_target_pairs={{0,1},{1,0},{2,3},{3,2},{4,5},{5,4},{6,7},{7,6},{8,9},{9,8},{10,11... | collective-permute-start | bytes 786440 | tf_op jit(solution)/shard_map/ppermute | solution.py:43
  5.6 28.7 %collective-permute-start.4 = (bf16[128,1024]{1,0:T(8,128)(2,1)S(1)}, bf16[128,1024]{1,0:T(8,128)(2,1)S(1)}, u32[]{:S(2)}, u32[]{:S(2)}) collective-permute-start(bf16[128,1024]{1,0:T(8,128)(2,1)S(1)} %get-tuple-element.23.top), channel_id=1, source_target_pairs={{0,1},{1,0},{2,3},{3,2},{4,5},{5,4},{6,7},{7,6},{8,9},{9,8},{10,11... | collective-permute-start | bytes 786440 | tf_op jit(solution)/shard_map/ppermute | solution.py:43
  6.2 28.2 %collective-permute-start.5 = (bf16[128,1024]{1,0:T(8,128)(2,1)S(1)}, bf16[128,1024]{1,0:T(8,128)(2,1)S(1)}, u32[]{:S(2)}, u32[]{:S(2)}) collective-permute-start(bf16[128,1024]{1,0:T(8,128)(2,1)S(1)} %get-tuple-element.24.bottom), channel_id=1, source_target_pairs={{0,2},{1,3},{2,0},{3,1},{4,6},{5,7},{6,4},{7,5},{8,10},{9,11},{10,... | collective-permute-start | bytes 786440 | tf_op jit(solution)/shard_map/ppermute | solution.py:43
  11.3 24.6 %collective-permute-start.1 = (bf16[128,1024]{1,0:T(8,128)(2,1)S(1)}, bf16[128,1024]{1,0:T(8,128)(2,1)S(1)}, u32[]{:S(2)}, u32[]{:S(2)}) collective-permute-start(bf16[128,1024]{1,0:T(8,128)(2,1)S(1)} %collective-permute-done.refs_2_), channel_id=1, source_target_pairs={{0,1},{1,0},{2,3},{3,2},{4,5},{5,4},{6,7},{7,6},{8,9},{9,8},{10,11... | collective-permute-start | bytes 786440 | tf_op jit(solution)/shard_map/ppermute | solution.py:43
  13.3 22.6 %collective-permute-start.3 = (bf16[128,1024]{1,0:T(8,128)(2,1)S(1)}, bf16[128,1024]{1,0:T(8,128)(2,1)S(1)}, u32[]{:S(2)}, u32[]{:S(2)}) collective-permute-start(bf16[128,1024]{1,0:T(8,128)(2,1)S(1)} %collective-permute-done.2.refs_1_), channel_id=1, source_target_pairs={{0,2},{1,3},{2,0},{3,1},{4,6},{5,7},{6,4},{7,5},{8,10},{9,11},{10,... | collective-permute-start | bytes 786440 | tf_op jit(solution)/shard_map/ppermute | solution.py:43
  14.8 5.0 %collective-permute-start.6 = (bf16[8,1024]{1,0:T(8,128)(2,1)S(1)}, bf16[8,1024]{1,0:T(8,128)(2,1)S(1)}, u32[]{:S(2)}, u32[]{:S(2)}) collective-permute-start(bf16[8,1024]{1,0:T(8,128)(2,1)S(1)} %get-tuple-element.27), channel_id=1, source_target_pairs={{0,4},{4,8},{8,12},{12,16},{16,20},{20,24},{24,28},{28,0},{1,5},{5... | collective-permute-start | bytes 49160 | tf_op jit(solution)/shard_map/ppermute | solution.py:52
  19.8 3.7 %collective-permute-start.7 = (bf16[8,1024]{1,0:T(8,128)(2,1)S(1)}, bf16[8,1024]{1,0:T(8,128)(2,1)S(1)}, u32[]{:S(2)}, u32[]{:S(2)}) collective-permute-start(bf16[8,1024]{1,0:T(8,128)(2,1)S(1)} %collective-permute-done.6.refs_0_), channel_id=1, source_target_pairs={{0,1},{1,0},{2,3},{3,2},{4,5},{5,4},{6,7},{7,6},{8,9},{9,8},{10,11... | collective-permute-start | bytes 49160 | tf_op jit(solution)/shard_map/ppermute | solution.py:43
  23.5 3.7 %collective-permute-start.8 = (bf16[8,1024]{1,0:T(8,128)(2,1)S(1)}, bf16[8,1024]{1,0:T(8,128)(2,1)S(1)}, u32[]{:S(2)}, u32[]{:S(2)}) collective-permute-start(bf16[8,1024]{1,0:T(8,128)(2,1)S(1)} %collective-permute-done.6.refs_0_), channel_id=1, source_target_pairs={{0,2},{1,3},{2,0},{3,1},{4,6},{5,7},{6,4},{7,5},{8,10},{9,11},{10,... | collective-permute-start | bytes 49160 | tf_op jit(solution)/shard_map/ppermute | solution.py:43
  27.2 6.3 %collective-permute-start.9 = (bf16[8,1024]{1,0:T(8,128)(2,1)S(1)}, bf16[8,1024]{1,0:T(8,128)(2,1)S(1)}, u32[]{:S(2)}, u32[]{:S(2)}) collective-permute-start(bf16[8,1024]{1,0:T(8,128)(2,1)S(1)} %collective-permute-done.6.refs_0_), channel_id=1, source_target_pairs={{0,3},{1,2},{2,1},{3,0},{4,7},{5,6},{6,5},{7,4},{8,11},{9,10},{10,... | collective-permute-start | bytes 49160 | tf_op jit(solution)/shard_map/ppermute | solution.py:43
  34.3 1.6 %copy-start.2 = (f32[4,128]{1,0:T(4,128)S(1)}, f32[4,128]{1,0:T(4,128)}, u32[]{:S(2)}) copy-start(f32[4,128]{1,0:T(4,128)} %refs_5_.2) | copy-start | bytes 6148
  34.3 1.6 %copy-start.4 = (f32[128]{0:T(128)S(1)}, f32[128]{0:T(128)}, u32[]{:S(2)}) copy-start(f32[128]{0:T(128)} %param.19) | copy-start | bytes 1540
  35.9 2.9 %copy-start = (f32[4,512]{1,0:T(4,128)S(1)}, f32[4,512]{1,0:T(4,128)}, u32[]{:S(2)}) copy-start(f32[4,512]{1,0:T(4,128)} %refs_5_.3) | copy-start | bytes 24580
  35.9 2.9 %copy-start.1 = (f32[512]{0:T(512)S(1)}, f32[512]{0:T(512)}, u32[]{:S(2)}) copy-start(f32[512]{0:T(512)} %param.18) | copy-start | bytes 6148
  36.3 4.3 %collective-permute-start.10 = (bf16[256,128]{1,0:T(8,128)(2,1)S(1)}, bf16[256,128]{1,0:T(8,128)(2,1)S(1)}, u32[]{:S(2)}, u32[]{:S(2)}) collective-permute-start(bf16[256,128]{1,0:T(8,128)(2,1)S(1)} %shard_map.123.own_bc), channel_id=1, source_target_pairs={{0,1},{1,0},{2,3},{3,2},{4,5},{5,4},{6,7},{7,6},{8,9},{9,8},{10,11... | collective-permute-start | bytes 196616 | tf_op jit(solution)/shard_map/ppermute | solution.py:43
  40.9 1.3 %collective-permute-start.11 = (bf16[136,256]{1,0:T(8,128)(2,1)S(1)}, bf16[136,256]{1,0:T(8,128)(2,1)S(1)}, u32[]{:S(2)}, u32[]{:S(2)}) collective-permute-start(bf16[136,256]{1,0:T(8,128)(2,1)S(1)} %get-tuple-element.32), channel_id=1, source_target_pairs={{0,4},{4,0},{8,12},{12,8},{16,20},{20,16},{24,28},{28,24},{1,5},{5... | collective-permute-start | bytes 208904 | tf_op jit(solution)/shard_map/ppermute | solution.py:43
  42.2 5.7 %collective-permute-start.12 = (bf16[136,256]{1,0:T(8,128)(2,1)S(1)}, bf16[136,256]{1,0:T(8,128)(2,1)S(1)}, u32[]{:S(2)}, u32[]{:S(2)}) collective-permute-start(bf16[136,256]{1,0:T(8,128)(2,1)S(1)} %shard_map.127._.refs_4_), channel_id=1, source_target_pairs={{0,8},{4,12},{8,0},{12,4},{16,24},{20,28},{24,16},{28,20},{1,9},{5... | collective-permute-start | bytes 208904 | tf_op jit(solution)/shard_map/ppermute | solution.py:43
  43.8 7.8 %collective-permute-start.13 = (bf16[136,256]{1,0:T(8,128)(2,1)S(1)}, bf16[136,256]{1,0:T(8,128)(2,1)S(1)}, u32[]{:S(2)}, u32[]{:S(2)}) collective-permute-start(bf16[136,256]{1,0:T(8,128)(2,1)S(1)} %shard_map.127._.refs_4_), channel_id=1, source_target_pairs={{0,16},{4,20},{8,24},{12,28},{16,0},{20,4},{24,8},{28,12},{1,17},{... | collective-permute-start | bytes 208904 | tf_op jit(solution)/shard_map/ppermute | solution.py:43
  46.4 6.2 %collective-permute-start.14 = (bf16[136,256]{1,0:T(8,128)(2,1)S(1)}, bf16[136,256]{1,0:T(8,128)(2,1)S(1)}, u32[]{:S(2)}, u32[]{:S(2)}) collective-permute-start(bf16[136,256]{1,0:T(8,128)(2,1)S(1)} %shard_map.127._.refs_4_), channel_id=1, source_target_pairs={{0,24},{4,28},{8,16},{12,20},{16,8},{20,12},{24,0},{28,4},{1,25},{... | collective-permute-start | bytes 208904 | tf_op jit(solution)/shard_map/ppermute | solution.py:43
  47.4 10.9 %copy-start.3 = (f32[512]{0:T(512)S(1)}, f32[512]{0:T(512)}, u32[]{:S(2)}) copy-start(f32[512]{0:T(512)} %param.23) | copy-start | bytes 6148
  52.7 1.3 %collective-permute-start.15 = (bf16[128,256]{1,0:T(8,128)(2,1)S(1)}, bf16[128,256]{1,0:T(8,128)(2,1)S(1)}, u32[]{:S(2)}, u32[]{:S(2)}) collective-permute-start(bf16[128,256]{1,0:T(8,128)(2,1)S(1)} %get-tuple-element.37), channel_id=1, source_target_pairs={{0,4},{4,0},{8,12},{12,8},{16,20},{20,16},{24,28},{28,24},{1,5},{5... | collective-permute-start | bytes 196616 | tf_op jit(solution)/shard_map/ppermute | solution.py:43
  54.6 3.7 %collective-permute-start.16 = (f32[8,256]{1,0:T(8,128)S(1)}, f32[8,256]{1,0:T(8,128)S(1)}, u32[]{:S(2)}, u32[]{:S(2)}) collective-permute-start(f32[8,256]{1,0:T(8,128)S(1)} %get-tuple-element.40.square), channel_id=1, source_target_pairs={{0,1},{1,0},{2,3},{3,2},{4,5},{5,4},{6,7},{7,6},{8,9},{9,8},{10,11... | collective-permute-start | bytes 24584 | tf_op jit(solution)/shard_map/ppermute | solution.py:43

commit v5 on v4

--- a/solution.py
+++ b/solution.py
@@ -9,9 +9,10 @@
 
 
 KERNEL = 4
-UPPER = 8
+UPPER = 9
 RIM = 8
 ROWS = 8
+CHUNKS = 4
 PAD = 4
 F32, BF16 = jnp.float32, jnp.bfloat16
 EXACT = lax.Precision.HIGHEST
@@ -19,7 +20,7 @@
 HBM = pl.BlockSpec(memory_space=pltpu.HBM)
 
 
-def run(body, outs, *operands, scratch=(), flops=1000000, hbm=0, limit=4 << 20):
+def run(body, outs, *operands, scratch=(), flops=1000000, hbm=0, out=VMEM, limit=4 << 20):
     single = not isinstance(outs, list)
     shapes = [jax.ShapeDtypeStruct(*o) for o in ([outs] if single else outs)]
     operands = [
@@ -30,7 +31,7 @@
         body,
         out_shape=shapes,
         in_specs=[HBM] * hbm + [VMEM] * (len(operands) - hbm),
-        out_specs=[VMEM] * len(shapes),
+        out_specs=[out] * len(shapes),
         scratch_shapes=list(scratch),
         compiler_params=pltpu.CompilerParams(vmem_limit_bytes=limit),
         cost_estimate=pl.CostEstimate(flops=flops, bytes_accessed=flops // 400, transcendentals=0),
@@ -56,6 +57,11 @@
     return jnp.dot(a, b, preferred_element_type=F32, **kwargs)
 
 
+def two_parts(value):
+    high = value.astype(BF16)
+    return high, (value - high.astype(F32)).astype(BF16)
+
+
 def silu(v):
     return v / (1.0 + jnp.exp(-v))
 
@@ -68,7 +74,19 @@
     return lax.axis_index("ctx") % 2 == 0
 
 
-def fetched_halves(source, top, bottom, rim, arrivals):
+def whole_copies(sources, targets, arrivals, first):
+    copies = [
+        pltpu.make_async_copy(source, target, arrivals.at[first + i])
+        for i, (source, target) in enumerate(zip(sources, targets))
+    ]
+    for copy in copies:
+        copy.start()
+    return copies
+
+
+def fetched_halves(source, *refs):
+    count = (len(refs) - 4) // 2
+    small, (top, bottom, rim, *held, arrivals) = refs[:count], refs[count:]
     rows = source.shape[0]
     copies = [
         pltpu.make_async_copy(source.at[pl.ds(start, out.shape[0])], out, arrivals.at[i])
@@ -76,7 +94,7 @@
     ]
     for copy in copies:
         copy.start()
-    for copy in copies:
+    for copy in copies + whole_copies(small, held, arrivals, 3):
         copy.wait()
 
 
@@ -97,8 +115,11 @@
     return copies
 
 
-def last_weights(masks, w_bc, w_x, w_z, weights, arrivals):
-    for copy in weight_copies((w_bc, w_x, w_z), weights, arrivals, masks):
+def last_weights(masks, w_bc, w_x, w_z, *refs):
+    count = (len(refs) - 3) // 2
+    small, (weights, *held, arrivals, small_arrivals) = refs[:count], refs[count:]
+    copies = weight_copies((w_bc, w_x, w_z), weights, arrivals, masks)
+    for copy in copies + whole_copies(small, held, small_arrivals, 0):
         copy.wait()
 
 
@@ -179,18 +200,7 @@
     out[...] = silu(finished(masks, pieces, weights, before, before.shape[1] - width, width))
 
 
-def decays(*refs):
-    sources, refs = refs[:3], refs[3:]
-    segment, grown, end_weight, whole, skip_wide, *held, arrivals = refs
-    copies = [
-        pltpu.make_async_copy(source, there, arrivals.at[i])
-        for i, (source, there) in enumerate(zip(sources, held))
-    ]
-    for copy in copies:
-        copy.start()
-    for copy in copies:
-        copy.wait()
-    decay_t, step, skip = held
+def decays(decay_t, step, skip, segment, grown, end_weight, whole, skip_wide):
     heads, rows = decay_t.shape
     width = grown.shape[1]
     dim = width // heads
@@ -313,38 +323,61 @@
         out[:, columns] = dot(mixing, stacked) + skip_wide[:, columns] * wide
 
 
-def gated_output(own_bc, other_bc, keep, take, within, grown, gate, gated_out, square_out):
-    lead = first_core()
-    low = jnp.where(lead, keep[...], take[...])
-    high = jnp.where(lead, take[...], keep[...])
+def gated_half(c, state, start, within, grown, gate):
+    half = state.shape[1]
+    columns = pl.ds(start, half)
+    gated = (within[:, columns] + dot(c, state) * grown[:, columns]) * gate[:, columns]
+    squares = None
+    for lane in range(0, half, 128):
+        part = gated[:, lane : lane + 128]
+        squares = part * part if squares is None else squares + part * part
+    return gated, squares
+
+
+def half_starts(half):
+    core = lax.axis_index("ctx") % 2
+    return [pl.multiple_of(place * half, 128) for place in (core, 1 - core)]
+
+
+def gated_mine(own_bc, other_bc, keep, within, grown, gate, gated_out, squares_out):
     c = jnp.where(holds_b(), other_bc[...], own_bc[...])
-    half = low.shape[1]
-    squares = None
-    for s, entering in enumerate((low, high)):
-        columns = pl.ds(s * half, half)
-        inter = dot(c, entering) * grown[:, columns]
-        gated = (within[:, columns] + inter) * gate[:, columns]
-        gated_out[:, columns] = gated
-        for start in range(0, half, 128):
-            part = gated[:, start : start + 128]
-            squares = part * part if squares is None else squares + part * part
-    ones = jnp.ones((ROWS, squares.shape[1]), F32)
-    square_out[...] = lax.dot_general(
-        ones, squares, (((1,), (1,)), ((), ())), precision=EXACT, preferred_element_type=F32
-    )
-
-
-def normed_output(gated, square, other_square, gain, out):
-    width = gated.shape[1]
-    mean = (square[...] + other_square[...]) / (2 * width)
-    factor = lax.rsqrt(mean + 1e-05)
-    share = jnp.full((ROWS, 128), 1.0 / ROWS, F32)
-    column = lax.dot_general(
-        factor, share, (((0,), (0,)), ((), ())), precision=EXACT, preferred_element_type=F32
-    )
-    for start in range(0, width, 128):
-        columns = pl.ds(start, 128)
-        out[:, columns] = (gated[:, columns] * column * gain[:, columns]).astype(BF16)
+    mine, _ = half_starts(keep.shape[1])
+    gated_out[...], squares_out[...] = gated_half(c, keep[...], mine, within, grown, gate)
+
+
+def gated_other(own_bc, other_bc, take, within, grown, gate, squares, gated_out, square_out):
+    c = jnp.where(holds_b(), other_bc[...], own_bc[...])
+    _, other = half_starts(take.shape[1])
+    gated_out[...], more = gated_half(c, take[...], other, within, grown, gate)
+    ones = jnp.ones((ROWS, more.shape[1]), BF16)
+    square_out[...] = sum(
+        lax.dot_general(ones, part, (((1,), (1,)), ((), ())), preferred_element_type=F32)
+        for part in two_parts(squares[...] + more)
+    )
+
+
+def normed_output(mine, other, square, other_square, gain, out, held, sent):
+    rows, half = mine.shape
+    mean = (square[...] + other_square[...]) / (4 * half)
+    share = jnp.full((ROWS, 128), 1.0 / ROWS, BF16)
+    factor = sum(
+        lax.dot_general(part, share, (((0,), (0,)), ((), ())), preferred_element_type=F32)
+        for part in two_parts(lax.rsqrt(mean + 1e-05))
+    )
+    copies = []
+    count = rows // CHUNKS
+    for chunk in range(CHUNKS):
+        some = pl.ds(chunk * count, count)
+        column = factor[chunk * count : (chunk + 1) * count]
+        for gated, start in zip((mine, other), half_starts(half)):
+            for lane in range(0, half, 128):
+                columns = pl.ds(pl.multiple_of(start + lane, 128), 128)
+                wide = gated[some, pl.ds(lane, 128)] * column * gain[:, columns]
+                held[some, columns] = wide.astype(BF16)
+        copies.append(pltpu.make_async_copy(held.at[some], out.at[some], sent.at[chunk]))
+        copies[-1].start()
+    for copy in copies:
+        copy.wait()
 
 
 def gather_pieces(top, bottom, axis):
@@ -383,12 +416,18 @@
     chips = lax.axis_size("ctx") // 2
 
     upper = rows * UPPER // 16
-    top, bottom, rim = run(
+    small = (decay_logarithm.T, head_step.reshape(1, -1), skip.reshape(1, -1))
+    top, bottom, rim, *small = run(
         fetched_halves,
-        [((upper, depth), BF16), ((rows - upper, depth), BF16), ((RIM, depth), BF16)],
-        tokens,
-        scratch=[pltpu.SemaphoreType.DMA((3,))],
-        hbm=1,
+        [
+            ((upper, depth), BF16),
+            ((rows - upper, depth), BF16),
+            ((RIM, depth), BF16),
+            *[(a.shape, F32) for a in small],
+        ],
+        tokens, *small,
+        scratch=[pltpu.SemaphoreType.DMA((3 + len(small),))],
+        hbm=1 + len(small),
     )
 
     def flops(*sizes):
@@ -410,12 +449,16 @@
         hbm=3,
     )
     masks = tuple(sorted(last))
-    weights_end = run(
+    vectors = (conv_bc, bias_bc.reshape(1, -1), conv_x, bias_x.reshape(1, -1), gain.reshape(1, -1))
+    weights_end, conv_bc, bias_bc, conv_x, bias_x, gain = run(
         functools.partial(last_weights, masks),
-        ((len(masks), depth, everything), BF16),
-        w_bc, w_x, w_z,
-        scratch=[pltpu.SemaphoreType.DMA((len(masks), 3))],
-        hbm=3,
+        [((len(masks), depth, everything), BF16), *[(v.shape, F32) for v in vectors]],
+        w_bc, w_x, w_z, *vectors,
+        scratch=[
+            pltpu.SemaphoreType.DMA((len(masks), 3)),
+            pltpu.SemaphoreType.DMA((len(vectors),)),
+        ],
+        hbm=3 + len(vectors),
     )
     segment, grown, end_weight, whole, skip_wide = run(
         decays,
@@ -426,14 +469,7 @@
             ((ROWS, width), F32),
             ((1, width), F32),
         ],
-        decay_logarithm.T, head_step.reshape(1, -1), skip.reshape(1, -1),
-        scratch=[
-            pltpu.VMEM((heads, rows), F32),
-            pltpu.VMEM((1, heads), F32),
-            pltpu.VMEM((1, heads), F32),
-            pltpu.SemaphoreType.DMA((3,)),
-        ],
-        hbm=3,
+        *small,
         flops=flops(rows, rows, width),
     )
     masks = tuple(sorted(early))
@@ -455,7 +491,7 @@
     own_bc = run(
         functools.partial(last_bc, masks),
         ((rows, bc_width), BF16),
-        *ends, weights_end, sums, rim_sums, conv_bc, bias_bc.reshape(1, -1),
+        *ends, weights_end, sums, rim_sums, conv_bc, bias_bc,
         scratch=[pltpu.VMEM((rows + RIM, bc_width), F32)],
         flops=flops(rows, depth, bc_width),
     )
@@ -463,7 +499,7 @@
     x, weighted = run(
         functools.partial(last_x, masks),
         [((rows, width), BF16), ((rows, width), BF16)],
-        *ends, weights_end, sums, rim_sums, conv_x, bias_x.reshape(1, -1), end_weight,
+        *ends, weights_end, sums, rim_sums, conv_x, bias_x, end_weight,
         scratch=[pltpu.VMEM((rows + RIM, width), F32)],
         flops=flops(rows, depth, width),
     )
@@ -496,15 +532,26 @@
         entering_state, [(state_shape, BF16), (state_shape, BF16)], kept, whole, received, *got, within, gate
     )
     take = partner(give, "ctx", 1)
-    gated, square = run(
-        gated_output,
-        [((rows, width), F32), ((ROWS, rows), F32)],
-        own_bc, other_bc, keep, take, within, grown, gate,
-        flops=flops(rows, n, width),
+    half = width // 2
+    mine, squares = run(
+        gated_mine,
+        [((rows, half), F32), ((rows, 128), F32)],
+        own_bc, other_bc, keep, within, grown, gate,
+        flops=flops(rows, n, half),
+    )
+    other, square = run(
+        gated_other,
+        [((rows, half), F32), ((ROWS, rows), F32)],
+        own_bc, other_bc, take, within, grown, gate, squares,
+        flops=flops(rows, n, half),
     )
     other_square = partner(square, "tp", 1)
     return run(
-        normed_output, ((rows, width), BF16), gated, square, other_square, gain.reshape(1, -1)
+        normed_output,
+        ((rows, width), BF16),
+        mine, other, square, other_square, gain,
+        scratch=[pltpu.VMEM((rows, width), BF16), pltpu.SemaphoreType.DMA((CHUNKS,))],
+        out=HBM,
     )
 
 

time: 59.5 us -> 60 us (level)
  waiting for transfers between devices: 27.3 us -> 29.6 us
  starting transfers between devices: 17.2 us -> 16.1 us
    ppermute x16, waiting for transfers between devices: 22.3 us -> 26.2 us  [partner(): lax.ppermute(value, axis, [(i, i ^ mask) for i in range(lax.axis_size(axi...]
    ppermute x1, waiting for transfers between devices: 4.96 us -> 3.43 us  [onward(): return lax.ppermute(value, axis, [(i, (i + 1) % size) for i in range(size)])]
    ppermute x16, starting transfers between devices: 17.2 us -> 16.1 us  [partner(): lax.ppermute(value, axis, [(i, i ^ mask) for i in range(lax.axis_size(axi...]
    pallas_call x15 -> x16, Pallas kernels: 14.6 us -> 14 us  [run(): results = call(*operands)]
  transfers between devices with their start and end apart: 17 -> 17, of which waited for: 10 -> 10; matrix products, arithmetic and copies ran while one was open for 0% -> 0% of each run, Pallas kernels for 19% -> 18%
where the time goes in v5:
time: 60 us; the launch traced here: 59.9 us
  waiting for transfers between devices  29.6 us (49%)
  starting transfers between devices  16.1 us (27%)
  Pallas kernels  14 us (23%)
    ppermute x16, waiting for transfers between devices, partner(): lax.ppermute(value, axis, [(i, i ^ mask) for i in range(lax.axis_size(axi...  26.2 us
    ppermute x16, starting transfers between devices, partner(): lax.ppermute(value, axis, [(i, i ^ mask) for i in range(lax.axis_size(axi...  16.1 us
    pallas_call x16, Pallas kernels, run(): results = call(*operands)  14 us
    ppermute x1, waiting for transfers between devices, onward(): return lax.ppermute(value, axis, [(i, (i + 1) % size) for i in range(size)])  3.43 us
  transfers between devices with their start and end apart: 17, of which 10 were waited for; matrix products, arithmetic and copies ran while one was open for 0% of the time, Pallas kernels for 18%

profile of v5, /device:TPU:0, one launch (start us, length us, event | category | flops | bytes accessed | tf_op | source)
XLA Modules:
  0.0 59.9 jit_solution(7246423612109714914)
XLA Ops:
  0.0 1.1 %shard_map.118 = (bf16[144,1024]{1,0:T(8,128)(2,1)S(1)}, bf16[112,1024]{1,0:T(8,128)(2,1)S(1)}, bf16[8,1024]{1,0:T(8,128)(2,1)S(1)}, f32[8,256]{1,0:T(8,128)S(1)...) custom-call(bf16[256,1024]{1,0:T(8,128)(2,1)} %source.1, f32[8,256]{1,0:T(8,128)} %bitcast.6, f32[1,8]{1,0:T(1,128)} %bitcast.10, ...), custom_call_target="tpu_custom_call" | custom-call | flops 1000000 | bytes 2500 | tf_op jit(solution)/shard_map/pallas_call | solution.py:39
  1.1 3.1 %collective-permute-start = (bf16[144,1024]{1,0:T(8,128)(2,1)S(1)}, bf16[144,1024]{1,0:T(8,128)(2,1)S(1)}, u32[]{:S(2)}, u32[]{:S(2)}) collective-permute-start(bf16[144,1024]{1,0:T(8,128)(2,1)S(1)} %get-tuple-element.34.top), channel_id=1, source_target_pairs={{0,2},{1,3},{2,0},{3,1},{4,6},{5,7},{6,4},{7,5},{8,10},{9,11},{10,... | collective-permute-start | bytes 884744 | tf_op jit(solution)/shard_map/ppermute | solution.py:44
  4.2 1.5 %collective-permute-start.2 = (bf16[112,1024]{1,0:T(8,128)(2,1)S(1)}, bf16[112,1024]{1,0:T(8,128)(2,1)S(1)}, u32[]{:S(2)}, u32[]{:S(2)}) collective-permute-start(bf16[112,1024]{1,0:T(8,128)(2,1)S(1)} %get-tuple-element.35.bottom), channel_id=1, source_target_pairs={{0,1},{1,0},{2,3},{3,2},{4,5},{5,4},{6,7},{7,6},{8,9},{9,8},{10,11... | collective-permute-start | bytes 688136 | tf_op jit(solution)/shard_map/ppermute | solution.py:44
  5.7 0.5 collective-permute-start.4
  6.2 0.1 collective-permute-start.5
  6.3 5.8 %collective-permute-done.refs_2_ = bf16[144,1024]{1,0:T(8,128)(2,1)S(1)} collective-permute-done((bf16[144,1024]{1,0:T(8,128)(2,1)S(1)}, bf16[144,1024]{1,0:T(8,128)(2,1)S(1)}, u32[]{:S(2)}, u32[]{:S(2)}) %collective-permute-start) | collective-permute-done | bytes 294944 | tf_op jit(solution)/shard_map/ppermute | solution.py:44
  12.1 2.0 %collective-permute-start.1 = (bf16[144,1024]{1,0:T(8,128)(2,1)S(1)}, bf16[144,1024]{1,0:T(8,128)(2,1)S(1)}, u32[]{:S(2)}, u32[]{:S(2)}) collective-permute-start(bf16[144,1024]{1,0:T(8,128)(2,1)S(1)} %collective-permute-done.refs_2_), channel_id=1, source_target_pairs={{0,1},{1,0},{2,3},{3,2},{4,5},{5,4},{6,7},{7,6},{8,9},{9,8},{10,11... | collective-permute-start | bytes 884744 | tf_op jit(solution)/shard_map/ppermute | solution.py:44
  14.1 0.0 collective-permute-start.6
  14.1 0.0 collective-permute-done.2.refs_1_
  14.1 1.5 %collective-permute-start.3 = (bf16[112,1024]{1,0:T(8,128)(2,1)S(1)}, bf16[112,1024]{1,0:T(8,128)(2,1)S(1)}, u32[]{:S(2)}, u32[]{:S(2)}) collective-permute-start(bf16[112,1024]{1,0:T(8,128)(2,1)S(1)} %collective-permute-done.2.refs_1_), channel_id=1, source_target_pairs={{0,2},{1,3},{2,0},{3,1},{4,6},{5,7},{6,4},{7,5},{8,10},{9,11},{10,... | collective-permute-start | bytes 688136 | tf_op jit(solution)/shard_map/ppermute | solution.py:44
  15.6 3.4 %collective-permute-done.6.refs_0_ = bf16[8,1024]{1,0:T(8,128)(2,1)S(1)} collective-permute-done((bf16[8,1024]{1,0:T(8,128)(2,1)S(1)}, bf16[8,1024]{1,0:T(8,128)(2,1)S(1)}, u32[]{:S(2)}, u32[]{:S(2)}) %collective-permute-start.6) | collective-permute-done | bytes 16416 | tf_op jit(solution)/shard_map/ppermute | solution.py:53
  19.0 0.0 collective-permute-start.7
  19.1 5.2 %collective-permute-done.7.refs_1_ = bf16[8,1024]{1,0:T(8,128)(2,1)S(1)} collective-permute-done((bf16[8,1024]{1,0:T(8,128)(2,1)S(1)}, bf16[8,1024]{1,0:T(8,128)(2,1)S(1)}, u32[]{:S(2)}, u32[]{:S(2)}) %collective-permute-start.7) | collective-permute-done | bytes 16416 | tf_op jit(solution)/shard_map/ppermute | solution.py:44
  24.3 0.4 collective-permute-start.8
  24.6 3.4 %collective-permute-done.8.refs_2_ = bf16[8,1024]{1,0:T(8,128)(2,1)S(1)} collective-permute-done((bf16[8,1024]{1,0:T(8,128)(2,1)S(1)}, bf16[8,1024]{1,0:T(8,128)(2,1)S(1)}, u32[]{:S(2)}, u32[]{:S(2)}) %collective-permute-start.8) | collective-permute-done | bytes 16416 | tf_op jit(solution)/shard_map/ppermute | solution.py:44
  28.0 1.4 %collective-permute-start.9 = (bf16[8,1024]{1,0:T(8,128)(2,1)S(1)}, bf16[8,1024]{1,0:T(8,128)(2,1)S(1)}, u32[]{:S(2)}, u32[]{:S(2)}) collective-permute-start(bf16[8,1024]{1,0:T(8,128)(2,1)S(1)} %collective-permute-done.6.refs_0_), channel_id=1, source_target_pairs={{0,3},{1,2},{2,1},{3,0},{4,7},{5,6},{6,5},{7,4},{8,11},{9,10},{10,... | collective-permute-start | bytes 49160 | tf_op jit(solution)/shard_map/ppermute | solution.py:44
  29.4 3.1 %shard_map.120 = (f32[256,1152]{1,0:T(8,128)S(1)}, bf16[3,1024,1152]{2,1,0:T(8,128)(2,1)S(1)}) custom-call(bf16[4096,128]{1,0:T(8,128)(2,1)} %w_bc.3, bf16[4096,512]{1,0:T(8,128)(2,1)} %w_x.3, bf16[4096,512]{1,0:T(8,128)(2,1)} %w_z.3, bf16[144,1024]{1,0:T(8,128)(2,1)S(1)} %get-tuple-element.34.top, bf16[112,1024]{1,0:T(8,128)(2,1)S(1)} %get-tuple-element.35.bottom), custom_call_target="tpu_custom_call" | custom-call | flops 603979776 | bytes 1509949 | tf_op jit(solution)/shard_map/pallas_call | solution.py:39
  32.6 1.8 %shard_map.119 = (bf16[1,1024,1152]{2,1,0:T(8,128)(2,1)S(1)}, f32[4,128]{1,0:T(4,128)S(1)}, f32[1,128]{1,0:T(1,128)S(1)}, f32[4,512]{1,0:T(4,128)S(1)}, f32[1,512]{1,0:T(1,128)S(1)}, /*index=5*/f32[1,512]{1,0:T(1,128)S(1)}) custom-call(bf16[4096,128]{1,0:T(8,128)(2,1)} %w_bc.3, bf16[4096,512]{1,0:T(8,128)(2,1)} %w_x.3, bf16[4096,512]{1,0:T(8,128)(2,1)} %w_z.3, ...), custom_call_target="tpu_custom_call" | custom-call | flops 1000000 | bytes 2500 | tf_op jit(solution)/shard_map/pallas_call | solution.py:39
  34.3 0.0 collective-permute-done.9.refs_3_
  34.4 0.8 %shard_map.122.refs_4_ = f32[8,640]{1,0:T(8,128)S(1)} custom-call(bf16[8,1024]{1,0:T(8,128)(2,1)S(1)} %collective-permute-done.6.refs_0_, bf16[8,1024]{1,0:T(8,128)(2,1)S(1)} %collective-permute-done.7.refs_1_, bf16[8,1024]{1,0:T(8,128)(2,1)S(1)} %collective-permute-done.8.refs_2_, bf16[8,1024]{1,0:T(8,128)(2,1)S(1)} %collective-permute-done.9.refs_3_, ...), custom_call_target="tpu_custom_call" | custom-call | flops 268435456 | bytes 671088 | tf_op jit(solution)/shard_map/pallas_call | solution.py:39
  35.1 0.0 collective-permute-done.5.refs_3_
  35.1 0.0 collective-permute-done.4.refs_0_
  35.2 1.5 %shard_map.121.refs_3_ = f32[256,1152]{1,0:T(8,128)S(1)} custom-call(bf16[144,1024]{1,0:T(8,128)(2,1)S(1)} %collective-permute-done.4.refs_0_, bf16[112,1024]{1,0:T(8,128)(2,1)S(1)} %collective-permute-done.2.refs_1_, bf16[144,1024]{1,0:T(8,128)(2,1)S(1)} %collective-permute-done.refs_2_, bf16[112,1024]{1,0:T(8,128)(2,1)S(1)} %collective-permute-done.5.refs_3_, ...), custom_call_target="tpu_custom_call" | custom-call | flops 1207959552 | bytes 3019898 | tf_op jit(solution)/shard_map/pallas_call | solution.py:39
  36.7 0.0 collective-permute-done.3.refs_1_
  36.7 0.0 collective-permute-done.1.refs_0_
  36.7 0.4 shard_map.123.own_bc
  37.1 0.4 collective-permute-start.10
  37.5 1.1 %shard_map.124 = (bf16[8,256,256]{2,1,0:T(8,128)(2,1)S(1)}, f32[256,512]{1,0:T(8,128)S(1)}, f32[256,512]{1,0:T(8,128)S(1)}, f32[8,512]{1,0:T(8,128)S(1)}, f32[1,512]{1,0:T(1,128)S(1)}) custom-call(f32[8,256]{1,0:T(8,128)S(1)} %get-tuple-element.44.decay_t, f32[1,8]{1,0:T(1,128)S(1)} %get-tuple-element.45.step, f32[1,8]{1,0:T(1,128)S(1)} %get-tuple-element.46.skip), custom_call_target="tpu_custom_call" | custom-call | flops 67108864 | bytes 167772 | tf_op jit(solution)/shard_map/pallas_call | solution.py:39
  38.7 1.1 %shard_map.125 = (bf16[256,512]{1,0:T(8,128)(2,1)S(1)}, bf16[256,512]{1,0:T(8,128)(2,1)S(1)}) custom-call(bf16[144,1024]{1,0:T(8,128)(2,1)S(1)} %collective-permute-done.1.refs_0_, bf16[112,1024]{1,0:T(8,128)(2,1)S(1)} %collective-permute-done.3.refs_1_, bf16[1,1024,1152]{2,1,0:T(8,128)(2,1)S(1)} %get-tuple-element.36.refs_5_.refs_2_, ...), custom_call_target="tpu_custom_call" | custom-call | flops 268435456 | bytes 671088 | tf_op jit(solution)/shard_map/pallas_call | solution.py:39
  39.8 1.7 %collective-permute-done.10.other_bc = bf16[256,128]{1,0:T(8,128)(2,1)S(1)} collective-permute-done((bf16[256,128]{1,0:T(8,128)(2,1)S(1)}, bf16[256,128]{1,0:T(8,128)(2,1)S(1)}, u32[]{:S(2)}, u32[]{:S(2)}) %collective-permute-start.10) | collective-permute-done | bytes 65568 | tf_op jit(solution)/shard_map/ppermute | solution.py:44
  41.4 0.2 shard_map.126
  41.7 0.1 collective-permute-start.11
  41.7 1.2 %collective-permute-done.11.received = bf16[136,256]{1,0:T(8,128)(2,1)S(1)} collective-permute-done((bf16[136,256]{1,0:T(8,128)(2,1)S(1)}, bf16[136,256]{1,0:T(8,128)(2,1)S(1)}, u32[]{:S(2)}, u32[]{:S(2)}) %collective-permute-start.11) | collective-permute-done | bytes 69664 | tf_op jit(solution)/shard_map/ppermute | solution.py:44
  43.0 1.6 %collective-permute-start.12 = (bf16[136,256]{1,0:T(8,128)(2,1)S(1)}, bf16[136,256]{1,0:T(8,128)(2,1)S(1)}, u32[]{:S(2)}, u32[]{:S(2)}) collective-permute-start(bf16[136,256]{1,0:T(8,128)(2,1)S(1)} %shard_map.127._.refs_4_), channel_id=1, source_target_pairs={{0,8},{4,12},{8,0},{12,4},{16,24},{20,28},{24,16},{28,20},{1,9},{5... | collective-permute-start | bytes 208904 | tf_op jit(solution)/shard_map/ppermute | solution.py:44
  44.7 2.6 %collective-permute-start.13 = (bf16[136,256]{1,0:T(8,128)(2,1)S(1)}, bf16[136,256]{1,0:T(8,128)(2,1)S(1)}, u32[]{:S(2)}, u32[]{:S(2)}) collective-permute-start(bf16[136,256]{1,0:T(8,128)(2,1)S(1)} %shard_map.127._.refs_4_), channel_id=1, source_target_pairs={{0,16},{4,20},{8,24},{12,28},{16,0},{20,4},{24,8},{28,12},{1,17},{... | collective-permute-start | bytes 208904 | tf_op jit(solution)/shard_map/ppermute | solution.py:44
  47.3 0.2 collective-permute-start.14
  47.5 0.7 %shard_map.128.refs_3_.within = f32[256,512]{1,0:T(8,128)S(1)} custom-call(bf16[256,128]{1,0:T(8,128)(2,1)S(1)} %shard_map.123.own_bc, bf16[256,128]{1,0:T(8,128)(2,1)S(1)} %collective-permute-done.10.other_bc, bf16[256,512]{1,0:T(8,128)(2,1)S(1)} %get-tuple-element.52.x, bf16[8,256,256]{2,1,0:T(8,128)(2,1)S(1)} %get-tuple-element.53.segment, ...), custom_call_target="tpu_custom_call" | custom-call | flops 201326592 | bytes 503316 | tf_op jit(solution)/shard_map/pallas_call | solution.py:39
  48.1 0.5 shard_map.129.refs_4_.gate
  48.7 0.0 collective-permute-done.12.refs_0_
  48.7 3.8 %collective-permute-done.13.refs_1_ = bf16[136,256]{1,0:T(8,128)(2,1)S(1)} collective-permute-done((bf16[136,256]{1,0:T(8,128)(2,1)S(1)}, bf16[136,256]{1,0:T(8,128)(2,1)S(1)}, u32[]{:S(2)}, u32[]{:S(2)}) %collective-permute-start.13) | collective-permute-done | bytes 69664 | tf_op jit(solution)/shard_map/ppermute | solution.py:44
  52.5 1.0 %collective-permute-done.14.refs_2_ = bf16[136,256]{1,0:T(8,128)(2,1)S(1)} collective-permute-done((bf16[136,256]{1,0:T(8,128)(2,1)S(1)}, bf16[136,256]{1,0:T(8,128)(2,1)S(1)}, u32[]{:S(2)}, u32[]{:S(2)}) %collective-permute-start.14) | collective-permute-done | bytes 69664 | tf_op jit(solution)/shard_map/ppermute | solution.py:44
  53.5 0.1 shard_map.130
  53.6 0.1 collective-permute-start.15
  53.6 0.2 shard_map.131
  53.8 1.0 %collective-permute-done.15.take = bf16[128,256]{1,0:T(8,128)(2,1)S(1)} collective-permute-done((bf16[128,256]{1,0:T(8,128)(2,1)S(1)}, bf16[128,256]{1,0:T(8,128)(2,1)S(1)}, u32[]{:S(2)}, u32[]{:S(2)}) %collective-permute-start.15) | collective-permute-done | bytes 65568 | tf_op jit(solution)/shard_map/ppermute | solution.py:44
  54.9 0.3 shard_map.132
  55.2 0.6 collective-permute-start.16
  55.8 3.1 %collective-permute-done.16.other_square = f32[8,256]{1,0:T(8,128)S(1)} collective-permute-done((f32[8,256]{1,0:T(8,128)S(1)}, f32[8,256]{1,0:T(8,128)S(1)}, u32[]{:S(2)}, u32[]{:S(2)}) %collective-permute-start.16) | collective-permute-done | bytes 8224 | tf_op jit(solution)/shard_map/ppermute | solution.py:44
  58.9 1.0 %shard_map.133 = bf16[256,512]{1,0:T(8,128)(2,1)} custom-call(f32[256,256]{1,0:T(8,128)S(1)} %get-tuple-element.57.mine, f32[256,256]{1,0:T(8,128)S(1)} %get-tuple-element.60.other, f32[8,256]{1,0:T(8,128)S(1)} %get-tuple-element.61.square, f32[8,256]{1,0:T(8,128)S(1)} %collective-permute-done.16.other_square, f32[1,512]{1,0:T(1,128)S(1)} %get-tuple-element.62.gain), custom_call_target="tpu_custom_call" | custom-call | flops 1000000 | bytes 2500 | tf_op jit(solution)/shard_map/pallas_call | solution.py:39
  (1 shorter events, 0.0 us)
Async XLA Ops:
  1.1 10.9 %collective-permute-start = (bf16[144,1024]{1,0:T(8,128)(2,1)S(1)}, bf16[144,1024]{1,0:T(8,128)(2,1)S(1)}, u32[]{:S(2)}, u32[]{:S(2)}) collective-permute-start(bf16[144,1024]{1,0:T(8,128)(2,1)S(1)} %get-tuple-element.34.top), channel_id=1, source_target_pairs={{0,2},{1,3},{2,0},{3,1},{4,6},{5,7},{6,4},{7,5},{8,10},{9,11},{10,... | collective-permute-start | bytes 884744 | tf_op jit(solution)/shard_map/ppermute | solution.py:44
  4.2 9.9 %collective-permute-start.2 = (bf16[112,1024]{1,0:T(8,128)(2,1)S(1)}, bf16[112,1024]{1,0:T(8,128)(2,1)S(1)}, u32[]{:S(2)}, u32[]{:S(2)}) collective-permute-start(bf16[112,1024]{1,0:T(8,128)(2,1)S(1)} %get-tuple-element.35.bottom), channel_id=1, source_target_pairs={{0,1},{1,0},{2,3},{3,2},{4,5},{5,4},{6,7},{7,6},{8,9},{9,8},{10,11... | collective-permute-start | bytes 688136 | tf_op jit(solution)/shard_map/ppermute | solution.py:44
  5.7 29.5 %collective-permute-start.4 = (bf16[144,1024]{1,0:T(8,128)(2,1)S(1)}, bf16[144,1024]{1,0:T(8,128)(2,1)S(1)}, u32[]{:S(2)}, u32[]{:S(2)}) collective-permute-start(bf16[144,1024]{1,0:T(8,128)(2,1)S(1)} %get-tuple-element.34.top), channel_id=1, source_target_pairs={{0,1},{1,0},{2,3},{3,2},{4,5},{5,4},{6,7},{7,6},{8,9},{9,8},{10,11... | collective-permute-start | bytes 884744 | tf_op jit(solution)/shard_map/ppermute | solution.py:44
  6.2 28.9 %collective-permute-start.5 = (bf16[112,1024]{1,0:T(8,128)(2,1)S(1)}, bf16[112,1024]{1,0:T(8,128)(2,1)S(1)}, u32[]{:S(2)}, u32[]{:S(2)}) collective-permute-start(bf16[112,1024]{1,0:T(8,128)(2,1)S(1)} %get-tuple-element.35.bottom), channel_id=1, source_target_pairs={{0,2},{1,3},{2,0},{3,1},{4,6},{5,7},{6,4},{7,5},{8,10},{9,11},{10,... | collective-permute-start | bytes 688136 | tf_op jit(solution)/shard_map/ppermute | solution.py:44
  12.1 24.6 %collective-permute-start.1 = (bf16[144,1024]{1,0:T(8,128)(2,1)S(1)}, bf16[144,1024]{1,0:T(8,128)(2,1)S(1)}, u32[]{:S(2)}, u32[]{:S(2)}) collective-permute-start(bf16[144,1024]{1,0:T(8,128)(2,1)S(1)} %collective-permute-done.refs_2_), channel_id=1, source_target_pairs={{0,1},{1,0},{2,3},{3,2},{4,5},{5,4},{6,7},{7,6},{8,9},{9,8},{10,11... | collective-permute-start | bytes 884744 | tf_op jit(solution)/shard_map/ppermute | solution.py:44
  14.1 5.0 %collective-permute-start.6 = (bf16[8,1024]{1,0:T(8,128)(2,1)S(1)}, bf16[8,1024]{1,0:T(8,128)(2,1)S(1)}, u32[]{:S(2)}, u32[]{:S(2)}) collective-permute-start(bf16[8,1024]{1,0:T(8,128)(2,1)S(1)} %get-tuple-element.39), channel_id=1, source_target_pairs={{0,4},{4,8},{8,12},{12,16},{16,20},{20,24},{24,28},{28,0},{1,5},{5... | collective-permute-start | bytes 49160 | tf_op jit(solution)/shard_map/ppermute | solution.py:53
  14.1 22.6 %collective-permute-start.3 = (bf16[112,1024]{1,0:T(8,128)(2,1)S(1)}, bf16[112,1024]{1,0:T(8,128)(2,1)S(1)}, u32[]{:S(2)}, u32[]{:S(2)}) collective-permute-start(bf16[112,1024]{1,0:T(8,128)(2,1)S(1)} %collective-permute-done.2.refs_1_), channel_id=1, source_target_pairs={{0,2},{1,3},{2,0},{3,1},{4,6},{5,7},{6,4},{7,5},{8,10},{9,11},{10,... | collective-permute-start | bytes 688136 | tf_op jit(solution)/shard_map/ppermute | solution.py:44
  19.0 5.2 %collective-permute-start.7 = (bf16[8,1024]{1,0:T(8,128)(2,1)S(1)}, bf16[8,1024]{1,0:T(8,128)(2,1)S(1)}, u32[]{:S(2)}, u32[]{:S(2)}) collective-permute-start(bf16[8,1024]{1,0:T(8,128)(2,1)S(1)} %collective-permute-done.6.refs_0_), channel_id=1, source_target_pairs={{0,1},{1,0},{2,3},{3,2},{4,5},{5,4},{6,7},{7,6},{8,9},{9,8},{10,11... | collective-permute-start | bytes 49160 | tf_op jit(solution)/shard_map/ppermute | solution.py:44
  24.3 3.7 %collective-permute-start.8 = (bf16[8,1024]{1,0:T(8,128)(2,1)S(1)}, bf16[8,1024]{1,0:T(8,128)(2,1)S(1)}, u32[]{:S(2)}, u32[]{:S(2)}) collective-permute-start(bf16[8,1024]{1,0:T(8,128)(2,1)S(1)} %collective-permute-done.6.refs_0_), channel_id=1, source_target_pairs={{0,2},{1,3},{2,0},{3,1},{4,6},{5,7},{6,4},{7,5},{8,10},{9,11},{10,... | collective-permute-start | bytes 49160 | tf_op jit(solution)/shard_map/ppermute | solution.py:44
  28.0 6.3 %collective-permute-start.9 = (bf16[8,1024]{1,0:T(8,128)(2,1)S(1)}, bf16[8,1024]{1,0:T(8,128)(2,1)S(1)}, u32[]{:S(2)}, u32[]{:S(2)}) collective-permute-start(bf16[8,1024]{1,0:T(8,128)(2,1)S(1)} %collective-permute-done.6.refs_0_), channel_id=1, source_target_pairs={{0,3},{1,2},{2,1},{3,0},{4,7},{5,6},{6,5},{7,4},{8,11},{9,10},{10,... | collective-permute-start | bytes 49160 | tf_op jit(solution)/shard_map/ppermute | solution.py:44
  37.1 4.3 %collective-permute-start.10 = (bf16[256,128]{1,0:T(8,128)(2,1)S(1)}, bf16[256,128]{1,0:T(8,128)(2,1)S(1)}, u32[]{:S(2)}, u32[]{:S(2)}) collective-permute-start(bf16[256,128]{1,0:T(8,128)(2,1)S(1)} %shard_map.123.own_bc), channel_id=1, source_target_pairs={{0,1},{1,0},{2,3},{3,2},{4,5},{5,4},{6,7},{7,6},{8,9},{9,8},{10,11... | collective-permute-start | bytes 196616 | tf_op jit(solution)/shard_map/ppermute | solution.py:44
  41.7 1.3 %collective-permute-start.11 = (bf16[136,256]{1,0:T(8,128)(2,1)S(1)}, bf16[136,256]{1,0:T(8,128)(2,1)S(1)}, u32[]{:S(2)}, u32[]{:S(2)}) collective-permute-start(bf16[136,256]{1,0:T(8,128)(2,1)S(1)} %get-tuple-element.51), channel_id=1, source_target_pairs={{0,4},{4,0},{8,12},{12,8},{16,20},{20,16},{24,28},{28,24},{1,5},{5... | collective-permute-start | bytes 208904 | tf_op jit(solution)/shard_map/ppermute | solution.py:44
  43.0 5.7 %collective-permute-start.12 = (bf16[136,256]{1,0:T(8,128)(2,1)S(1)}, bf16[136,256]{1,0:T(8,128)(2,1)S(1)}, u32[]{:S(2)}, u32[]{:S(2)}) collective-permute-start(bf16[136,256]{1,0:T(8,128)(2,1)S(1)} %shard_map.127._.refs_4_), channel_id=1, source_target_pairs={{0,8},{4,12},{8,0},{12,4},{16,24},{20,28},{24,16},{28,20},{1,9},{5... | collective-permute-start | bytes 208904 | tf_op jit(solution)/shard_map/ppermute | solution.py:44
  44.7 7.8 %collective-permute-start.13 = (bf16[136,256]{1,0:T(8,128)(2,1)S(1)}, bf16[136,256]{1,0:T(8,128)(2,1)S(1)}, u32[]{:S(2)}, u32[]{:S(2)}) collective-permute-start(bf16[136,256]{1,0:T(8,128)(2,1)S(1)} %shard_map.127._.refs_4_), channel_id=1, source_target_pairs={{0,16},{4,20},{8,24},{12,28},{16,0},{20,4},{24,8},{28,12},{1,17},{... | collective-permute-start | bytes 208904 | tf_op jit(solution)/shard_map/ppermute | solution.py:44
  47.3 6.2 %collective-permute-start.14 = (bf16[136,256]{1,0:T(8,128)(2,1)S(1)}, bf16[136,256]{1,0:T(8,128)(2,1)S(1)}, u32[]{:S(2)}, u32[]{:S(2)}) collective-permute-start(bf16[136,256]{1,0:T(8,128)(2,1)S(1)} %shard_map.127._.refs_4_), channel_id=1, source_target_pairs={{0,24},{4,28},{8,16},{12,20},{16,8},{20,12},{24,0},{28,4},{1,25},{... | collective-permute-start | bytes 208904 | tf_op jit(solution)/shard_map/ppermute | solution.py:44
  53.6 1.3 %collective-permute-start.15 = (bf16[128,256]{1,0:T(8,128)(2,1)S(1)}, bf16[128,256]{1,0:T(8,128)(2,1)S(1)}, u32[]{:S(2)}, u32[]{:S(2)}) collective-permute-start(bf16[128,256]{1,0:T(8,128)(2,1)S(1)} %get-tuple-element.58), channel_id=1, source_target_pairs={{0,4},{4,0},{8,12},{12,8},{16,20},{20,16},{24,28},{28,24},{1,5},{5... | collective-permute-start | bytes 196616 | tf_op jit(solution)/shard_map/ppermute | solution.py:44
  55.2 3.7 %collective-permute-start.16 = (f32[8,256]{1,0:T(8,128)S(1)}, f32[8,256]{1,0:T(8,128)S(1)}, u32[]{:S(2)}, u32[]{:S(2)}) collective-permute-start(f32[8,256]{1,0:T(8,128)S(1)} %get-tuple-element.61.square), channel_id=1, source_target_pairs={{0,1},{1,0},{2,3},{3,2},{4,5},{5,4},{6,7},{7,6},{8,9},{9,8},{10,11... | collective-permute-start | bytes 24584 | tf_op jit(solution)/shard_map/ppermute | solution.py:44

commit v6 on v5

--- a/solution.py
+++ b/solution.py
@@ -13,7 +13,7 @@
 RIM = 8
 ROWS = 8
 CHUNKS = 4
-PAD = 4
+TAIL = 8
 F32, BF16 = jnp.float32, jnp.bfloat16
 EXACT = lax.Precision.HIGHEST
 VMEM = pl.BlockSpec(memory_space=pltpu.VMEM)
@@ -84,18 +84,19 @@
     return copies
 
 
-def fetched_halves(source, *refs):
-    count = (len(refs) - 4) // 2
-    small, (top, bottom, rim, *held, arrivals) = refs[:count], refs[count:]
+def fetched_halves(source, top, bottom, rim, tail, arrivals):
     rows = source.shape[0]
     copies = [
         pltpu.make_async_copy(source.at[pl.ds(start, out.shape[0])], out, arrivals.at[i])
-        for i, (start, out) in enumerate(((top.shape[0], bottom), (0, top), (rows - RIM, rim)))
+        for i, (start, out) in enumerate(((top.shape[0], bottom), (0, top), (rows - RIM, tail)))
     ]
     for copy in copies:
         copy.start()
-    for copy in copies + whole_copies(small, held, arrivals, 3):
+    for copy in copies:
         copy.wait()
+    half = tail.shape[1] // 2
+    last = tail[...].astype(F32)[RIM // 2 :]
+    rim[...] = jnp.concatenate([last[:, :half], last[:, half:]], axis=0).astype(BF16)
 
 
 def weight_copies(sources, weights, arrivals, masks):
@@ -150,11 +151,15 @@
     total = None
     for mask, piece in enumerate(pieces):
         count = early.shape[0]
-        part = early[mask, :, columns] if mask < count else last[mask - count, :, columns]
-        term = dot(piece[...], part)
-        total = term if total is None else total + term
+        weights, slot = (early, mask) if mask < count else (last, mask - count)
+        half = piece.shape[1]
+        for side in range(2):
+            term = dot(piece[...], weights[slot, pl.ds(side * half, half), columns])
+            term = term[side * RIM // 2 : (side + 1) * RIM // 2]
+            total = term if total is None else total + term
     inside = lax.axis_index("ctx") > 0
-    out[...] = jnp.where(inside, total, 0.0).astype(BF16).astype(F32)
+    total = jnp.where(inside, total, 0.0).astype(BF16).astype(F32)
+    out[...] = jnp.concatenate([jnp.zeros_like(total), total], axis=0)
 
 
 def finished(masks, pieces, weights, before, start, width):
@@ -243,17 +248,25 @@
 
 
 def write_message(out, state, decay):
-    n = state.shape[0]
-    out[pl.ds(0, n), :] = state.astype(BF16)
-    decay = jnp.broadcast_to(decay, (PAD, decay.shape[1]))
-    high = decay.astype(BF16).astype(F32)
-    out[pl.ds(n, 2 * PAD), :] = jnp.concatenate([high, decay - high], axis=0).astype(BF16)
-
-
-def read_message(ref):
-    n = ref.shape[0] - 2 * PAD
-    tail = ref[pl.ds(n, 2 * PAD), :].astype(F32)
-    return ref[pl.ds(0, n), :].astype(F32), tail[:1] + tail[PAD : PAD + 1]
+    n, width = state.shape
+    tail = []
+    for block in range(width // 128):
+        columns = slice(block * 128, (block + 1) * 128)
+        out[pl.ds(block * n, n), :] = state[:, columns].astype(BF16)
+        high = decay[:, columns].astype(BF16).astype(F32)
+        tail += [high, decay[:, columns] - high]
+    rest = TAIL - len(tail)
+    if rest:
+        tail.append(jnp.zeros((rest, 128), F32))
+    out[pl.ds(out.shape[0] - TAIL, TAIL), :] = jnp.concatenate(tail, axis=0).astype(BF16)
+
+
+def read_message(ref, n):
+    blocks = (ref.shape[0] - TAIL) // n
+    tail = ref[pl.ds(blocks * n, TAIL), :].astype(F32)
+    state = jnp.concatenate([ref[pl.ds(b * n, n), :] for b in range(blocks)], axis=1)
+    decay = [tail[2 * b : 2 * b + 1] + tail[2 * b + 1 : 2 * b + 2] for b in range(blocks)]
+    return state.astype(F32), jnp.concatenate(decay, axis=1)
 
 
 def section_state(own_bc, other_bc, weighted, whole, message, kept):
@@ -268,7 +281,7 @@
 
 
 def pair_states(kept, whole, received):
-    sibling, sibling_decay = read_message(received)
+    sibling, sibling_decay = read_message(received, kept.shape[0])
     mine_decay, _ = mine_other(whole[...])
     mine_decay = mine_decay[:1]
     first = first_core()
@@ -288,7 +301,7 @@
     got, (_, _, keep, give) = refs[:-4], refs[-4:]
     (first, first_decay), _ = pair_states(kept, whole, received)
     chip = lax.axis_index("ctx") // 2
-    messages = [read_message(ref) for ref in got]
+    messages = [read_message(ref, kept.shape[0]) for ref in got]
     places = [jnp.bitwise_xor(chip, mask) for mask in range(1, len(got) + 1)]
     before = jnp.zeros_like(first)
     for place, (state, _) in zip(places, messages):
@@ -416,18 +429,12 @@
     chips = lax.axis_size("ctx") // 2
 
     upper = rows * UPPER // 16
-    small = (decay_logarithm.T, head_step.reshape(1, -1), skip.reshape(1, -1))
-    top, bottom, rim, *small = run(
+    top, bottom, rim = run(
         fetched_halves,
-        [
-            ((upper, depth), BF16),
-            ((rows - upper, depth), BF16),
-            ((RIM, depth), BF16),
-            *[(a.shape, F32) for a in small],
-        ],
-        tokens, *small,
-        scratch=[pltpu.SemaphoreType.DMA((3 + len(small),))],
-        hbm=1 + len(small),
+        [((upper, depth), BF16), ((rows - upper, depth), BF16), ((RIM, depth // 2), BF16)],
+        tokens,
+        scratch=[pltpu.VMEM((RIM, depth), BF16), pltpu.SemaphoreType.DMA((3,))],
+        hbm=1,
     )
 
     def flops(*sizes):
@@ -449,8 +456,9 @@
         hbm=3,
     )
     masks = tuple(sorted(last))
-    vectors = (conv_bc, bias_bc.reshape(1, -1), conv_x, bias_x.reshape(1, -1), gain.reshape(1, -1))
-    weights_end, conv_bc, bias_bc, conv_x, bias_x, gain = run(
+    vectors = [conv_bc, bias_bc, conv_x, bias_x, gain, decay_logarithm.T, head_step, skip]
+    vectors = [v if v.ndim == 2 else v.reshape(1, -1) for v in vectors]
+    weights_end, conv_bc, bias_bc, conv_x, bias_x, gain, *small = run(
         functools.partial(last_weights, masks),
         [((len(masks), depth, everything), BF16), *[(v.shape, F32) for v in vectors]],
         w_bc, w_x, w_z, *vectors,
@@ -503,7 +511,7 @@
         scratch=[pltpu.VMEM((rows + RIM, width), F32)],
         flops=flops(rows, depth, width),
     )
-    message_shape = ((n + 2 * PAD, width // 2), BF16)
+    message_shape = ((n * width // 256 + TAIL, 128), BF16)
     state_shape = (n, width // 2)
     message, kept = run(
         section_state,

time: 60 us -> 59.8 us (level)
  waiting for transfers between devices: 29.6 us -> 28.5 us
  starting transfers between devices: 16.1 us -> 16.9 us
    ppermute x16, waiting for transfers between devices: 26.2 us -> 23.6 us  [partner(): lax.ppermute(value, axis, [(i, i ^ mask) for i in range(lax.axis_size(axi...]
    ppermute x1, waiting for transfers between devices: 3.43 us -> 4.87 us  [onward(): return lax.ppermute(value, axis, [(i, (i + 1) % size) for i in range(size)])]
    ppermute x16, starting transfers between devices: 16.1 us -> 16.9 us  [partner(): lax.ppermute(value, axis, [(i, i ^ mask) for i in range(lax.axis_size(axi...]
where the time goes in v6:
time: 59.8 us; the launch traced here: 59.6 us
  waiting for transfers between devices  28.5 us (48%)
  starting transfers between devices  16.9 us (28%)
  Pallas kernels  14 us (23%)
    ppermute x16, waiting for transfers between devices, partner(): lax.ppermute(value, axis, [(i, i ^ mask) for i in range(lax.axis_size(axi...  23.6 us
    ppermute x16, starting transfers between devices, partner(): lax.ppermute(value, axis, [(i, i ^ mask) for i in range(lax.axis_size(axi...  16.9 us
    pallas_call x16, Pallas kernels, run(): results = call(*operands)  14 us
    ppermute x1, waiting for transfers between devices, onward(): return lax.ppermute(value, axis, [(i, (i + 1) % size) for i in range(size)])  4.87 us
  transfers between devices with their start and end apart: 17, of which 10 were waited for; matrix products, arithmetic and copies ran while one was open for 0% of the time, Pallas kernels for 18%

profile of v6, /device:TPU:0, one launch (start us, length us, event | category | flops | bytes accessed | tf_op | source)
XLA Modules:
  0.0 59.6 jit_solution(14330641420909710946)
XLA Ops:
  0.0 1.1 %shard_map.118 = (bf16[144,1024]{1,0:T(8,128)(2,1)S(1)}, bf16[112,1024]{1,0:T(8,128)(2,1)S(1)}, bf16[8,512]{1,0:T(8,128)(2,1)S(1)}) custom-call(bf16[256,1024]{1,0:T(8,128)(2,1)} %source.1), custom_call_target="tpu_custom_call" | custom-call | flops 1000000 | bytes 2500 | tf_op jit(solution)/shard_map/pallas_call | solution.py:39
  1.1 3.1 %collective-permute-start = (bf16[144,1024]{1,0:T(8,128)(2,1)S(1)}, bf16[144,1024]{1,0:T(8,128)(2,1)S(1)}, u32[]{:S(2)}, u32[]{:S(2)}) collective-permute-start(bf16[144,1024]{1,0:T(8,128)(2,1)S(1)} %get-tuple-element.34.top), channel_id=1, source_target_pairs={{0,2},{1,3},{2,0},{3,1},{4,6},{5,7},{6,4},{7,5},{8,10},{9,11},{10,... | collective-permute-start | bytes 884744 | tf_op jit(solution)/shard_map/ppermute | solution.py:44
  4.2 1.5 %collective-permute-start.2 = (bf16[112,1024]{1,0:T(8,128)(2,1)S(1)}, bf16[112,1024]{1,0:T(8,128)(2,1)S(1)}, u32[]{:S(2)}, u32[]{:S(2)}) collective-permute-start(bf16[112,1024]{1,0:T(8,128)(2,1)S(1)} %get-tuple-element.35.bottom), channel_id=1, source_target_pairs={{0,1},{1,0},{2,3},{3,2},{4,5},{5,4},{6,7},{7,6},{8,9},{9,8},{10,11... | collective-permute-start | bytes 688136 | tf_op jit(solution)/shard_map/ppermute | solution.py:44
  5.7 0.5 collective-permute-start.4
  6.2 0.1 collective-permute-start.5
  6.3 5.8 %collective-permute-done.refs_2_ = bf16[144,1024]{1,0:T(8,128)(2,1)S(1)} collective-permute-done((bf16[144,1024]{1,0:T(8,128)(2,1)S(1)}, bf16[144,1024]{1,0:T(8,128)(2,1)S(1)}, u32[]{:S(2)}, u32[]{:S(2)}) %collective-permute-start) | collective-permute-done | bytes 294944 | tf_op jit(solution)/shard_map/ppermute | solution.py:44
  12.0 2.0 %collective-permute-start.1 = (bf16[144,1024]{1,0:T(8,128)(2,1)S(1)}, bf16[144,1024]{1,0:T(8,128)(2,1)S(1)}, u32[]{:S(2)}, u32[]{:S(2)}) collective-permute-start(bf16[144,1024]{1,0:T(8,128)(2,1)S(1)} %collective-permute-done.refs_2_), channel_id=1, source_target_pairs={{0,1},{1,0},{2,3},{3,2},{4,5},{5,4},{6,7},{7,6},{8,9},{9,8},{10,11... | collective-permute-start | bytes 884744 | tf_op jit(solution)/shard_map/ppermute | solution.py:44
  14.0 0.0 collective-permute-done.2.refs_1_
  14.0 1.5 %collective-permute-start.3 = (bf16[112,1024]{1,0:T(8,128)(2,1)S(1)}, bf16[112,1024]{1,0:T(8,128)(2,1)S(1)}, u32[]{:S(2)}, u32[]{:S(2)}) collective-permute-start(bf16[112,1024]{1,0:T(8,128)(2,1)S(1)} %collective-permute-done.2.refs_1_), channel_id=1, source_target_pairs={{0,2},{1,3},{2,0},{3,1},{4,6},{5,7},{6,4},{7,5},{8,10},{9,11},{10,... | collective-permute-start | bytes 688136 | tf_op jit(solution)/shard_map/ppermute | solution.py:44
  15.6 0.0 collective-permute-start.6
  15.6 4.9 %collective-permute-done.6.refs_0_ = bf16[8,512]{1,0:T(8,128)(2,1)S(1)} collective-permute-done((bf16[8,512]{1,0:T(8,128)(2,1)S(1)}, bf16[8,512]{1,0:T(8,128)(2,1)S(1)}, u32[]{:S(2)}, u32[]{:S(2)}) %collective-permute-start.6) | collective-permute-done | bytes 8224 | tf_op jit(solution)/shard_map/ppermute | solution.py:53
  20.4 0.5 collective-permute-start.7
  21.0 3.1 %collective-permute-done.7.refs_1_ = bf16[8,512]{1,0:T(8,128)(2,1)S(1)} collective-permute-done((bf16[8,512]{1,0:T(8,128)(2,1)S(1)}, bf16[8,512]{1,0:T(8,128)(2,1)S(1)}, u32[]{:S(2)}, u32[]{:S(2)}) %collective-permute-start.7) | collective-permute-done | bytes 8224 | tf_op jit(solution)/shard_map/ppermute | solution.py:44
  24.1 0.5 collective-permute-start.8
  24.6 3.1 %collective-permute-done.8.refs_2_ = bf16[8,512]{1,0:T(8,128)(2,1)S(1)} collective-permute-done((bf16[8,512]{1,0:T(8,128)(2,1)S(1)}, bf16[8,512]{1,0:T(8,128)(2,1)S(1)}, u32[]{:S(2)}, u32[]{:S(2)}) %collective-permute-start.8) | collective-permute-done | bytes 8224 | tf_op jit(solution)/shard_map/ppermute | solution.py:44
  27.7 1.4 %collective-permute-start.9 = (bf16[8,512]{1,0:T(8,128)(2,1)S(1)}, bf16[8,512]{1,0:T(8,128)(2,1)S(1)}, u32[]{:S(2)}, u32[]{:S(2)}) collective-permute-start(bf16[8,512]{1,0:T(8,128)(2,1)S(1)} %collective-permute-done.6.refs_0_), channel_id=1, source_target_pairs={{0,3},{1,2},{2,1},{3,0},{4,7},{5,6},{6,5},{7,4},{8,11},{9,10},{10,... | collective-permute-start | bytes 24584 | tf_op jit(solution)/shard_map/ppermute | solution.py:44
  29.1 3.1 %shard_map.120 = (f32[256,1152]{1,0:T(8,128)S(1)}, bf16[3,1024,1152]{2,1,0:T(8,128)(2,1)S(1)}) custom-call(bf16[4096,128]{1,0:T(8,128)(2,1)} %w_bc.3, bf16[4096,512]{1,0:T(8,128)(2,1)} %w_x.3, bf16[4096,512]{1,0:T(8,128)(2,1)} %w_z.3, bf16[144,1024]{1,0:T(8,128)(2,1)S(1)} %get-tuple-element.34.top, bf16[112,1024]{1,0:T(8,128)(2,1)S(1)} %get-tuple-element.35.bottom), custom_call_target="tpu_custom_call" | custom-call | flops 603979776 | bytes 1509949 | tf_op jit(solution)/shard_map/pallas_call | solution.py:39
  32.3 1.8 %shard_map.119 = (bf16[1,1024,1152]{2,1,0:T(8,128)(2,1)S(1)}, f32[4,128]{1,0:T(4,128)S(1)}, f32[1,128]{1,0:T(1,128)S(1)}, f32[4,512]{1,0:T(4,128)S(1)}, f32[1,51...) custom-call(bf16[4096,128]{1,0:T(8,128)(2,1)} %w_bc.3, ...), custom_call_target="tpu_custom_call" | custom-call | flops 1000000 | bytes 2500 | tf_op jit(solution)/shard_map/pallas_call | solution.py:39
  34.1 0.0 collective-permute-done.9.refs_3_
  34.1 0.8 %shard_map.122.refs_4_ = f32[8,640]{1,0:T(8,128)S(1)} custom-call(bf16[8,512]{1,0:T(8,128)(2,1)S(1)} %collective-permute-done.6.refs_0_, bf16[8,512]{1,0:T(8,128)(2,1)S(1)} %collective-permute-done.7.refs_1_, bf16[8,512]{1,0:T(8,128)(2,1)S(1)} %collective-permute-done.8.refs_2_, bf16[8,512]{1,0:T(8,128)(2,1)S(1)} %collective-permute-done.9.refs_3_, ...), custom_call_target="tpu_custom_call" | custom-call | flops 268435456 | bytes 671088 | tf_op jit(solution)/shard_map/pallas_call | solution.py:39
  34.9 0.0 collective-permute-done.5.refs_3_
  34.9 0.0 collective-permute-done.4.refs_0_
  35.0 1.5 %shard_map.121.refs_3_ = f32[256,1152]{1,0:T(8,128)S(1)} custom-call(bf16[144,1024]{1,0:T(8,128)(2,1)S(1)} %collective-permute-done.4.refs_0_, bf16[112,1024]{1,0:T(8,128)(2,1)S(1)} %collective-permute-done.2.refs_1_, bf16[144,1024]{1,0:T(8,128)(2,1)S(1)} %collective-permute-done.refs_2_, bf16[112,1024]{1,0:T(8,128)(2,1)S(1)} %collective-permute-done.5.refs_3_, ...), custom_call_target="tpu_custom_call" | custom-call | flops 1207959552 | bytes 3019898 | tf_op jit(solution)/shard_map/pallas_call | solution.py:39
  36.5 0.0 collective-permute-done.3.refs_1_
  36.5 0.0 collective-permute-done.1.refs_0_
  36.5 0.4 shard_map.123.own_bc
  36.9 0.6 %collective-permute-start.10 = (bf16[256,128]{1,0:T(8,128)(2,1)S(1)}, bf16[256,128]{1,0:T(8,128)(2,1)S(1)}, u32[]{:S(2)}, u32[]{:S(2)}) collective-permute-start(bf16[256,128]{1,0:T(8,128)(2,1)S(1)} %shard_map.123.own_bc), channel_id=1, source_target_pairs={{0,1},{1,0},{2,3},{3,2},{4,5},{5,4},{6,7},{7,6},{8,9},{9,8},{10,11... | collective-permute-start | bytes 196616 | tf_op jit(solution)/shard_map/ppermute | solution.py:44
  37.5 1.2 %shard_map.124 = (bf16[8,256,256]{2,1,0:T(8,128)(2,1)S(1)}, f32[256,512]{1,0:T(8,128)S(1)}, f32[256,512]{1,0:T(8,128)S(1)}, f32[8,512]{1,0:T(8,128)S(1)}, f32[1,512]{1,0:T(1,128)S(1)}) custom-call(f32[8,256]{1,0:T(8,128)S(1)} %get-tuple-element.44.decay_t, f32[1,8]{1,0:T(1,128)S(1)} %get-tuple-element.45.step, f32[1,8]{1,0:T(1,128)S(1)} %get-tuple-element.46.skip), custom_call_target="tpu_custom_call" | custom-call | flops 67108864 | bytes 167772 | tf_op jit(solution)/shard_map/pallas_call | solution.py:39
  38.7 1.1 %shard_map.125 = (bf16[256,512]{1,0:T(8,128)(2,1)S(1)}, bf16[256,512]{1,0:T(8,128)(2,1)S(1)}) custom-call(bf16[144,1024]{1,0:T(8,128)(2,1)S(1)} %collective-permute-done.1.refs_0_, bf16[112,1024]{1,0:T(8,128)(2,1)S(1)} %collective-permute-done.3.refs_1_, bf16[1,1024,1152]{2,1,0:T(8,128)(2,1)S(1)} %get-tuple-element.36.refs_5_.refs_2_, ...), custom_call_target="tpu_custom_call" | custom-call | flops 268435456 | bytes 671088 | tf_op jit(solution)/shard_map/pallas_call | solution.py:39
  39.7 1.5 %collective-permute-done.10.other_bc = bf16[256,128]{1,0:T(8,128)(2,1)S(1)} collective-permute-done((bf16[256,128]{1,0:T(8,128)(2,1)S(1)}, bf16[256,128]{1,0:T(8,128)(2,1)S(1)}, u32[]{:S(2)}, u32[]{:S(2)}) %collective-permute-start.10) | collective-permute-done | bytes 65568 | tf_op jit(solution)/shard_map/ppermute | solution.py:44
  41.2 0.2 shard_map.126
  41.4 0.1 collective-permute-start.11
  41.5 1.2 %collective-permute-done.11.received = bf16[264,128]{1,0:T(8,128)(2,1)S(1)} collective-permute-done((bf16[264,128]{1,0:T(8,128)(2,1)S(1)}, bf16[264,128]{1,0:T(8,128)(2,1)S(1)}, u32[]{:S(2)}, u32[]{:S(2)}) %collective-permute-start.11) | collective-permute-done | bytes 67616 | tf_op jit(solution)/shard_map/ppermute | solution.py:44
  42.8 1.6 %collective-permute-start.12 = (bf16[264,128]{1,0:T(8,128)(2,1)S(1)}, bf16[264,128]{1,0:T(8,128)(2,1)S(1)}, u32[]{:S(2)}, u32[]{:S(2)}) collective-permute-start(bf16[264,128]{1,0:T(8,128)(2,1)S(1)} %shard_map.127._.refs_4_), channel_id=1, source_target_pairs={{0,8},{4,12},{8,0},{12,4},{16,24},{20,28},{24,16},{28,20},{1,9},{5... | collective-permute-start | bytes 202760 | tf_op jit(solution)/shard_map/ppermute | solution.py:44
  44.4 2.6 %collective-permute-start.13 = (bf16[264,128]{1,0:T(8,128)(2,1)S(1)}, bf16[264,128]{1,0:T(8,128)(2,1)S(1)}, u32[]{:S(2)}, u32[]{:S(2)}) collective-permute-start(bf16[264,128]{1,0:T(8,128)(2,1)S(1)} %shard_map.127._.refs_4_), channel_id=1, source_target_pairs={{0,16},{4,20},{8,24},{12,28},{16,0},{20,4},{24,8},{28,12},{1,17},{... | collective-permute-start | bytes 202760 | tf_op jit(solution)/shard_map/ppermute | solution.py:44
  47.0 0.2 collective-permute-start.14
  47.3 0.7 %shard_map.128.refs_3_.within = f32[256,512]{1,0:T(8,128)S(1)} custom-call(bf16[256,128]{1,0:T(8,128)(2,1)S(1)} %shard_map.123.own_bc, bf16[256,128]{1,0:T(8,128)(2,1)S(1)} %collective-permute-done.10.other_bc, bf16[256,512]{1,0:T(8,128)(2,1)S(1)} %get-tuple-element.52.x, bf16[8,256,256]{2,1,0:T(8,128)(2,1)S(1)} %get-tuple-element.53.segment, ...), custom_call_target="tpu_custom_call" | custom-call | flops 201326592 | bytes 503316 | tf_op jit(solution)/shard_map/pallas_call | solution.py:39
  47.9 0.5 shard_map.129.refs_4_.gate
  48.5 0.0 collective-permute-done.12.refs_0_
  48.5 3.6 %collective-permute-done.13.refs_1_ = bf16[264,128]{1,0:T(8,128)(2,1)S(1)} collective-permute-done((bf16[264,128]{1,0:T(8,128)(2,1)S(1)}, bf16[264,128]{1,0:T(8,128)(2,1)S(1)}, u32[]{:S(2)}, u32[]{:S(2)}) %collective-permute-start.13) | collective-permute-done | bytes 67616 | tf_op jit(solution)/shard_map/ppermute | solution.py:44
  52.1 1.1 %collective-permute-done.14.refs_2_ = bf16[264,128]{1,0:T(8,128)(2,1)S(1)} collective-permute-done((bf16[264,128]{1,0:T(8,128)(2,1)S(1)}, bf16[264,128]{1,0:T(8,128)(2,1)S(1)}, u32[]{:S(2)}, u32[]{:S(2)}) %collective-permute-start.14) | collective-permute-done | bytes 67616 | tf_op jit(solution)/shard_map/ppermute | solution.py:44
  53.2 0.1 shard_map.130
  53.3 0.1 collective-permute-start.15
  53.4 0.2 shard_map.131
  53.6 1.0 %collective-permute-done.15.take = bf16[128,256]{1,0:T(8,128)(2,1)S(1)} collective-permute-done((bf16[128,256]{1,0:T(8,128)(2,1)S(1)}, bf16[128,256]{1,0:T(8,128)(2,1)S(1)}, u32[]{:S(2)}, u32[]{:S(2)}) %collective-permute-start.15) | collective-permute-done | bytes 65568 | tf_op jit(solution)/shard_map/ppermute | solution.py:44
  54.6 0.3 shard_map.132
  55.0 0.6 collective-permute-start.16
  55.5 3.1 %collective-permute-done.16.other_square = f32[8,256]{1,0:T(8,128)S(1)} collective-permute-done((f32[8,256]{1,0:T(8,128)S(1)}, f32[8,256]{1,0:T(8,128)S(1)}, u32[]{:S(2)}, u32[]{:S(2)}) %collective-permute-start.16) | collective-permute-done | bytes 8224 | tf_op jit(solution)/shard_map/ppermute | solution.py:44
  58.7 1.0 %shard_map.133 = bf16[256,512]{1,0:T(8,128)(2,1)} custom-call(f32[256,256]{1,0:T(8,128)S(1)} %get-tuple-element.57.mine, f32[256,256]{1,0:T(8,128)S(1)} %get-tuple-element.60.other, f32[8,256]{1,0:T(8,128)S(1)} %get-tuple-element.61.square, f32[8,256]{1,0:T(8,128)S(1)} %collective-permute-done.16.other_square, f32[1,512]{1,0:T(1,128)S(1)} %get-tuple-element.62.gain), custom_call_target="tpu_custom_call" | custom-call | flops 1000000 | bytes 2500 | tf_op jit(solution)/shard_map/pallas_call | solution.py:39
  (1 shorter events, 0.0 us)
Async XLA Ops:
  1.1 10.9 %collective-permute-start = (bf16[144,1024]{1,0:T(8,128)(2,1)S(1)}, bf16[144,1024]{1,0:T(8,128)(2,1)S(1)}, u32[]{:S(2)}, u32[]{:S(2)}) collective-permute-start(bf16[144,1024]{1,0:T(8,128)(2,1)S(1)} %get-tuple-element.34.top), channel_id=1, source_target_pairs={{0,2},{1,3},{2,0},{3,1},{4,6},{5,7},{6,4},{7,5},{8,10},{9,11},{10,... | collective-permute-start | bytes 884744 | tf_op jit(solution)/shard_map/ppermute | solution.py:44
  4.2 9.9 %collective-permute-start.2 = (bf16[112,1024]{1,0:T(8,128)(2,1)S(1)}, bf16[112,1024]{1,0:T(8,128)(2,1)S(1)}, u32[]{:S(2)}, u32[]{:S(2)}) collective-permute-start(bf16[112,1024]{1,0:T(8,128)(2,1)S(1)} %get-tuple-element.35.bottom), channel_id=1, source_target_pairs={{0,1},{1,0},{2,3},{3,2},{4,5},{5,4},{6,7},{7,6},{8,9},{9,8},{10,11... | collective-permute-start | bytes 688136 | tf_op jit(solution)/shard_map/ppermute | solution.py:44
  5.7 29.3 %collective-permute-start.4 = (bf16[144,1024]{1,0:T(8,128)(2,1)S(1)}, bf16[144,1024]{1,0:T(8,128)(2,1)S(1)}, u32[]{:S(2)}, u32[]{:S(2)}) collective-permute-start(bf16[144,1024]{1,0:T(8,128)(2,1)S(1)} %get-tuple-element.34.top), channel_id=1, source_target_pairs={{0,1},{1,0},{2,3},{3,2},{4,5},{5,4},{6,7},{7,6},{8,9},{9,8},{10,11... | collective-permute-start | bytes 884744 | tf_op jit(solution)/shard_map/ppermute | solution.py:44
  6.2 28.7 %collective-permute-start.5 = (bf16[112,1024]{1,0:T(8,128)(2,1)S(1)}, bf16[112,1024]{1,0:T(8,128)(2,1)S(1)}, u32[]{:S(2)}, u32[]{:S(2)}) collective-permute-start(bf16[112,1024]{1,0:T(8,128)(2,1)S(1)} %get-tuple-element.35.bottom), channel_id=1, source_target_pairs={{0,2},{1,3},{2,0},{3,1},{4,6},{5,7},{6,4},{7,5},{8,10},{9,11},{10,... | collective-permute-start | bytes 688136 | tf_op jit(solution)/shard_map/ppermute | solution.py:44
  12.0 24.5 %collective-permute-start.1 = (bf16[144,1024]{1,0:T(8,128)(2,1)S(1)}, bf16[144,1024]{1,0:T(8,128)(2,1)S(1)}, u32[]{:S(2)}, u32[]{:S(2)}) collective-permute-start(bf16[144,1024]{1,0:T(8,128)(2,1)S(1)} %collective-permute-done.refs_2_), channel_id=1, source_target_pairs={{0,1},{1,0},{2,3},{3,2},{4,5},{5,4},{6,7},{7,6},{8,9},{9,8},{10,11... | collective-permute-start | bytes 884744 | tf_op jit(solution)/shard_map/ppermute | solution.py:44
  14.0 22.5 %collective-permute-start.3 = (bf16[112,1024]{1,0:T(8,128)(2,1)S(1)}, bf16[112,1024]{1,0:T(8,128)(2,1)S(1)}, u32[]{:S(2)}, u32[]{:S(2)}) collective-permute-start(bf16[112,1024]{1,0:T(8,128)(2,1)S(1)} %collective-permute-done.2.refs_1_), channel_id=1, source_target_pairs={{0,2},{1,3},{2,0},{3,1},{4,6},{5,7},{6,4},{7,5},{8,10},{9,11},{10,... | collective-permute-start | bytes 688136 | tf_op jit(solution)/shard_map/ppermute | solution.py:44
  15.6 4.9 %collective-permute-start.6 = (bf16[8,512]{1,0:T(8,128)(2,1)S(1)}, bf16[8,512]{1,0:T(8,128)(2,1)S(1)}, u32[]{:S(2)}, u32[]{:S(2)}) collective-permute-start(bf16[8,512]{1,0:T(8,128)(2,1)S(1)} %get-tuple-element.39), channel_id=1, source_target_pairs={{0,4},{4,8},{8,12},{12,16},{16,20},{20,24},{24,28},{28,0},{1,5},{5... | collective-permute-start | bytes 24584 | tf_op jit(solution)/shard_map/ppermute | solution.py:53
  20.4 3.7 %collective-permute-start.7 = (bf16[8,512]{1,0:T(8,128)(2,1)S(1)}, bf16[8,512]{1,0:T(8,128)(2,1)S(1)}, u32[]{:S(2)}, u32[]{:S(2)}) collective-permute-start(bf16[8,512]{1,0:T(8,128)(2,1)S(1)} %collective-permute-done.6.refs_0_), channel_id=1, source_target_pairs={{0,1},{1,0},{2,3},{3,2},{4,5},{5,4},{6,7},{7,6},{8,9},{9,8},{10,11... | collective-permute-start | bytes 24584 | tf_op jit(solution)/shard_map/ppermute | solution.py:44
  24.1 3.7 %collective-permute-start.8 = (bf16[8,512]{1,0:T(8,128)(2,1)S(1)}, bf16[8,512]{1,0:T(8,128)(2,1)S(1)}, u32[]{:S(2)}, u32[]{:S(2)}) collective-permute-start(bf16[8,512]{1,0:T(8,128)(2,1)S(1)} %collective-permute-done.6.refs_0_), channel_id=1, source_target_pairs={{0,2},{1,3},{2,0},{3,1},{4,6},{5,7},{6,4},{7,5},{8,10},{9,11},{10,... | collective-permute-start | bytes 24584 | tf_op jit(solution)/shard_map/ppermute | solution.py:44
  27.7 6.4 %collective-permute-start.9 = (bf16[8,512]{1,0:T(8,128)(2,1)S(1)}, bf16[8,512]{1,0:T(8,128)(2,1)S(1)}, u32[]{:S(2)}, u32[]{:S(2)}) collective-permute-start(bf16[8,512]{1,0:T(8,128)(2,1)S(1)} %collective-permute-done.6.refs_0_), channel_id=1, source_target_pairs={{0,3},{1,2},{2,1},{3,0},{4,7},{5,6},{6,5},{7,4},{8,11},{9,10},{10,... | collective-permute-start | bytes 24584 | tf_op jit(solution)/shard_map/ppermute | solution.py:44
  36.9 4.3 %collective-permute-start.10 = (bf16[256,128]{1,0:T(8,128)(2,1)S(1)}, bf16[256,128]{1,0:T(8,128)(2,1)S(1)}, u32[]{:S(2)}, u32[]{:S(2)}) collective-permute-start(bf16[256,128]{1,0:T(8,128)(2,1)S(1)} %shard_map.123.own_bc), channel_id=1, source_target_pairs={{0,1},{1,0},{2,3},{3,2},{4,5},{5,4},{6,7},{7,6},{8,9},{9,8},{10,11... | collective-permute-start | bytes 196616 | tf_op jit(solution)/shard_map/ppermute | solution.py:44
  41.4 1.3 %collective-permute-start.11 = (bf16[264,128]{1,0:T(8,128)(2,1)S(1)}, bf16[264,128]{1,0:T(8,128)(2,1)S(1)}, u32[]{:S(2)}, u32[]{:S(2)}) collective-permute-start(bf16[264,128]{1,0:T(8,128)(2,1)S(1)} %get-tuple-element.51), channel_id=1, source_target_pairs={{0,4},{4,0},{8,12},{12,8},{16,20},{20,16},{24,28},{28,24},{1,5},{5... | collective-permute-start | bytes 202760 | tf_op jit(solution)/shard_map/ppermute | solution.py:44
  42.8 5.7 %collective-permute-start.12 = (bf16[264,128]{1,0:T(8,128)(2,1)S(1)}, bf16[264,128]{1,0:T(8,128)(2,1)S(1)}, u32[]{:S(2)}, u32[]{:S(2)}) collective-permute-start(bf16[264,128]{1,0:T(8,128)(2,1)S(1)} %shard_map.127._.refs_4_), channel_id=1, source_target_pairs={{0,8},{4,12},{8,0},{12,4},{16,24},{20,28},{24,16},{28,20},{1,9},{5... | collective-permute-start | bytes 202760 | tf_op jit(solution)/shard_map/ppermute | solution.py:44
  44.4 7.7 %collective-permute-start.13 = (bf16[264,128]{1,0:T(8,128)(2,1)S(1)}, bf16[264,128]{1,0:T(8,128)(2,1)S(1)}, u32[]{:S(2)}, u32[]{:S(2)}) collective-permute-start(bf16[264,128]{1,0:T(8,128)(2,1)S(1)} %shard_map.127._.refs_4_), channel_id=1, source_target_pairs={{0,16},{4,20},{8,24},{12,28},{16,0},{20,4},{24,8},{28,12},{1,17},{... | collective-permute-start | bytes 202760 | tf_op jit(solution)/shard_map/ppermute | solution.py:44
  47.0 6.2 %collective-permute-start.14 = (bf16[264,128]{1,0:T(8,128)(2,1)S(1)}, bf16[264,128]{1,0:T(8,128)(2,1)S(1)}, u32[]{:S(2)}, u32[]{:S(2)}) collective-permute-start(bf16[264,128]{1,0:T(8,128)(2,1)S(1)} %shard_map.127._.refs_4_), channel_id=1, source_target_pairs={{0,24},{4,28},{8,16},{12,20},{16,8},{20,12},{24,0},{28,4},{1,25},{... | collective-permute-start | bytes 202760 | tf_op jit(solution)/shard_map/ppermute | solution.py:44
  53.3 1.3 %collective-permute-start.15 = (bf16[128,256]{1,0:T(8,128)(2,1)S(1)}, bf16[128,256]{1,0:T(8,128)(2,1)S(1)}, u32[]{:S(2)}, u32[]{:S(2)}) collective-permute-start(bf16[128,256]{1,0:T(8,128)(2,1)S(1)} %get-tuple-element.58), channel_id=1, source_target_pairs={{0,4},{4,0},{8,12},{12,8},{16,20},{20,16},{24,28},{28,24},{1,5},{5... | collective-permute-start | bytes 196616 | tf_op jit(solution)/shard_map/ppermute | solution.py:44
  55.0 3.7 %collective-permute-start.16 = (f32[8,256]{1,0:T(8,128)S(1)}, f32[8,256]{1,0:T(8,128)S(1)}, u32[]{:S(2)}, u32[]{:S(2)}) collective-permute-start(f32[8,256]{1,0:T(8,128)S(1)} %get-tuple-element.61.square), channel_id=1, source_target_pairs={{0,1},{1,0},{2,3},{3,2},{4,5},{5,4},{6,7},{7,6},{8,9},{9,8},{10,11... | collective-permute-start | bytes 24584 | tf_op jit(solution)/shard_map/ppermute | solution.py:44
